TPU v7x, 32 devices: a whole 2x2x4 slice. The times are simulated.
32 devices in a mesh: fields: 2 (over x), seq: 8 (over z, y), head: 2 (over core).
Axes of the slice: x: 2, y: 2, z: 4, core: 2. Of those that a mesh axis runs over, the one named last changes fastest.
Arguments:
- tokens: bfloat16 [65536, 512], P(('fields', 'seq')), parts along dimension 0, may hold values from -6 to 6
- norm_gain: float32 [512], replicated, may hold values from 0.1 to 1.9
- coarse_gain: float32 [512], replicated, may hold values from 0.25 to 2.5
- w_query: bfloat16 [512, 512], P(None, 'head'), may hold values from -0.25 to 0.25
- w_key: bfloat16 [512, 512], P(None, 'head'), may hold values from -0.25 to 0.25
- w_value: bfloat16 [512, 512], P(None, 'head'), may hold values from -0.25 to 0.25
- w_out: bfloat16 [512, 512], replicated, may hold values from -0.25 to 0.25
- score_scale: float32 [8], P('head'), may hold values from 1 to 40, as said below
Outputs:
- attn_out: bfloat16 [65536, 512], P(('fields', 'seq'), 'head'), parts along dimension 0
There are 2 independent parts, one for each index of `fields`. A program takes and returns all parts, laid end to end along the dimension named above; an argument that names none is the same for every part. Nothing has to cross between parts.
Inputs may be any that keep to these rules, and one draw needn't show every extreme that they name: `score_scale`: per-head score temperature.
All inputs are finite; a program needn't handle non-finite values.
Results may differ from a plain program's by a relative error of at most 0.0035.
The roundings to bfloat16 on the way count: a program that leaves them out, or rounds other values in their place, can miss the bound.
Values may be sent and summed in bfloat16 or wider, within the bound.
No kernel may reach another device: no remote copies, remote signals or barrier semaphores. Data moves between devices by JAX's collectives and lax.ppermute only.
A program may use at most 64 MiB of HBM per device.

v0:
```python
import jax
import jax.numpy as jnp
from jax import lax
from jax.sharding import PartitionSpec as P

HEAD_DIM = 64
WINDOW = 256
POOL = 1024
QB = 512


def with_halo(block, sides, width):
    for axis, dim in sides:
        count = lax.axis_size(axis)
        forward = [(i, i + 1) for i in range(count - 1)]
        backward = [(target, source) for source, target in forward]
        low = lax.ppermute(
            lax.slice_in_dim(block, block.shape[dim] - width, None, axis=dim), axis, forward
        )
        high = lax.ppermute(lax.slice_in_dim(block, 0, width, axis=dim), axis, backward)
        block = jnp.concatenate([low, block, high], axis=dim)
    return block


def rms_rows(matrix, scaling):
    return matrix * lax.rsqrt(jnp.mean(matrix * matrix, axis=-1, keepdims=True) + 1e-05) * scaling


def unit_heads(matrix, head_count):
    split = matrix.reshape(matrix.shape[0], head_count, HEAD_DIM)
    return split * lax.rsqrt(jnp.mean(split * split, axis=-1, keepdims=True) + 1e-06)


def body(tokens, norm_gain, coarse_gain, w_query, w_key, w_value, w_out, score_scale):
    tok_count = tokens.shape[0]
    full_width = tokens.shape[1]
    local_heads = score_scale.shape[0]
    width = local_heads * HEAD_DIM
    seq_index = lax.axis_index("seq")
    total_tokens = tok_count * lax.axis_size("seq")
    normed = rms_rows(tokens.astype(jnp.float32), norm_gain).astype(jnp.bfloat16)
    factor = (score_scale * HEAD_DIM ** (-0.5))[None, :, None]
    queries = (
        unit_heads(jnp.dot(normed, w_query, preferred_element_type=jnp.float32), local_heads)
        * factor
    ).astype(jnp.bfloat16)
    key_rows = unit_heads(
        jnp.dot(normed, w_key, preferred_element_type=jnp.float32), local_heads
    ).astype(jnp.bfloat16)
    value_rows = jnp.dot(normed, w_value, preferred_element_type=jnp.float32).astype(jnp.bfloat16)
    stacked = jnp.stack([key_rows.reshape(tok_count, width), value_rows])
    extended = with_halo(stacked, (("seq", 1),), WINDOW)
    extended = extended.reshape(2, tok_count + 2 * WINDOW, local_heads, HEAD_DIM)
    normed_kept = lax.optimization_barrier(normed)
    pooled = jnp.mean(
        normed_kept.astype(jnp.float32).reshape(tok_count // POOL, POOL, full_width), axis=1
    )
    coarse = rms_rows(pooled, coarse_gain).astype(jnp.bfloat16)
    coarse_keys = unit_heads(
        jnp.dot(coarse, w_key, preferred_element_type=jnp.float32), local_heads
    ).astype(jnp.bfloat16)
    coarse_values = jnp.dot(coarse, w_value, preferred_element_type=jnp.float32).astype(
        jnp.bfloat16
    )
    coarse_stack = jnp.stack([coarse_keys.reshape(coarse.shape[0], width), coarse_values])
    coarse_all = lax.all_gather(coarse_stack, "seq", axis=1, tiled=True)
    coarse_all = coarse_all.reshape(2, coarse_all.shape[1], local_heads, HEAD_DIM)
    span = QB + 2 * WINDOW
    offsets = (
        jnp.arange(QB, dtype=jnp.int32)[:, None]
        - jnp.arange(span, dtype=jnp.int32)[None, :]
        + WINDOW
    )
    near = jnp.abs(offsets) <= WINDOW

    def one_block(block_id):
        row_start = block_id * QB
        block_queries = lax.dynamic_slice_in_dim(queries, row_start, QB, 0)
        block_keys = lax.dynamic_slice_in_dim(extended[0], row_start, span, 0)
        block_values = lax.dynamic_slice_in_dim(extended[1], row_start, span, 0)
        band = jnp.einsum(
            "qhd,khd->hqk", block_queries, block_keys, preferred_element_type=jnp.float32
        )
        positions = seq_index * tok_count + row_start + jnp.arange(span, dtype=jnp.int32) - WINDOW
        inside = (positions >= 0) & (positions < total_tokens)
        band = jnp.where(near[None] & inside[None, None, :], band, -1e30)
        far = jnp.einsum(
            "qhd,khd->hqk", block_queries, coarse_all[0], preferred_element_type=jnp.float32
        )
        peak = jnp.maximum(
            jnp.max(band, axis=-1, keepdims=True), jnp.max(far, axis=-1, keepdims=True)
        )
        band_exp = jnp.exp(band - peak)
        far_exp = jnp.exp(far - peak)
        total = jnp.sum(band_exp, axis=-1, keepdims=True) + jnp.sum(far_exp, axis=-1, keepdims=True)
        band_weights = (band_exp / total).astype(jnp.bfloat16)
        far_weights = (far_exp / total).astype(jnp.bfloat16)
        mixed = jnp.einsum(
            "hqk,khd->qhd", band_weights, block_values, preferred_element_type=jnp.float32
        )
        mixed = mixed + jnp.einsum(
            "hqk,khd->qhd", far_weights, coarse_all[1], preferred_element_type=jnp.float32
        )
        return mixed.astype(jnp.bfloat16).reshape(QB, width)

    attended = lax.map(one_block, jnp.arange(tok_count // QB, dtype=jnp.int32)).reshape(
        tok_count, width
    )
    head_index = lax.axis_index("head")
    own_rows = lax.dynamic_slice_in_dim(w_out, head_index * width, width, 0)
    partial_out = jnp.dot(attended, own_rows, preferred_element_type=jnp.float32)
    summed = lax.psum_scatter(partial_out, "head", scatter_dimension=1, tiled=True)
    return summed.astype(jnp.bfloat16)


def solution(mesh):
    return jax.shard_map(
        body,
        mesh=mesh,
        in_specs=(
            P(("fields", "seq"), None),
            P(),
            P(),
            P(None, "head"),
            P(None, "head"),
            P(None, "head"),
            P(),
            P("head"),
        ),
        out_specs=P(("fields", "seq"), "head"),
        check_vma=False,
    )
```

profile of v0, /device:TPU:7, one launch (start us, length us, event | category | flops | bytes accessed | tf_op | source)
XLA Modules:
  0.0 214.5 jit_solution(245271120795114434)
XLA Ops:
  6.5 3.2 %fusion.30 = f32[4096]{0:T(1024)S(1)} fusion(bf16[4096,512]{1,0:T(8,128)(2,1)} %param.10), kind=kLoop, calls=%fused_computation.40 | loop fusion | flops 6287360 | bytes 4210688 | tf_op jit(solution)/shard_map/reduce_sum | solution.py:26
  15.5 3.1 %collective-permute-start = (bf16[2,256,256]{1,2,0:T(8,128)(2,1)}, bf16[2,256,256]{1,2,0:T(8,128)(2,1)S(1)}, u32[]{:S(2)}, u32[]{:S(2)}) collective-permute-start(bf16[2,256,256]{1,2,0:T(8,128)(2,1)} %get-tuple-element.173), channel_id=1, source_target_pairs={{0,2},{2,4},{4,6},{6,8},{8,10},{10,12},{12,14},{1,3},{3,5},{5,7},{... | collective-permute-start | bytes 786440 | tf_op jit(solution)/shard_map/ppermute | solution.py:17
  22.1 3.6 %multiply_reduce_fusion = (f32[4096,4]{0,1:T(4,128)S(1)}, f32[4096,256]{0,1:T(8,128)S(1)}) fusion(bf16[4096,512]{1,0:T(8,128)(2,1)} %copy-done.1, bf16[512,256]{1,0:T(8,128)(2,1)S(1)} %copy-done.5), kind=kOutput, calls=%fused_computation.51 | convolution fusion | flops 1075822592 | bytes 8716288 | tf_op jit(solution)/shard_map/dot_general | solution.py:44
  28.8 25.3 %all_gather.3 = bf16[2,32,256]{2,0,1:T(2,128)(2,1)S(1)} all-gather(bf16[2,4,256]{2,0,1:T(2,128)(2,1)S(1)} %copy.19), channel_id=1, replica_groups=mesh['fields'=2,'seq'=8,'head'=2] {'seq'}, dimensions={1}, use_global_device_ids=true | all-gather | bytes 36864 | tf_op jit(solution)/shard_map/all_gather | solution.py:66
  54.2 3.6 %pad_maximum_fusion = bf16[2,4608,256]{1,2,0:T(8,128)(2,1)} fusion(bf16[2,256,256]{1,2,0:T(8,128)(2,1)} %collective-permute-done.1, bf16[1,4096,256]{1,2,0:T(8,128)(2,1)} %copy-done.3, bf16[1,4096,256]{1,2,0:T(8,128)(2,1)S(1)} %bitcast.76, bf16[2,256,256]{1,2,0:T(8,128)(2,1)S(1)} %collective-permute-done), kind=kLoop, calls=%fused_computation.46 | loop fusion | flops 18874368 | bytes 9437184 | tf_op jit(solution)/shard_map/concatenate | solution.py:21
  57.8 114.6 %while.13 = (s32[]{:T(128)}, bf16[8,512,256]{2,1,0:T(8,128)(2,1)}, bf16[2,4608,4,64]{1,3,2,0:T(8,128)(2,1)}, s32[8]{0:T(128)S(1)}, s32[]{:T(128)}, /*index=5*/bf...) while((s32[]{:T(128)}, bf16[8,512,256]{2,1,0:T(8,128)(2,1)}, ...), condition=%wide.region_11.12_spmd.clone, body=%wide.region_6.11_spmd.clone.sunk | while | flops 575800320 | bytes 41618152 | solution.py:106
  59.7 2.8 %fusion.67 = (bf16[1,4608,4,64]{1,3,2,0:T(8,128)(2,1)S(1)}, bf16[1,4608,4,64]{1,3,2,0:T(8,128)(2,1)S(1)}) fusion(bf16[2,4608,4,64]{1,3,2,0:T(8,128)(2,1)} %get-tuple-element.262), kind=kLoop, calls=%fused_computation.71.clone.1 | loop fusion | bytes 9437184 | tf_op jit(solution)/shard_map/while/body/eval_jaxpr/slice | solution.py:80
  62.5 2.5 %select_reduce_fusion.2 = (f32[4,512]{1,0:T(4,128)S(1)}, f32[4,512,1024]{2,1,0:T(8,128)S(1)}) fusion(pred[512,1024]{1,0:T(8,128)(4,1)S(1)} %fusion.66, bf16[1,4608,4,64]{1,3,2,0:T(8,128)(2,1)S(1)} %get-tuple-element.230, s32[]{:T(128)S(6)} %select_n.44, bf16[4096,4,64]{0,2,1:T(8,128)(2,1)} %get-tuple-element.265, s32[]{:T(128)S(6)} %select_n.45), kind=kOutput, calls=%fused_computation.3.clone.1 | convolution fusion | flops 272627712 | bytes 9707528 | tf_op jit(solution)/shard_map/while/body/eval_jaxpr/qhd,khd->hqk/dot_general | solution.py:81
  68.5 2.5 %fusion.71 = f32[512,4,64]{0,2,1:T(8,128)S(1)} fusion(f32[4,512,1024]{2,1,0:T(8,128)S(1)} %get-tuple-element.231, f32[4,512]{1,0:T(4,128)S(1)} %add.173, f32[4,512]{1,0:T(4,128)S(1)} %max.13, pred[512,1024]{1,0:T(8,128)(4,1)S(1)} %fusion.66, bf16[1,4608,4,64]{1,3,2,0:T(8,128)(2,1)S(1)} %get-tuple-element.235, s32[]{:T(128)S(6)} %select_n.44), kind=kOutput, calls=%fused_computation.8.clone.1 | convolution fusion | flops 276824064 | bytes 9977860 | tf_op jit(solution)/shard_map/while/body/eval_jaxpr/hqk,khd->qhd/dot_general | solution.py:98
  74.0 2.8 %fusion.67 = (bf16[1,4608,4,64]{1,3,2,0:T(8,128)(2,1)S(1)}, bf16[1,4608,4,64]{1,3,2,0:T(8,128)(2,1)S(1)}) fusion(bf16[2,4608,4,64]{1,3,2,0:T(8,128)(2,1)} %get-tuple-element.262), kind=kLoop, calls=%fused_computation.71.clone.1 | loop fusion | bytes 9437184 | tf_op jit(solution)/shard_map/while/body/eval_jaxpr/slice | solution.py:80
  76.8 2.5 %select_reduce_fusion.2 = (f32[4,512]{1,0:T(4,128)S(1)}, f32[4,512,1024]{2,1,0:T(8,128)S(1)}) fusion(pred[512,1024]{1,0:T(8,128)(4,1)S(1)} %fusion.66, bf16[1,4608,4,64]{1,3,2,0:T(8,128)(2,1)S(1)} %get-tuple-element.230, s32[]{:T(128)S(6)} %select_n.44, bf16[4096,4,64]{0,2,1:T(8,128)(2,1)} %get-tuple-element.265, s32[]{:T(128)S(6)} %select_n.45), kind=kOutput, calls=%fused_computation.3.clone.1 | convolution fusion | flops 272627712 | bytes 9707528 | tf_op jit(solution)/shard_map/while/body/eval_jaxpr/qhd,khd->hqk/dot_general | solution.py:81
  82.8 2.5 %fusion.71 = f32[512,4,64]{0,2,1:T(8,128)S(1)} fusion(f32[4,512,1024]{2,1,0:T(8,128)S(1)} %get-tuple-element.231, f32[4,512]{1,0:T(4,128)S(1)} %add.173, f32[4,512]{1,0:T(4,128)S(1)} %max.13, pred[512,1024]{1,0:T(8,128)(4,1)S(1)} %fusion.66, bf16[1,4608,4,64]{1,3,2,0:T(8,128)(2,1)S(1)} %get-tuple-element.235, s32[]{:T(128)S(6)} %select_n.44), kind=kOutput, calls=%fused_computation.8.clone.1 | convolution fusion | flops 276824064 | bytes 9977860 | tf_op jit(solution)/shard_map/while/body/eval_jaxpr/hqk,khd->qhd/dot_general | solution.py:98
  88.3 2.8 %fusion.67 = (bf16[1,4608,4,64]{1,3,2,0:T(8,128)(2,1)S(1)}, bf16[1,4608,4,64]{1,3,2,0:T(8,128)(2,1)S(1)}) fusion(bf16[2,4608,4,64]{1,3,2,0:T(8,128)(2,1)} %get-tuple-element.262), kind=kLoop, calls=%fused_computation.71.clone.1 | loop fusion | bytes 9437184 | tf_op jit(solution)/shard_map/while/body/eval_jaxpr/slice | solution.py:80
  91.2 2.5 %select_reduce_fusion.2 = (f32[4,512]{1,0:T(4,128)S(1)}, f32[4,512,1024]{2,1,0:T(8,128)S(1)}) fusion(pred[512,1024]{1,0:T(8,128)(4,1)S(1)} %fusion.66, bf16[1,4608,4,64]{1,3,2,0:T(8,128)(2,1)S(1)} %get-tuple-element.230, s32[]{:T(128)S(6)} %select_n.44, bf16[4096,4,64]{0,2,1:T(8,128)(2,1)} %get-tuple-element.265, s32[]{:T(128)S(6)} %select_n.45), kind=kOutput, calls=%fused_computation.3.clone.1 | convolution fusion | flops 272627712 | bytes 9707528 | tf_op jit(solution)/shard_map/while/body/eval_jaxpr/qhd,khd->hqk/dot_general | solution.py:81
  97.1 2.5 %fusion.71 = f32[512,4,64]{0,2,1:T(8,128)S(1)} fusion(f32[4,512,1024]{2,1,0:T(8,128)S(1)} %get-tuple-element.231, f32[4,512]{1,0:T(4,128)S(1)} %add.173, f32[4,512]{1,0:T(4,128)S(1)} %max.13, pred[512,1024]{1,0:T(8,128)(4,1)S(1)} %fusion.66, bf16[1,4608,4,64]{1,3,2,0:T(8,128)(2,1)S(1)} %get-tuple-element.235, s32[]{:T(128)S(6)} %select_n.44), kind=kOutput, calls=%fused_computation.8.clone.1 | convolution fusion | flops 276824064 | bytes 9977860 | tf_op jit(solution)/shard_map/while/body/eval_jaxpr/hqk,khd->qhd/dot_general | solution.py:98
  102.6 2.8 %fusion.67 = (bf16[1,4608,4,64]{1,3,2,0:T(8,128)(2,1)S(1)}, bf16[1,4608,4,64]{1,3,2,0:T(8,128)(2,1)S(1)}) fusion(bf16[2,4608,4,64]{1,3,2,0:T(8,128)(2,1)} %get-tuple-element.262), kind=kLoop, calls=%fused_computation.71.clone.1 | loop fusion | bytes 9437184 | tf_op jit(solution)/shard_map/while/body/eval_jaxpr/slice | solution.py:80
  105.5 2.5 %select_reduce_fusion.2 = (f32[4,512]{1,0:T(4,128)S(1)}, f32[4,512,1024]{2,1,0:T(8,128)S(1)}) fusion(pred[512,1024]{1,0:T(8,128)(4,1)S(1)} %fusion.66, bf16[1,4608,4,64]{1,3,2,0:T(8,128)(2,1)S(1)} %get-tuple-element.230, s32[]{:T(128)S(6)} %select_n.44, bf16[4096,4,64]{0,2,1:T(8,128)(2,1)} %get-tuple-element.265, s32[]{:T(128)S(6)} %select_n.45), kind=kOutput, calls=%fused_computation.3.clone.1 | convolution fusion | flops 272627712 | bytes 9707528 | tf_op jit(solution)/shard_map/while/body/eval_jaxpr/qhd,khd->hqk/dot_general | solution.py:81
  111.5 2.5 %fusion.71 = f32[512,4,64]{0,2,1:T(8,128)S(1)} fusion(f32[4,512,1024]{2,1,0:T(8,128)S(1)} %get-tuple-element.231, f32[4,512]{1,0:T(4,128)S(1)} %add.173, f32[4,512]{1,0:T(4,128)S(1)} %max.13, pred[512,1024]{1,0:T(8,128)(4,1)S(1)} %fusion.66, bf16[1,4608,4,64]{1,3,2,0:T(8,128)(2,1)S(1)} %get-tuple-element.235, s32[]{:T(128)S(6)} %select_n.44), kind=kOutput, calls=%fused_computation.8.clone.1 | convolution fusion | flops 276824064 | bytes 9977860 | tf_op jit(solution)/shard_map/while/body/eval_jaxpr/hqk,khd->qhd/dot_general | solution.py:98
  116.9 2.8 %fusion.67 = (bf16[1,4608,4,64]{1,3,2,0:T(8,128)(2,1)S(1)}, bf16[1,4608,4,64]{1,3,2,0:T(8,128)(2,1)S(1)}) fusion(bf16[2,4608,4,64]{1,3,2,0:T(8,128)(2,1)} %get-tuple-element.262), kind=kLoop, calls=%fused_computation.71.clone.1 | loop fusion | bytes 9437184 | tf_op jit(solution)/shard_map/while/body/eval_jaxpr/slice | solution.py:80
  119.8 2.5 %select_reduce_fusion.2 = (f32[4,512]{1,0:T(4,128)S(1)}, f32[4,512,1024]{2,1,0:T(8,128)S(1)}) fusion(pred[512,1024]{1,0:T(8,128)(4,1)S(1)} %fusion.66, bf16[1,4608,4,64]{1,3,2,0:T(8,128)(2,1)S(1)} %get-tuple-element.230, s32[]{:T(128)S(6)} %select_n.44, bf16[4096,4,64]{0,2,1:T(8,128)(2,1)} %get-tuple-element.265, s32[]{:T(128)S(6)} %select_n.45), kind=kOutput, calls=%fused_computation.3.clone.1 | convolution fusion | flops 272627712 | bytes 9707528 | tf_op jit(solution)/shard_map/while/body/eval_jaxpr/qhd,khd->hqk/dot_general | solution.py:81
  125.8 2.5 %fusion.71 = f32[512,4,64]{0,2,1:T(8,128)S(1)} fusion(f32[4,512,1024]{2,1,0:T(8,128)S(1)} %get-tuple-element.231, f32[4,512]{1,0:T(4,128)S(1)} %add.173, f32[4,512]{1,0:T(4,128)S(1)} %max.13, pred[512,1024]{1,0:T(8,128)(4,1)S(1)} %fusion.66, bf16[1,4608,4,64]{1,3,2,0:T(8,128)(2,1)S(1)} %get-tuple-element.235, s32[]{:T(128)S(6)} %select_n.44), kind=kOutput, calls=%fused_computation.8.clone.1 | convolution fusion | flops 276824064 | bytes 9977860 | tf_op jit(solution)/shard_map/while/body/eval_jaxpr/hqk,khd->qhd/dot_general | solution.py:98
  131.3 2.8 %fusion.67 = (bf16[1,4608,4,64]{1,3,2,0:T(8,128)(2,1)S(1)}, bf16[1,4608,4,64]{1,3,2,0:T(8,128)(2,1)S(1)}) fusion(bf16[2,4608,4,64]{1,3,2,0:T(8,128)(2,1)} %get-tuple-element.262), kind=kLoop, calls=%fused_computation.71.clone.1 | loop fusion | bytes 9437184 | tf_op jit(solution)/shard_map/while/body/eval_jaxpr/slice | solution.py:80
  134.1 2.5 %select_reduce_fusion.2 = (f32[4,512]{1,0:T(4,128)S(1)}, f32[4,512,1024]{2,1,0:T(8,128)S(1)}) fusion(pred[512,1024]{1,0:T(8,128)(4,1)S(1)} %fusion.66, bf16[1,4608,4,64]{1,3,2,0:T(8,128)(2,1)S(1)} %get-tuple-element.230, s32[]{:T(128)S(6)} %select_n.44, bf16[4096,4,64]{0,2,1:T(8,128)(2,1)} %get-tuple-element.265, s32[]{:T(128)S(6)} %select_n.45), kind=kOutput, calls=%fused_computation.3.clone.1 | convolution fusion | flops 272627712 | bytes 9707528 | tf_op jit(solution)/shard_map/while/body/eval_jaxpr/qhd,khd->hqk/dot_general | solution.py:81
  140.1 2.5 %fusion.71 = f32[512,4,64]{0,2,1:T(8,128)S(1)} fusion(f32[4,512,1024]{2,1,0:T(8,128)S(1)} %get-tuple-element.231, f32[4,512]{1,0:T(4,128)S(1)} %add.173, f32[4,512]{1,0:T(4,128)S(1)} %max.13, pred[512,1024]{1,0:T(8,128)(4,1)S(1)} %fusion.66, bf16[1,4608,4,64]{1,3,2,0:T(8,128)(2,1)S(1)} %get-tuple-element.235, s32[]{:T(128)S(6)} %select_n.44), kind=kOutput, calls=%fused_computation.8.clone.1 | convolution fusion | flops 276824064 | bytes 9977860 | tf_op jit(solution)/shard_map/while/body/eval_jaxpr/hqk,khd->qhd/dot_general | solution.py:98
  145.6 2.8 %fusion.67 = (bf16[1,4608,4,64]{1,3,2,0:T(8,128)(2,1)S(1)}, bf16[1,4608,4,64]{1,3,2,0:T(8,128)(2,1)S(1)}) fusion(bf16[2,4608,4,64]{1,3,2,0:T(8,128)(2,1)} %get-tuple-element.262), kind=kLoop, calls=%fused_computation.71.clone.1 | loop fusion | bytes 9437184 | tf_op jit(solution)/shard_map/while/body/eval_jaxpr/slice | solution.py:80
  148.4 2.5 %select_reduce_fusion.2 = (f32[4,512]{1,0:T(4,128)S(1)}, f32[4,512,1024]{2,1,0:T(8,128)S(1)}) fusion(pred[512,1024]{1,0:T(8,128)(4,1)S(1)} %fusion.66, bf16[1,4608,4,64]{1,3,2,0:T(8,128)(2,1)S(1)} %get-tuple-element.230, s32[]{:T(128)S(6)} %select_n.44, bf16[4096,4,64]{0,2,1:T(8,128)(2,1)} %get-tuple-element.265, s32[]{:T(128)S(6)} %select_n.45), kind=kOutput, calls=%fused_computation.3.clone.1 | convolution fusion | flops 272627712 | bytes 9707528 | tf_op jit(solution)/shard_map/while/body/eval_jaxpr/qhd,khd->hqk/dot_general | solution.py:81
  154.4 2.5 %fusion.71 = f32[512,4,64]{0,2,1:T(8,128)S(1)} fusion(f32[4,512,1024]{2,1,0:T(8,128)S(1)} %get-tuple-element.231, f32[4,512]{1,0:T(4,128)S(1)} %add.173, f32[4,512]{1,0:T(4,128)S(1)} %max.13, pred[512,1024]{1,0:T(8,128)(4,1)S(1)} %fusion.66, bf16[1,4608,4,64]{1,3,2,0:T(8,128)(2,1)S(1)} %get-tuple-element.235, s32[]{:T(128)S(6)} %select_n.44), kind=kOutput, calls=%fused_computation.8.clone.1 | convolution fusion | flops 276824064 | bytes 9977860 | tf_op jit(solution)/shard_map/while/body/eval_jaxpr/hqk,khd->qhd/dot_general | solution.py:98
  159.9 2.8 %fusion.67 = (bf16[1,4608,4,64]{1,3,2,0:T(8,128)(2,1)S(1)}, bf16[1,4608,4,64]{1,3,2,0:T(8,128)(2,1)S(1)}) fusion(bf16[2,4608,4,64]{1,3,2,0:T(8,128)(2,1)} %get-tuple-element.262), kind=kLoop, calls=%fused_computation.71.clone.1 | loop fusion | bytes 9437184 | tf_op jit(solution)/shard_map/while/body/eval_jaxpr/slice | solution.py:80
  168.7 2.5 %fusion.71 = f32[512,4,64]{0,2,1:T(8,128)S(1)} fusion(f32[4,512,1024]{2,1,0:T(8,128)S(1)} %get-tuple-element.231, f32[4,512]{1,0:T(4,128)S(1)} %add.173, f32[4,512]{1,0:T(4,128)S(1)} %max.13, pred[512,1024]{1,0:T(8,128)(4,1)S(1)} %fusion.66, bf16[1,4608,4,64]{1,3,2,0:T(8,128)(2,1)S(1)} %get-tuple-element.235, s32[]{:T(128)S(6)} %select_n.44), kind=kOutput, calls=%fused_computation.8.clone.1 | convolution fusion | flops 276824064 | bytes 9977860 | tf_op jit(solution)/shard_map/while/body/eval_jaxpr/hqk,khd->qhd/dot_general | solution.py:98
  172.4 6.1 %fusion.36 = f32[4096,512]{1,0:T(8,128)} fusion(bf16[4096,256]{1,0:T(8,128)(2,1)} %bitcast.78, bf16[512,512]{1,0:T(8,128)(2,1)S(1)} %copy-done, s32[]{:T(128)S(6)} %select_n.23), kind=kOutput, calls=%fused_computation.56 | convolution fusion | flops 1073741824 | bytes 10747908 | tf_op jit(solution)/shard_map/dot_general | solution.py:111
  178.5 25.5 %reduce-scatter.2.cloned.1.call-done = f32[4096,256]{1,0:T(8,128)} async-done(((f32[4096,512]{1,0:T(8,128)}), f32[4096,256]{1,0:T(8,128)}) %reduce-scatter.2.cloned.1.call-update) | async-done | bytes 4194320 | tf_op jit(solution)/shard_map/reduce_scatter | solution.py:112
  204.0 3.7 %convert_element_type.64 = bf16[4096,256]{1,0:T(8,128)(2,1)} convert(f32[4096,256]{1,0:T(8,128)} %reduce-scatter.2.cloned.1.call-done) | non-fusion elementwise | flops 1048576 | bytes 6291456 | tf_op jit(solution)/shard_map/convert_element_type | solution.py:113
  (141 shorter events, 60.5 us)
Async XLA Ops:
  6.5 165.9 %copy-start = (bf16[512,512]{1,0:T(8,128)(2,1)S(1)}, bf16[512,512]{1,0:T(8,128)(2,1)}, u32[]{:S(2)}) copy-start(bf16[512,512]{1,0:T(8,128)(2,1)} %param.16) | copy-start | bytes 1572868
  6.5 3.3 %copy-start.6 = (f32[512]{0:T(512)S(1)}, f32[512]{0:T(512)}, u32[]{:S(2)}) copy-start(f32[512]{0:T(512)} %param.11) | copy-start | bytes 6148
  6.5 197.4 %reduce-scatter.2.cloned.1.call-start = ((), (), s32[]{:S(2)}) async-start(), calls=%async_computation.1 | async-start | bytes 12582912 | tf_op jit(solution)/shard_map/reduce_scatter | solution.py:112
  6.5 3.5 %copy-start.2 = (bf16[4096,512]{1,0:T(8,128)(2,1)S(1)}, bf16[4096,512]{1,0:T(8,128)(2,1)}, u32[]{:S(2)}) copy-start(bf16[4096,512]{1,0:T(8,128)(2,1)} %param.10) | copy-start | bytes 12582916
  10.1 1.1 copy-start.4
  11.2 9.6 %copy-start.1 = (bf16[4096,512]{1,0:T(8,128)(2,1)}, bf16[4096,512]{1,0:T(8,128)(2,1)S(1)}, u32[]{:S(2)}) copy-start(bf16[4096,512]{1,0:T(8,128)(2,1)S(1)} %fusion.32) | copy-start | bytes 12582916
  11.2 1.5 copy-start.7
  14.0 1.5 copy-start.3
  14.4 7.1 %copy-start.8 = (f32[512]{0:T(512)S(1)}, f32[512]{0:T(512)}, u32[]{:S(2)}) copy-start(f32[512]{0:T(512)} %param.12) | copy-start | bytes 6148
  14.4 7.6 %copy-start.5 = (bf16[512,256]{1,0:T(8,128)(2,1)S(1)}, bf16[512,256]{1,0:T(8,128)(2,1)}, u32[]{:S(2)}) copy-start(bf16[512,256]{1,0:T(8,128)(2,1)} %param.13) | copy-start | bytes 786436
  15.5 38.7 %collective-permute-start = (bf16[2,256,256]{1,2,0:T(8,128)(2,1)}, bf16[2,256,256]{1,2,0:T(8,128)(2,1)S(1)}, u32[]{:S(2)}, u32[]{:S(2)}) collective-permute-start(bf16[2,256,256]{1,2,0:T(8,128)(2,1)} %get-tuple-element.173), channel_id=1, source_target_pairs={{0,2},{2,4},{4,6},{6,8},{8,10},{10,12},{12,14},{1,3},{3,5},{5,7},{... | collective-permute-start | bytes 786440 | tf_op jit(solution)/shard_map/ppermute | solution.py:17
  18.6 35.5 %collective-permute-start.1 = (bf16[2,256,256]{1,2,0:T(8,128)(2,1)S(1)}, bf16[2,256,256]{1,2,0:T(8,128)(2,1)}, u32[]{:S(2)}, u32[]{:S(2)}) collective-permute-start(bf16[2,256,256]{1,2,0:T(8,128)(2,1)S(1)} %get-tuple-element.174), channel_id=1, source_target_pairs={{2,0},{4,2},{6,4},{8,6},{10,8},{12,10},{14,12},{3,1},{5,3},{7,5},{... | collective-permute-start | bytes 786440 | tf_op jit(solution)/shard_map/ppermute | solution.py:20
  22.0 3.6 %copy-start.9 = (f32[4]{0:T(128)S(1)}, f32[4]{0:T(128)}, u32[]{:S(2)}) copy-start(f32[4]{0:T(128)} %param.17) | copy-start | bytes 52
Sparse Core Ops, SparseCore 0:
  178.6 25.2 reduce-scatter.1
where the time goes:
time: 216 us; the launch traced here: 215 us
  matrix products  64.9 us (30%)
  other arithmetic  37.8 us (17%)
  local copies, waits for them, and re-layouts  36 us (17%)
  waiting for transfers between devices  25.5 us (12%)
  blocking collectives  25.3 us (12%)
  between operations  13.6 us (6%)
  loops' own time  6.09 us (3%)
  starting transfers between devices  5.28 us (2%)
    reduce_scatter x1, waiting for transfers between devices, body(): lax.psum_scatter(partial_out, 'head', scatter_dimension=1, tiled=True)  25.5 us
    all_gather x1, blocking collectives, body(): coarse_all = lax.all_gather(coarse_stack, 'seq', axis=1, tiled=True)  25.3 us
    slice x8, local copies, waits for them, and re-layouts, one_block(): block_values = lax.dynamic_slice_in_dim(extended[1], row_start, span, 0)  22.7 us
    dot_general x8, matrix products, one_block(): jnp.einsum('hqk,khd->qhd', band_weights, block_values, preferred_element_...  20.1 us
    dot_general x8, matrix products, one_block(): jnp.einsum('qhd,khd->hqk', block_queries, block_keys, preferred_element_t...  19.9 us
    reduce_sum x8, other arithmetic, one_block(): jnp.sum(band_exp, axis=-1, keepdims=True)  18.2 us
    dot_general x8, matrix products, one_block(): jnp.einsum('qhd,khd->hqk', block_queries, coarse_all[0], preferred_elemen...  9.05 us
    dynamic_update_slice x16, local copies, waits for them, and re-layouts, body(): lax.map(one_block, jnp.arange(tok_count // QB, dtype=jnp.int32))  6.92 us
  transfers between devices with their start and end apart: 3, of which 1 were waited for; matrix products, arithmetic and copies ran while one was open for 4% of the time, Pallas kernels for 0%

commit v1 on v0

v1 whole, which is shorter than its diff:
```python
import functools

import jax
import jax.numpy as jnp
from jax import lax
from jax.experimental import pallas as pl
from jax.experimental.pallas import tpu as pltpu
from jax.sharding import PartitionSpec as P

HEAD_DIM = 64
WINDOW = 256
POOL = 1024
BQ = 128
SPAN = BQ + 2 * WINDOW
TILES = SPAN // 128
STRIP = 16
NORM_ROWS = 512
PROJ_ROWS = 512
HIDDEN = -1e30
CHUNKS = 2

VMEM = pl.BlockSpec(memory_space=pltpu.VMEM)
ANY = pl.BlockSpec(memory_space=pl.ANY)
BF16 = jnp.bfloat16
F32 = jnp.float32


def sds(shape, dtype):
    return jax.ShapeDtypeStruct(shape, dtype)


def dot(a, b):
    return jnp.dot(a, b, preferred_element_type=F32)


def call(kernel, outs, *args, in_specs=None, out_specs=None, scratch=(), limit=24, flops=0, name=None):
    cost = pl.CostEstimate(flops=flops, bytes_accessed=4 << 20, transcendentals=0)
    return pl.pallas_call(
        kernel,
        out_shape=outs,
        in_specs=in_specs or [VMEM] * len(args),
        out_specs=out_specs or jax.tree.map(lambda _: VMEM, outs),
        scratch_shapes=scratch,
        compiler_params=pltpu.CompilerParams(vmem_limit_bytes=limit << 20),
        cost_estimate=cost,
        name=name,
    )(*args)


def rms(x, gain):
    return x * lax.rsqrt(jnp.mean(x * x, axis=-1, keepdims=True) + 1e-05) * gain


def unit(x, ones_ref):
    square = x * x
    high = square.astype(BF16)
    low = (square - high.astype(F32)).astype(BF16)
    mean = dot(high, ones_ref[...]) + dot(low, ones_ref[...])
    return x * lax.rsqrt(mean + 1e-06)


def norm_kernel(tok_ref, gain_ref, coarse_gain_ref, normed_ref, coarse_ref, buf, sems):
    rows = tok_ref.shape[0]
    count = rows // NORM_ROWS
    copies = []
    for c in range(count):
        part = pl.ds(c * NORM_ROWS, NORM_ROWS)
        copies.append(pltpu.make_async_copy(tok_ref.at[part], buf.at[part], sems.at[c]))
        copies[-1].start()
    gain = gain_ref[...]
    ones = jnp.ones((8, NORM_ROWS), BF16)
    pooled = []
    for c in range(count):
        part = pl.ds(c * NORM_ROWS, NORM_ROWS)
        copies[c].wait()
        normed = rms(buf[part, :].astype(F32), gain).astype(BF16)
        normed_ref[part, :] = normed
        total = dot(ones, normed)[:1]
        if c * NORM_ROWS % POOL:
            pooled[-1] = pooled[-1] + total
        else:
            pooled.append(total)
    pooled = jnp.concatenate(pooled, 0) * (1.0 / POOL)
    coarse_ref[...] = rms(pooled, coarse_gain_ref[...]).astype(BF16)


def query_kernel(normed_ref, w_ref, ones_ref, factor_ref, q_ref):
    @pl.loop(0, normed_ref.shape[0] // PROJ_ROWS)
    def _(c):
        part = pl.ds(pl.multiple_of(c * PROJ_ROWS, PROJ_ROWS), PROJ_ROWS)
        q = unit(dot(normed_ref[part, :], w_ref[...]), ones_ref) * factor_ref[...]
        q_ref[part, :] = q.astype(BF16)


def key_value_kernel(
    normed_ref, mine_ref, other_ref, gain_ref, wk_ref, wv_ref, ones_ref, k_ref, v_ref
):
    rows = normed_ref.shape[0]
    half = WINDOW // 2

    @pl.loop(0, rows // PROJ_ROWS)
    def _(c):
        part = pl.ds(pl.multiple_of(c * PROJ_ROWS, PROJ_ROWS), PROJ_ROWS)
        out = pl.ds(pl.multiple_of(c * PROJ_ROWS + WINDOW, WINDOW), PROJ_ROWS)
        normed = normed_ref[part, :]
        k_ref[out, :] = unit(dot(normed, wk_ref[...]), ones_ref).astype(BF16)
        v_ref[out, :] = dot(normed, wv_ref[...]).astype(BF16)

    far = jnp.concatenate([mine_ref[...], other_ref[...]], 0)
    normed = rms(far.astype(F32), gain_ref[...]).astype(BF16)
    keys = unit(dot(normed, wk_ref[...]), ones_ref).astype(BF16)
    values = dot(normed, wv_ref[...]).astype(BF16)
    odd = lax.axis_index("seq") % 2
    core = lax.axis_index("head")
    for piece in range(4):
        at_low = odd if piece % 2 == 0 else 1 - odd
        side = core if piece < 2 else 1 - core
        start = jnp.where(at_low == 1, 0, rows + WINDOW) + side * half
        out = pl.ds(pl.multiple_of(start, half), half)
        k_ref[out, :] = keys[piece * half : (piece + 1) * half]
        v_ref[out, :] = values[piece * half : (piece + 1) * half]


def attention_kernel(
    base, q_ref, k_ref, v_ref, coarse_ref, wk_ref, wv_ref, ones_ref, o_ref, s_ref, p_ref, far_ref
):
    blocks = o_ref.shape[0] // BQ
    width = q_ref.shape[1]
    heads = width // HEAD_DIM
    stack = heads * BQ
    far_count = coarse_ref.shape[0]
    far_width = far_ref.shape[1]
    far_tiles = far_width // 128
    tiles = TILES + far_tiles
    all_blocks = q_ref.shape[0] // BQ
    lane_head = lax.broadcasted_iota(jnp.int32, (BQ, width), 1) // HEAD_DIM
    seq_index = lax.axis_index("seq")
    is_first = seq_index == 0
    is_last = seq_index == lax.axis_size("seq") - 1

    far_ref[...] = jnp.zeros_like(far_ref)
    coarse = coarse_ref[...]
    far_ref[0, :far_count, :] = unit(dot(coarse, wk_ref[...]), ones_ref).astype(BF16)
    far_ref[1, :far_count, :] = dot(coarse, wv_ref[...]).astype(BF16)

    def rows_at(b, size):
        return pl.ds(pl.multiple_of(base + b * BQ, BQ), size)

    def scores(b, slot):
        q = q_ref[rows_at(b, BQ), :]
        queries = jnp.concatenate(
            [jnp.where(lane_head == h, q, jnp.zeros_like(q)) for h in range(heads)], 0
        )
        keys = jnp.concatenate([k_ref[rows_at(b, SPAN), :], far_ref[0]], 0)
        s_ref[slot] = lax.dot_general(
            queries, keys, (((1,), (1,)), ((), ())), preferred_element_type=F32
        )

    def hide_outside(b, slot):
        block = base // BQ + b
        for edge, distance, near, outer in (
            (is_first, block, 1, 0),
            (is_last, all_blocks - 1 - block, TILES - 2, TILES - 1),
        ):
            for tile, reach in ((near, 1), (outer, 2)):

                @pl.when(edge & (distance < reach))
                def _():
                    s_ref[slot, :, tile * 128 : tile * 128 + 128] = jnp.full(
                        (stack, 128), HIDDEN, F32
                    )

    def softmax(slot):
        lane = lax.broadcasted_iota(jnp.int32, (STRIP, 128), 1)
        ahead = lane - lax.broadcasted_iota(jnp.int32, (STRIP, 128), 0)
        for r in range(0, stack, STRIP):
            at = r % BQ
            part = [s_ref[slot, r : r + STRIP, 128 * t : 128 * t + 128] for t in range(tiles)]
            part[0] = jnp.where(ahead >= at, part[0], HIDDEN)
            part[TILES - 1] = jnp.where(ahead <= at, part[TILES - 1], HIDDEN)
            if far_count < far_width:
                used = far_count - (far_tiles - 1) * 128
                part[-1] = jnp.where(lane < used, part[-1], HIDDEN)
            peak = jnp.max(functools.reduce(jnp.maximum, part), axis=1, keepdims=True)
            part = [jnp.exp(x - peak) for x in part]
            total = jnp.sum(functools.reduce(jnp.add, part), axis=1, keepdims=True)
            scale = 1.0 / total
            for t in range(tiles):
                p_ref[slot, r : r + STRIP, 128 * t : 128 * t + 128] = (part[t] * scale).astype(BF16)

    def mix(b, slot):
        values = jnp.concatenate([v_ref[rows_at(b, SPAN), :], far_ref[1]], 0)
        mixed = dot(p_ref[slot], values)
        out = mixed[:BQ]
        for h in range(1, heads):
            out = jnp.where(lane_head == h, mixed[h * BQ : (h + 1) * BQ], out)
        o_ref[pl.ds(pl.multiple_of(b * BQ, BQ), BQ), :] = out.astype(BF16)

    scores(0, 0)

    @pl.loop(0, blocks // 2)
    def _(i):
        for slot in range(2):
            b = 2 * i + slot
            hide_outside(b, slot)
            mix(jnp.maximum(b - 1, 0), 1 - slot)
            scores(jnp.minimum(b + 1, blocks - 1), 1 - slot)
            softmax(slot)

    mix(blocks - 1, 1)


def out_kernel(own_ref, other_ref, w_ref, *rest):
    o_ref = rest[-1]
    core = lax.axis_index("head")
    width = own_ref.shape[1]

    def weight(rows_of):
        rows = pl.ds(pl.multiple_of(rows_of * width, width), width)
        return w_ref[rows, pl.ds(pl.multiple_of(core * width, width), width)]

    out = dot(own_ref[...], weight(core)) + dot(other_ref[...], weight(1 - core))
    o_ref[...] = out.astype(BF16)


def swap_heads(x):
    return lax.ppermute(x, "head", [(0, 1), (1, 0)])


def halo_rows(tokens, seq_size):
    rows = tokens.shape[0]
    half = WINDOW // 2
    even = lax.axis_index("seq") % 2 == 0
    side = lax.axis_index("head") * half
    first = lax.dynamic_slice_in_dim(tokens, jnp.where(even, rows - WINDOW, 0) + side, half, 0)
    second = lax.dynamic_slice_in_dim(tokens, jnp.where(even, 0, rows - WINDOW) + side, half, 0)
    moved = []
    for block, start in ((first, 0), (second, 1)):
        pairs = [(i, i + 1) for i in range(start, seq_size - 1, 2)]
        pairs = pairs + [(b, a) for a, b in pairs]
        moved.append(lax.ppermute(block, "seq", pairs))
    mine = jnp.concatenate(moved, 0)
    return mine, swap_heads(mine)


def gather_rows(rows, seq_size):
    if seq_size & (seq_size - 1):
        return lax.all_gather(rows, "seq", axis=0, tiled=True)
    step = 1
    while step < seq_size:
        pairs = [(i, i ^ step) for i in range(seq_size)]
        rows = jnp.concatenate([rows, lax.ppermute(rows, "seq", pairs)], 0)
        step *= 2
    return rows


def body(tokens, norm_gain, coarse_gain, w_query, w_key, w_value, w_out, score_scale):
    rows, full = tokens.shape
    heads = score_scale.shape[0]
    width = heads * HEAD_DIM
    seq_size = lax.axis_size("seq")
    gain = norm_gain[None]
    lane_head = jnp.arange(width) // HEAD_DIM
    ones = jnp.where(lane_head[:, None] == lane_head[None], 1.0 / HEAD_DIM, 0.0).astype(BF16)
    factor = jnp.repeat(score_scale * HEAD_DIM ** (-0.5), HEAD_DIM)[None]

    mine, other = halo_rows(tokens, seq_size)
    normed, coarse = call(
        norm_kernel,
        (sds((rows, full), BF16), sds((rows // POOL, full), BF16)),
        tokens,
        gain,
        coarse_gain[None],
        in_specs=[ANY, VMEM, VMEM],
        scratch=[
            pltpu.VMEM((rows, full), BF16),
            pltpu.SemaphoreType.DMA((rows // NORM_ROWS,)),
        ],
        flops=2 << 30,
        name="norm",
    )
    coarse_all = gather_rows(coarse, seq_size)
    queries = call(
        query_kernel,
        sds((rows, width), BF16),
        normed,
        w_query,
        ones,
        factor,
        flops=2 << 30,
        name="queries",
    )
    keys, values = call(
        key_value_kernel,
        (sds((rows + 2 * WINDOW, width), BF16),) * 2,
        normed,
        mine,
        other,
        gain,
        w_key,
        w_value,
        ones,
        flops=4 << 30,
        name="keys_values",
    )
    far_width = -(-coarse_all.shape[0] // 128) * 128
    chunk = rows // CHUNKS
    stack = heads * BQ
    out = ()
    for c in range(CHUNKS):
        attended = call(
            functools.partial(attention_kernel, c * chunk),
            sds((chunk, width), BF16),
            queries,
            keys,
            values,
            coarse_all,
            w_key,
            w_value,
            ones,
            scratch=[
                pltpu.VMEM((2, stack, SPAN + far_width), F32),
                pltpu.VMEM((2, stack, SPAN + far_width), BF16),
                pltpu.VMEM((2, far_width, width), BF16),
            ],
            flops=10 << 30,
            name="attention",
        )
        swapped = swap_heads(attended)
        first = c * chunk // PROJ_ROWS
        block = pl.BlockSpec((PROJ_ROWS, width), lambda i: (i, 0))
        out = pl.pallas_call(
            out_kernel,
            out_shape=sds((rows, width), BF16),
            grid=(chunk // PROJ_ROWS,),
            in_specs=[block, block, pl.BlockSpec((full, full), lambda i: (0, 0))] + [ANY] * (c > 0),
            out_specs=pl.BlockSpec((PROJ_ROWS, width), lambda i, first=first: (first + i, 0)),
            input_output_aliases={3: 0} if c else {},
            cost_estimate=pl.CostEstimate(
                flops=1 << 30, bytes_accessed=4 << 20, transcendentals=0
            ),
            name="out",
        )(attended, swapped, w_out, *([out] if c else []))
    return out


def solution(mesh):
    return jax.shard_map(
        body,
        mesh=mesh,
        in_specs=(
            P(("fields", "seq"), None),
            P(),
            P(),
            P(None, "head"),
            P(None, "head"),
            P(None, "head"),
            P(),
            P("head"),
        ),
        out_specs=P(("fields", "seq"), "head"),
        check_vma=False,
    )
```

time: 216 us -> 76 us (0.35)
  matrix products: 64.9 us -> 0 us
  Pallas kernels: 0 us -> 47.9 us
  other arithmetic: 37.8 us -> 0.14 us
  blocking collectives: 25.3 us -> 0 us
  local copies, waits for them, and re-layouts: 36 us -> 10.8 us
  waiting for transfers between devices: 25.5 us -> 3.4 us
  between operations: 13.6 us -> 0.21 us
  starting transfers between devices: 5.28 us -> 12.7 us
  loops' own time: 6.09 us -> 0 us
    dot_general x38 -> x0, matrix products: 64.9 us -> none  [the longest x8 20.1 us: one_block(): jnp.einsum('hqk,khd->qhd', band_weights, block_values, preferred_element_...]
    pallas_call x0 -> x7, Pallas kernels: none -> 47.9 us  [the longest x5 39.3 us: call(): pl.pallas_call(kernel, out_shape=outs, in_specs=in_specs or [VMEM] * len(...]
    reduce_scatter x1 -> x0, waiting for transfers between devices: 25.5 us -> none  [body(): lax.psum_scatter(partial_out, 'head', scatter_dimension=1, tiled=True)]
    all_gather x1 -> x0, blocking collectives: 25.3 us -> none  [body(): coarse_all = lax.all_gather(coarse_stack, 'seq', axis=1, tiled=True)]
    slice x8 -> x0, local copies, waits for them, and re-layouts: 22.7 us -> none  [one_block(): block_values = lax.dynamic_slice_in_dim(extended[1], row_start, span, 0)]
    reduce_sum x20 -> x0, other arithmetic: 22.7 us -> none  [the longest x8 18.2 us: one_block(): jnp.sum(band_exp, axis=-1, keepdims=True)]
    unnamed x21 -> x31, local copies, waits for them, and re-layouts: 0.65 us -> 9.66 us
    ppermute x2 -> x8, starting transfers between devices: 5.28 us -> 12.7 us  [the longest x3 4.52 us: swap_heads(): return lax.ppermute(x, 'head', [(0, 1), (1, 0)])]
  transfers between devices with their start and end apart: 3 -> 8, of which waited for: 1 -> 2; matrix products, arithmetic and copies ran while one was open for 4% -> 0% of each run, Pallas kernels for 0% -> 34%
where the time goes in v1:
time: 76 us; the launch traced here: 75.1 us
  Pallas kernels  47.9 us (63%)
  starting transfers between devices  12.7 us (17%)
  local copies, waits for them, and re-layouts  10.8 us (14%)
  waiting for transfers between devices  3.4 us (4%)
    pallas_call x5, Pallas kernels, call(): pl.pallas_call(kernel, out_shape=outs, in_specs=in_specs or [VMEM] * len(...  39.3 us
    unnamed x31, local copies, waits for them, and re-layouts  9.66 us
    pallas_call x2, Pallas kernels, body(): pl.pallas_call(out_kernel, out_shape=sds((rows, width), BF16), grid=(chun...  8.55 us
    ppermute x3, starting transfers between devices, swap_heads(): return lax.ppermute(x, 'head', [(0, 1), (1, 0)])  4.52 us
    ppermute x2, starting transfers between devices, halo_rows(): moved.append(lax.ppermute(block, 'seq', pairs))  4.44 us
    ppermute x3, starting transfers between devices, gather_rows(): rows = jnp.concatenate([rows, lax.ppermute(rows, 'seq', pairs)], 0)  3.74 us
    ppermute x3, waiting for transfers between devices, gather_rows(): rows = jnp.concatenate([rows, lax.ppermute(rows, 'seq', pairs)], 0)  3.38 us
  transfers between devices with their start and end apart: 8, of which 2 were waited for; matrix products, arithmetic and copies ran while one was open for 0% of the time, Pallas kernels for 34%

profile of v1, /device:TPU:7, one launch (start us, length us, event | category | flops | bytes accessed | tf_op | source)
XLA Modules:
  0.0 75.1 jit_solution(12612772172047995673)
XLA Ops:
  0.0 1.0 %constant_dynamic-slice_fusion = (bf16[128,512]{1,0:T(8,128)(2,1)S(1)}, bf16[128,512]{1,0:T(8,128)(2,1)S(1)}) fusion(bf16[4096,512]{1,0:T(8,128)(2,1)} %tok_ref.1, s32[]{:T(128)S(6)} %select_n.55, s32[]{:T(128)S(6)} %select_n.53), kind=kLoop, calls=%fused_computation.10 | loop fusion | bytes 524296 | tf_op jit(solution)/shard_map/dynamic_slice | solution.py:236
  1.0 0.3 collective-permute-start
  1.3 4.1 %collective-permute-start.1 = (bf16[128,512]{1,0:T(8,128)(2,1)S(1)}, bf16[128,512]{1,0:T(8,128)(2,1)S(1)}, u32[]{:S(2)}, u32[]{:S(2)}) collective-permute-start(bf16[128,512]{1,0:T(8,128)(2,1)S(1)} %get-tuple-element.13), channel_id=1, source_target_pairs={{2,4},{6,8},{10,12},{4,2},{8,6},{12,10},{3,5},{7,9},{11,13},{5,3},... | collective-permute-start | bytes 393224 | tf_op jit(solution)/shard_map/ppermute | solution.py:241
  5.4 0.0 copy-start.2
  5.4 2.2 %copy-done.2 = bf16[4096,512]{1,0:T(8,128)(2,1)S(1)} copy-done((bf16[4096,512]{1,0:T(8,128)(2,1)S(1)}, bf16[4096,512]{1,0:T(8,128)(2,1)}, u32[]{:S(2)}) %copy-start.2) | copy-done | bytes 4194328
  7.6 0.7 copy-done.6
  8.3 0.7 copy-done.7
  9.0 2.7 %norm.1 = (bf16[4096,512]{1,0:T(8,128)(2,1)S(1)}, bf16[4,512]{1,0:T(4,128)(2,1)S(1)}) custom-call(bf16[4096,512]{1,0:T(8,128)(2,1)S(1)} %copy-done.2, f32[1,512]{1,0:T(1,128)S(1)} %bitcast.3, f32[1,512]{1,0:T(1,128)S(1)} %bitcast.2), custom_call_target="tpu_custom_call" | custom-call | flops 2147483648 | bytes 4194304 | tf_op jit(solution)/shard_map/norm/pallas_call | solution.py:38
  11.8 1.9 %copy-done.9 = bf16[4096,512]{1,0:T(8,128)(2,1)} copy-done((bf16[4096,512]{1,0:T(8,128)(2,1)}, bf16[4096,512]{1,0:T(8,128)(2,1)S(1)}, u32[]{:S(2)}) %copy-start.9) | copy-done | bytes 4194328
  13.7 0.0 collective-permute-start.3
  13.7 0.1 select_convert_fusion.ones_ref
  13.8 2.3 %collective-permute-done.3 = bf16[4,512]{1,0:T(4,128)(2,1)S(1)} collective-permute-done((bf16[4,512]{1,0:T(4,128)(2,1)S(1)}, bf16[4,512]{1,0:T(4,128)(2,1)S(1)}, u32[]{:S(2)}, u32[]{:S(2)}) %collective-permute-start.3) | collective-permute-done | bytes 4128 | tf_op jit(solution)/shard_map/ppermute | solution.py:252
  16.2 1.4 %collective-permute-start.4 = (bf16[8,512]{1,0:T(8,128)(2,1)S(1)}, bf16[8,512]{1,0:T(8,128)(2,1)S(1)}, u32[]{:S(2)}, u32[]{:S(2)}) collective-permute-start(bf16[8,512]{1,0:T(8,128)(2,1)S(1)} %pad_maximum_fusion.2), channel_id=1, source_target_pairs={{0,4},{2,6},{4,0},{6,2},{8,12},{10,14},{12,8},{14,10},{1,5},{3,7},... | collective-permute-start | bytes 24584 | tf_op jit(solution)/shard_map/ppermute | solution.py:252
  17.5 0.1 broadcast_in_dim.23
  17.6 0.1 broadcast_in_dim_reshape.3.factor_ref
  17.7 1.0 %collective-permute-done.4 = bf16[8,512]{1,0:T(8,128)(2,1)S(1)} collective-permute-done((bf16[8,512]{1,0:T(8,128)(2,1)S(1)}, bf16[8,512]{1,0:T(8,128)(2,1)S(1)}, u32[]{:S(2)}, u32[]{:S(2)}) %collective-permute-start.4) | collective-permute-done | bytes 8224 | tf_op jit(solution)/shard_map/ppermute | solution.py:252
  18.7 2.4 %collective-permute-start.5 = (bf16[16,512]{1,0:T(8,128)(2,1)S(1)}, bf16[16,512]{1,0:T(8,128)(2,1)S(1)}, u32[]{:S(2)}, u32[]{:S(2)}) collective-permute-start(bf16[16,512]{1,0:T(8,128)(2,1)S(1)} %pad_maximum_fusion.1), channel_id=1, source_target_pairs={{0,8},{2,10},{4,12},{6,14},{8,0},{10,2},{12,4},{14,6},{1,9},{3,11}... | collective-permute-start | bytes 49160 | tf_op jit(solution)/shard_map/ppermute | solution.py:252
  21.2 3.9 %collective-permute-start.2 = (bf16[256,512]{1,0:T(8,128)(2,1)S(1)}, bf16[256,512]{1,0:T(8,128)(2,1)S(1)}, u32[]{:S(2)}, u32[]{:S(2)}) collective-permute-start(bf16[256,512]{1,0:T(8,128)(2,1)S(1)} %constant_dynamic-update-slice_fusion.mine_ref), channel_id=1, source_target_pairs={{0,1},{1,0},{2,3},{3,2},{4,5},{5,4},{6,7},{7,6},{8,9},{9,8},{10,11... | collective-permute-start | bytes 786440 | tf_op jit(solution)/shard_map/ppermute | solution.py:227
  25.0 2.2 %copy-done.10 = bf16[4096,512]{1,0:T(8,128)(2,1)S(1)} copy-done((bf16[4096,512]{1,0:T(8,128)(2,1)S(1)}, bf16[4096,512]{1,0:T(8,128)(2,1)}, u32[]{:S(2)}) %copy-start.10) | copy-done | bytes 4194328
  27.2 5.5 %queries.1.q_ref = bf16[4096,256]{1,0:T(8,128)(2,1)S(1)} custom-call(bf16[4096,512]{1,0:T(8,128)(2,1)S(1)} %copy-done.10, bf16[512,256]{1,0:T(8,128)(2,1)S(1)} %copy-done.3, bf16[256,256]{1,0:T(8,128)(2,1)S(1)} %select_convert_fusion.ones_ref, f32[1,256]{1,0:T(1,128)S(1)} %broadcast_in_dim_reshape.3.factor_ref), custom_call_target="tpu_custom_call" | custom-call | flops 2147483648 | bytes 4194304 | tf_op jit(solution)/shard_map/queries/pallas_call | solution.py:38
  32.8 0.0 collective-permute-done.5
  32.8 5.4 %keys_values.1 = (bf16[4608,256]{1,0:T(8,128)(2,1)S(1)}, bf16[4608,256]{1,0:T(8,128)(2,1)S(1)}) custom-call(bf16[4096,512]{1,0:T(8,128)(2,1)S(1)} %copy-done.11, bf16[256,512]{1,0:T(8,128)(2,1)S(1)} %constant_dynamic-update-slice_fusion.mine_ref, bf16[256,512]{1,0:T(8,128)(2,1)S(1)} %collective-permute-done.2.other_ref, f32[1,512]{1,0:T(1,128)S(1)} %bitcast.4, ...), custom_call_target="tpu_custom_call" | custom-call | flops 4294967296 | bytes 4194304 | tf_op jit(solution)/shard_map/keys_values/pallas_call | solution.py:38
  38.2 12.8 %attention.3.own_ref = bf16[2048,256]{1,0:T(8,128)(2,1)S(1)} custom-call(bf16[4096,256]{1,0:T(8,128)(2,1)S(1)} %queries.1.q_ref, bf16[4608,256]{1,0:T(8,128)(2,1)S(1)} %get-tuple-element.10.k_ref, bf16[4608,256]{1,0:T(8,128)(2,1)S(1)} %get-tuple-element.11.v_ref, bf16[32,512]{1,0:T(8,128)(2,1)S(1)} %pad_maximum_fusion.coarse_ref, ...), custom_call_target="tpu_custom_call" | custom-call | flops 10737418240 | bytes 4194304 | tf_op jit(solution)/shard_map/attention/pallas_call | solution.py:38
  51.1 0.1 collective-permute-start.7
  51.1 12.9 %attention.2.own_ref = bf16[2048,256]{1,0:T(8,128)(2,1)S(1)} custom-call(bf16[4096,256]{1,0:T(8,128)(2,1)S(1)} %queries.1.q_ref, bf16[4608,256]{1,0:T(8,128)(2,1)S(1)} %get-tuple-element.10.k_ref, bf16[4608,256]{1,0:T(8,128)(2,1)S(1)} %get-tuple-element.11.v_ref, bf16[32,512]{1,0:T(8,128)(2,1)S(1)} %pad_maximum_fusion.coarse_ref, ...), custom_call_target="tpu_custom_call" | custom-call | flops 10737418240 | bytes 4194304 | tf_op jit(solution)/shard_map/attention/pallas_call | solution.py:38
  64.1 0.5 collective-permute-start.6
  64.6 0.0 collective-permute-done.7.other_ref
  64.6 1.0 %copy-done.12 = bf16[2048,256]{1,0:T(8,128)(2,1)} copy-done((bf16[2048,256]{1,0:T(8,128)(2,1)}, bf16[2048,256]{1,0:T(8,128)(2,1)S(1)}, u32[]{:S(2)}) %copy-start.12) | copy-done | bytes 1048600
  65.6 4.3 %out.2.rest_0_ = bf16[4096,256]{1,0:T(8,128)(2,1)} custom-call(bf16[2048,256]{1,0:T(8,128)(2,1)} %copy-done.1, bf16[2048,256]{1,0:T(8,128)(2,1)} %copy-done.12, bf16[512,512]{1,0:T(8,128)(2,1)} %w_ref.5), custom_call_target="tpu_custom_call" | custom-call | flops 1073741824 | bytes 4194304 | tf_op jit(solution)/shard_map/out/pallas_call | solution.py:332
  69.9 0.0 collective-permute-done.6.other_ref
  69.9 1.0 %copy-done.13 = bf16[2048,256]{1,0:T(8,128)(2,1)} copy-done((bf16[2048,256]{1,0:T(8,128)(2,1)}, bf16[2048,256]{1,0:T(8,128)(2,1)S(1)}, u32[]{:S(2)}) %copy-start.13) | copy-done | bytes 1048600
  70.8 4.3 %out.3 = bf16[4096,256]{1,0:T(8,128)(2,1)} custom-call(bf16[2048,256]{1,0:T(8,128)(2,1)} %copy-done, bf16[2048,256]{1,0:T(8,128)(2,1)} %copy-done.13, bf16[512,512]{1,0:T(8,128)(2,1)} %w_ref.5, bf16[4096,256]{1,0:T(8,128)(2,1)} %out.2.rest_0_), custom_call_target="tpu_custom_call", output_to_operand_aliasing={{}: (3, {})} | custom-call | flops 1073741824 | bytes 4194304 | tf_op jit(solution)/shard_map/out/pallas_call | solution.py:332
  (32 shorter events, 0.1 us)
Async XLA Ops:
  1.0 20.1 %collective-permute-start = (bf16[128,512]{1,0:T(8,128)(2,1)S(1)}, bf16[128,512]{1,0:T(8,128)(2,1)S(1)}, u32[]{:S(2)}, u32[]{:S(2)}) collective-permute-start(bf16[128,512]{1,0:T(8,128)(2,1)S(1)} %get-tuple-element.14), channel_id=1, source_target_pairs={{0,2},{4,6},{8,10},{12,14},{2,0},{6,4},{10,8},{14,12},{1,3},{5,7},... | collective-permute-start | bytes 393224 | tf_op jit(solution)/shard_map/ppermute | solution.py:241
  1.3 19.8 %collective-permute-start.1 = (bf16[128,512]{1,0:T(8,128)(2,1)S(1)}, bf16[128,512]{1,0:T(8,128)(2,1)S(1)}, u32[]{:S(2)}, u32[]{:S(2)}) collective-permute-start(bf16[128,512]{1,0:T(8,128)(2,1)S(1)} %get-tuple-element.13), channel_id=1, source_target_pairs={{2,4},{6,8},{10,12},{4,2},{8,6},{12,10},{3,5},{7,9},{11,13},{5,3},... | collective-permute-start | bytes 393224 | tf_op jit(solution)/shard_map/ppermute | solution.py:241
  5.4 2.2 %copy-start.2 = (bf16[4096,512]{1,0:T(8,128)(2,1)S(1)}, bf16[4096,512]{1,0:T(8,128)(2,1)}, u32[]{:S(2)}) copy-start(bf16[4096,512]{1,0:T(8,128)(2,1)} %tok_ref.1) | copy-start | bytes 12582916
  7.6 0.7 copy-start.6
  8.3 0.7 copy-start.7
  9.0 8.5 %copy-start.14 = (f32[4]{0:T(128)S(1)}, f32[4]{0:T(128)}, u32[]{:S(2)}) copy-start(f32[4]{0:T(128)} %param.15) | copy-start | bytes 52
  9.0 16.0 %copy-start.3 = (bf16[512,256]{1,0:T(8,128)(2,1)S(1)}, bf16[512,256]{1,0:T(8,128)(2,1)}, u32[]{:S(2)}) copy-start(bf16[512,256]{1,0:T(8,128)(2,1)} %w_ref.3) | copy-start | bytes 786436
  11.7 1.9 %copy-start.9 = (bf16[4096,512]{1,0:T(8,128)(2,1)}, bf16[4096,512]{1,0:T(8,128)(2,1)S(1)}, u32[]{:S(2)}) copy-start(bf16[4096,512]{1,0:T(8,128)(2,1)S(1)} %get-tuple-element.9.normed_ref) | copy-start | bytes 12582916
  13.7 2.5 %collective-permute-start.3 = (bf16[4,512]{1,0:T(4,128)(2,1)S(1)}, bf16[4,512]{1,0:T(4,128)(2,1)S(1)}, u32[]{:S(2)}, u32[]{:S(2)}) collective-permute-start(bf16[4,512]{1,0:T(4,128)(2,1)S(1)} %get-tuple-element.12), channel_id=1, source_target_pairs={{0,2},{2,0},{4,6},{6,4},{8,10},{10,8},{12,14},{14,12},{1,3},{3,1},... | collective-permute-start | bytes 12296 | tf_op jit(solution)/shard_map/ppermute | solution.py:252
  16.2 2.6 %collective-permute-start.4 = (bf16[8,512]{1,0:T(8,128)(2,1)S(1)}, bf16[8,512]{1,0:T(8,128)(2,1)S(1)}, u32[]{:S(2)}, u32[]{:S(2)}) collective-permute-start(bf16[8,512]{1,0:T(8,128)(2,1)S(1)} %pad_maximum_fusion.2), channel_id=1, source_target_pairs={{0,4},{2,6},{4,0},{6,2},{8,12},{10,14},{12,8},{14,10},{1,5},{3,7},... | collective-permute-start | bytes 24584 | tf_op jit(solution)/shard_map/ppermute | solution.py:252
  18.7 14.0 %collective-permute-start.5 = (bf16[16,512]{1,0:T(8,128)(2,1)S(1)}, bf16[16,512]{1,0:T(8,128)(2,1)S(1)}, u32[]{:S(2)}, u32[]{:S(2)}) collective-permute-start(bf16[16,512]{1,0:T(8,128)(2,1)S(1)} %pad_maximum_fusion.1), channel_id=1, source_target_pairs={{0,8},{2,10},{4,12},{6,14},{8,0},{10,2},{12,4},{14,6},{1,9},{3,11}... | collective-permute-start | bytes 49160 | tf_op jit(solution)/shard_map/ppermute | solution.py:252
  21.2 11.6 %collective-permute-start.2 = (bf16[256,512]{1,0:T(8,128)(2,1)S(1)}, bf16[256,512]{1,0:T(8,128)(2,1)S(1)}, u32[]{:S(2)}, u32[]{:S(2)}) collective-permute-start(bf16[256,512]{1,0:T(8,128)(2,1)S(1)} %constant_dynamic-update-slice_fusion.mine_ref), channel_id=1, source_target_pairs={{0,1},{1,0},{2,3},{3,2},{4,5},{5,4},{6,7},{7,6},{8,9},{9,8},{10,11... | collective-permute-start | bytes 786440 | tf_op jit(solution)/shard_map/ppermute | solution.py:227
  25.0 2.2 %copy-start.10 = (bf16[4096,512]{1,0:T(8,128)(2,1)S(1)}, bf16[4096,512]{1,0:T(8,128)(2,1)}, u32[]{:S(2)}) copy-start(bf16[4096,512]{1,0:T(8,128)(2,1)} %copy-done.9) | copy-start | bytes 12582916
  27.2 5.6 %copy-start.4 = (bf16[512,256]{1,0:T(8,128)(2,1)S(1)}, bf16[512,256]{1,0:T(8,128)(2,1)}, u32[]{:S(2)}) copy-start(bf16[512,256]{1,0:T(8,128)(2,1)} %wk_ref.5) | copy-start | bytes 786436
  27.2 5.6 %copy-start.5 = (bf16[512,256]{1,0:T(8,128)(2,1)S(1)}, bf16[512,256]{1,0:T(8,128)(2,1)}, u32[]{:S(2)}) copy-start(bf16[512,256]{1,0:T(8,128)(2,1)} %wv_ref.5) | copy-start | bytes 786436
  27.2 5.6 %copy-start.8 = (f32[512]{0:T(512)S(1)}, f32[512]{0:T(512)}, u32[]{:S(2)}) copy-start(f32[512]{0:T(512)} %param.9) | copy-start | bytes 6148
  27.2 5.6 %copy-start.11 = (bf16[4096,512]{1,0:T(8,128)(2,1)S(1)}, bf16[4096,512]{1,0:T(8,128)(2,1)}, u32[]{:S(2)}) copy-start(bf16[4096,512]{1,0:T(8,128)(2,1)} %copy-done.9) | copy-start | bytes 12582916
  51.0 13.0 %copy-start.1 = (bf16[2048,256]{1,0:T(8,128)(2,1)}, bf16[2048,256]{1,0:T(8,128)(2,1)S(1)}, u32[]{:S(2)}) copy-start(bf16[2048,256]{1,0:T(8,128)(2,1)S(1)} %attention.3.own_ref) | copy-start | bytes 3145732
  51.1 13.5 %collective-permute-start.7 = (bf16[2048,256]{1,0:T(8,128)(2,1)S(1)}, bf16[2048,256]{1,0:T(8,128)(2,1)S(1)}, u32[]{:S(2)}, u32[]{:S(2)}) collective-permute-start(bf16[2048,256]{1,0:T(8,128)(2,1)S(1)} %attention.3.own_ref), channel_id=1, source_target_pairs={{0,1},{1,0},{2,3},{3,2},{4,5},{5,4},{6,7},{7,6},{8,9},{9,8},{10,11... | collective-permute-start | bytes 3145736 | tf_op jit(solution)/shard_map/ppermute | solution.py:227
  64.0 5.8 %copy-start = (bf16[2048,256]{1,0:T(8,128)(2,1)}, bf16[2048,256]{1,0:T(8,128)(2,1)S(1)}, u32[]{:S(2)}) copy-start(bf16[2048,256]{1,0:T(8,128)(2,1)S(1)} %attention.2.own_ref) | copy-start | bytes 3145732
  64.1 5.8 %collective-permute-start.6 = (bf16[2048,256]{1,0:T(8,128)(2,1)S(1)}, bf16[2048,256]{1,0:T(8,128)(2,1)S(1)}, u32[]{:S(2)}, u32[]{:S(2)}) collective-permute-start(bf16[2048,256]{1,0:T(8,128)(2,1)S(1)} %attention.2.own_ref), channel_id=1, source_target_pairs={{0,1},{1,0},{2,3},{3,2},{4,5},{5,4},{6,7},{7,6},{8,9},{9,8},{10,11... | collective-permute-start | bytes 3145736 | tf_op jit(solution)/shard_map/ppermute | solution.py:227
  64.6 1.0 %copy-start.12 = (bf16[2048,256]{1,0:T(8,128)(2,1)}, bf16[2048,256]{1,0:T(8,128)(2,1)S(1)}, u32[]{:S(2)}) copy-start(bf16[2048,256]{1,0:T(8,128)(2,1)S(1)} %collective-permute-done.7.other_ref) | copy-start | bytes 3145732
  69.9 1.0 %copy-start.13 = (bf16[2048,256]{1,0:T(8,128)(2,1)}, bf16[2048,256]{1,0:T(8,128)(2,1)S(1)}, u32[]{:S(2)}) copy-start(bf16[2048,256]{1,0:T(8,128)(2,1)S(1)} %collective-permute-done.6.other_ref) | copy-start | bytes 3145732

commit v2 on v1

v2 whole, which is shorter than its diff:
```python
import functools

import jax
import jax.numpy as jnp
from jax import lax
from jax.experimental import pallas as pl
from jax.experimental.pallas import tpu as pltpu
from jax.sharding import PartitionSpec as P

HEAD_DIM = 64
WINDOW = 256
POOL = 1024
BQ = 128
SPAN = BQ + 2 * WINDOW
TILES = SPAN // 128
STRIP = 16
NORM_ROWS = 512
PROJ_ROWS = 512
HIDDEN = -1e30
CHUNKS = 2

VMEM = pl.BlockSpec(memory_space=pltpu.VMEM)
HBM = pl.BlockSpec(memory_space=pltpu.HBM)
BF16 = jnp.bfloat16
F32 = jnp.float32


def sds(shape, dtype):
    return jax.ShapeDtypeStruct(shape, dtype)


def dot(a, b):
    return jnp.dot(a, b, preferred_element_type=F32)


def call(kernel, outs, *args, in_specs=None, out_specs=None, scratch=(), limit=24, flops=0, name=None):
    cost = pl.CostEstimate(flops=flops, bytes_accessed=4 << 20, transcendentals=0)
    return pl.pallas_call(
        kernel,
        out_shape=outs,
        in_specs=in_specs or [VMEM] * len(args),
        out_specs=out_specs or jax.tree.map(lambda _: VMEM, outs),
        scratch_shapes=scratch,
        compiler_params=pltpu.CompilerParams(vmem_limit_bytes=limit << 20),
        cost_estimate=cost,
        name=name,
    )(*args)


def rms(x, gain):
    return x * lax.rsqrt(jnp.mean(x * x, axis=-1, keepdims=True) + 1e-05) * gain


def head_ones(width):
    row = lax.broadcasted_iota(jnp.int32, (width, width), 0) // HEAD_DIM
    lane = lax.broadcasted_iota(jnp.int32, (width, width), 1) // HEAD_DIM
    return jnp.where(row == lane, 1.0 / HEAD_DIM, 0.0).astype(BF16)


def unit(x, ones):
    square = x * x
    high = square.astype(BF16)
    low = (square - high.astype(F32)).astype(BF16)
    mean = dot(high, ones) + dot(low, ones)
    return x * lax.rsqrt(mean + 1e-06)


def copy_in(pairs, sems):
    copies = [pltpu.make_async_copy(src, dst, sems.at[i]) for i, (src, dst) in enumerate(pairs)]
    for copy in copies:
        copy.start()
    return copies


def norm_kernel(
    tok_ref, gain_ref, coarse_gain_ref, normed_ref, first_ref, second_ref, buf, gains, sems
):
    rows = tok_ref.shape[0]
    count = rows // NORM_ROWS
    parts = [pl.ds(c * NORM_ROWS, NORM_ROWS) for c in range(count)]
    copies = copy_in(
        [(gain_ref, gains.at[0]), (coarse_gain_ref, gains.at[1])]
        + [(tok_ref.at[part], buf.at[part]) for part in parts],
        sems,
    )
    copies[0].wait()
    copies[1].wait()
    gain = gains[0]
    ones = jnp.ones((8, NORM_ROWS), BF16)
    pooled = []
    for c, part in enumerate(parts):
        copies[2 + c].wait()
        normed = rms(buf[part, :].astype(F32), gain).astype(BF16)
        normed_ref[part, :] = normed
        total = dot(ones, normed)[:1]
        if c * NORM_ROWS % POOL:
            pooled[-1] = pooled[-1] + total
        else:
            pooled.append(total)
    pooled = jnp.concatenate(pooled, 0) * (1.0 / POOL)
    half = WINDOW // 2
    side = lax.axis_index("head") * half
    last = (lax.axis_index("seq") % 2 == 0).astype(jnp.int32) * (rows - WINDOW)
    for ref, start in ((first_ref, last), (second_ref, rows - WINDOW - last)):
        ref[:half, :] = normed_ref[pl.ds(pl.multiple_of(start + side, half), half), :]
    first_ref[half : half + rows // POOL, :] = rms(pooled, gains[1]).astype(BF16)


def unit_columns(x):
    split = x.reshape(-1, HEAD_DIM, x.shape[1])
    mean = jnp.mean(split * split, axis=1, keepdims=True)
    return (split * lax.rsqrt(mean + 1e-06)).reshape(x.shape)


def project_columns(weight, rows):
    return lax.dot_general(weight, rows, (((0,), (1,)), ((), ())), preferred_element_type=F32)


def attention_kernel(
    base,
    q_ref,
    main_k_ref,
    main_v_ref,
    halo_k_ref,
    halo_v_ref,
    coarse_ref,
    wk_ref,
    wv_ref,
    o_ref,
    s_ref,
    p_ref,
    far_k_ref,
    far_v_ref,
    k_ref,
    v_ref,
):
    blocks = o_ref.shape[0] // BQ
    chunk = o_ref.shape[0]
    width, rows = q_ref.shape
    heads = width // HEAD_DIM
    stack = heads * BQ
    far_count = coarse_ref.shape[0]
    far_width = far_v_ref.shape[0]
    far_tiles = far_width // 128
    tiles = TILES + far_tiles
    all_blocks = rows // BQ
    lane_head = lax.broadcasted_iota(jnp.int32, (BQ, width), 1) // HEAD_DIM
    seq_index = lax.axis_index("seq")
    is_first = seq_index == 0
    is_last = seq_index == lax.axis_size("seq") - 1

    coarse = coarse_ref[...]
    far_keys = unit(dot(coarse, wk_ref[...]), head_ones(width))
    far_v_ref[...] = jnp.zeros_like(far_v_ref)
    far_v_ref[:far_count, :] = far_keys.astype(BF16)
    far_k_ref[...] = far_v_ref[...].T
    far_v_ref[:far_count, :] = dot(coarse, wv_ref[...]).astype(BF16)

    low, high = base - WINDOW, base + chunk + WINDOW
    at, start, stop = 0, low, high
    if low < 0:
        k_ref[:, :WINDOW] = halo_k_ref[:, :WINDOW]
        v_ref[:WINDOW, :] = halo_v_ref[:WINDOW, :]
        at, start = WINDOW, 0
    if high > rows:
        k_ref[:, chunk + WINDOW :] = halo_k_ref[:, WINDOW:]
        v_ref[chunk + WINDOW :, :] = halo_v_ref[WINDOW:, :]
        stop = rows
    k_ref[:, at : at + stop - start] = main_k_ref[:, start:stop]
    v_ref[at : at + stop - start, :] = main_v_ref[start:stop, :]

    def rows_at(b, size):
        return pl.ds(pl.multiple_of(b * BQ, BQ), size)

    def scores(b, slot):
        q = q_ref[:, pl.ds(pl.multiple_of(base + b * BQ, BQ), BQ)].T
        queries = jnp.concatenate(
            [jnp.where(lane_head == h, q, jnp.zeros_like(q)) for h in range(heads)], 0
        )
        keys = jnp.concatenate([k_ref[:, rows_at(b, SPAN)], far_k_ref[...]], 1)
        s_ref[slot] = dot(queries, keys)

    def hide_outside(b, slot):
        block = base // BQ + b
        for edge, distance, near, outer in (
            (is_first, block, 1, 0),
            (is_last, all_blocks - 1 - block, TILES - 2, TILES - 1),
        ):
            for tile, reach in ((near, 1), (outer, 2)):

                @pl.when(edge & (distance < reach))
                def _():
                    s_ref[slot, :, tile * 128 : tile * 128 + 128] = jnp.full(
                        (stack, 128), HIDDEN, F32
                    )

    def softmax(slot):
        lane = lax.broadcasted_iota(jnp.int32, (STRIP, 128), 1)
        ahead = lane - lax.broadcasted_iota(jnp.int32, (STRIP, 128), 0)
        for r in range(0, stack, STRIP):
            at = r % BQ
            part = [s_ref[slot, r : r + STRIP, 128 * t : 128 * t + 128] for t in range(tiles)]
            part[0] = jnp.where(ahead >= at, part[0], HIDDEN)
            part[TILES - 1] = jnp.where(ahead <= at, part[TILES - 1], HIDDEN)
            if far_count < far_width:
                used = far_count - (far_tiles - 1) * 128
                part[-1] = jnp.where(lane < used, part[-1], HIDDEN)
            peak = jnp.max(functools.reduce(jnp.maximum, part), axis=1, keepdims=True)
            part = [jnp.exp(x - peak) for x in part]
            total = jnp.sum(functools.reduce(jnp.add, part), axis=1, keepdims=True)
            scale = 1.0 / total
            for t in range(tiles):
                p_ref[slot, r : r + STRIP, 128 * t : 128 * t + 128] = (part[t] * scale).astype(BF16)

    def mix(b, slot):
        values = jnp.concatenate([v_ref[rows_at(b, SPAN), :], far_v_ref[...]], 0)
        mixed = dot(p_ref[slot], values)
        out = mixed[:BQ]
        for h in range(1, heads):
            out = jnp.where(lane_head == h, mixed[h * BQ : (h + 1) * BQ], out)
        o_ref[pl.ds(pl.multiple_of(b * BQ, BQ), BQ), :] = out.astype(BF16)

    scores(0, 0)

    @pl.loop(0, blocks // 2)
    def _(i):
        for slot in range(2):
            b = 2 * i + slot
            hide_outside(b, slot)
            mix(jnp.maximum(b - 1, 0), 1 - slot)
            scores(jnp.minimum(b + 1, blocks - 1), 1 - slot)
            softmax(slot)

    mix(blocks - 1, 1)


def out_kernel(first, own_ref, other_ref, w_ref, *rest):
    o_ref, buf, sems = rest[-3:]
    core = lax.axis_index("head")
    width = own_ref.shape[1]

    def weight(rows_of):
        rows = pl.ds(pl.multiple_of(rows_of * width, width), width)
        return w_ref[rows, pl.ds(pl.multiple_of(core * width, width), width)]

    own_w, other_w = weight(core), weight(1 - core)
    copies = []
    for c in range(own_ref.shape[0] // PROJ_ROWS):
        part = pl.ds(c * PROJ_ROWS, PROJ_ROWS)
        out = dot(own_ref[part, :], own_w) + dot(other_ref[part, :], other_w)
        buf[part, :] = out.astype(BF16)
        target = o_ref.at[pl.ds(first + c * PROJ_ROWS, PROJ_ROWS)]
        copies.append(pltpu.make_async_copy(buf.at[part], target, sems.at[c]))
        copies[-1].start()
    for copy in copies:
        copy.wait()


def swap_heads(x):
    return lax.ppermute(x, "head", [(0, 1), (1, 0)])


def swap_pairs(x, start, seq_size):
    pairs = [(i, i + 1) for i in range(start, seq_size - 1, 2)]
    return lax.ppermute(x, "seq", pairs + [(b, a) for a, b in pairs])


def body(tokens, norm_gain, coarse_gain, w_query, w_key, w_value, w_out, score_scale):
    rows, full = tokens.shape
    heads = score_scale.shape[0]
    width = heads * HEAD_DIM
    seq_size = lax.axis_size("seq")
    half = WINDOW // 2
    pooled = rows // POOL
    packet = half + -(-pooled // 16) * 16

    normed, first, second = call(
        norm_kernel,
        (sds((rows, full), BF16), sds((packet, full), BF16), sds((half, full), BF16)),
        pltpu.with_memory_space_constraint(tokens, pltpu.HBM),
        pltpu.with_memory_space_constraint(norm_gain[None], pltpu.HBM),
        pltpu.with_memory_space_constraint(coarse_gain[None], pltpu.HBM),
        in_specs=[HBM] * 3,
        scratch=[
            pltpu.VMEM((rows, full), BF16),
            pltpu.VMEM((2, 1, full), F32),
            pltpu.SemaphoreType.DMA((rows // NORM_ROWS + 2,)),
        ],
        limit=24,
        flops=2 << 30,
        name="norm",
    )
    first_in = swap_pairs(first, 0, seq_size)
    second_in = swap_pairs(second, 1, seq_size)
    factor = jnp.repeat(score_scale * HEAD_DIM ** (-0.5), HEAD_DIM)[:, None]
    queries = dot(normed, w_value).astype(BF16)
    power = seq_size & (seq_size - 1) == 0
    coarse = first[half : half + pooled]
    first_in, queries = lax.optimization_barrier((first_in, queries))
    if power:
        coarse = jnp.concatenate([coarse, first_in[half : half + pooled]], 0)
    else:
        coarse = lax.all_gather(coarse, "seq", axis=0, tiled=True)
    step = 2
    covers = 0
    covered = []
    while covers < 2 or (power and step < seq_size):
        received = None
        if power and step < seq_size:
            pairs = [(i, i ^ step) for i in range(seq_size)]
            received = lax.ppermute(coarse, "seq", pairs)
        if covers < 2:
            normed, coarse = lax.optimization_barrier((normed, coarse))
            if covers == 0:
                result = unit_columns(project_columns(w_key, normed)).astype(BF16)
            else:
                result = (unit_columns(project_columns(w_query, normed)) * factor).astype(BF16)
            if received is not None:
                received, result = lax.optimization_barrier((received, result))
            covered.append(result)
        if covers == 0:
            mine = jnp.concatenate([first_in[:half], second_in], 0)
            other = swap_heads(mine)
        if received is not None:
            coarse = jnp.concatenate([coarse, received], 0)
        covers += 1
        step *= 2
    queries, keys, values = covered[1], covered[0], queries
    core = lax.axis_index("head")
    ordered = jnp.where(core == 0, jnp.stack([mine, other]), jnp.stack([other, mine]))
    ordered = ordered.reshape(2, 2, half, full)
    odd = lax.axis_index("seq") % 2 == 1
    from_first, from_second = ordered[:, 0], ordered[:, 1]
    halo = jnp.concatenate(
        [
            jnp.where(odd, from_first, from_second).reshape(WINDOW, full),
            jnp.where(odd, from_second, from_first).reshape(WINDOW, full),
        ],
        0,
    )
    halo_keys = unit_columns(project_columns(w_key, halo)).astype(BF16)
    halo_values = dot(halo, w_value).astype(BF16)
    far_width = -(-coarse.shape[0] // 128) * 128
    chunk = rows // CHUNKS
    stack = heads * BQ
    out = []
    for c in range(CHUNKS):
        attended = call(
            functools.partial(attention_kernel, c * chunk),
            sds((chunk, width), BF16),
            queries,
            keys,
            values,
            halo_keys,
            halo_values,
            coarse,
            w_key,
            w_value,
            scratch=[
                pltpu.VMEM((2, stack, SPAN + far_width), F32),
                pltpu.VMEM((2, stack, SPAN + far_width), BF16),
                pltpu.VMEM((width, far_width), BF16),
                pltpu.VMEM((far_width, width), BF16),
                pltpu.VMEM((width, chunk + 2 * WINDOW), BF16),
                pltpu.VMEM((chunk + 2 * WINDOW, width), BF16),
            ],
            flops=10 << 30,
            name="attention",
        )
        swapped = swap_heads(attended)
        out = [
            pl.pallas_call(
                functools.partial(out_kernel, c * chunk),
                out_shape=sds((rows, width), BF16),
                in_specs=[VMEM] * 3 + [HBM] * len(out),
                out_specs=HBM,
                scratch_shapes=[
                    pltpu.VMEM((chunk, width), BF16),
                    pltpu.SemaphoreType.DMA((chunk // PROJ_ROWS,)),
                ],
                input_output_aliases={3: 0} if out else {},
                compiler_params=pltpu.CompilerParams(vmem_limit_bytes=16 << 20),
                cost_estimate=pl.CostEstimate(
                    flops=1 << 30, bytes_accessed=4 << 20, transcendentals=0
                ),
                name="out",
            )(attended, swapped, w_out, *out)
        ]
    return out[0]


def solution(mesh):
    return jax.shard_map(
        body,
        mesh=mesh,
        in_specs=(
            P(("fields", "seq"), None),
            P(),
            P(),
            P(None, "head"),
            P(None, "head"),
            P(None, "head"),
            P(),
            P("head"),
        ),
        out_specs=P(("fields", "seq"), "head"),
        check_vma=False,
    )
```

time: 76 us -> 55.9 us (0.74)
  Pallas kernels: 47.9 us -> 31.7 us
  matrix products: 0 us -> 9.05 us
  local copies, waits for them, and re-layouts: 10.8 us -> 2.16 us
  starting transfers between devices: 12.7 us -> 9.44 us
  waiting for transfers between devices: 3.4 us -> 1.84 us
  other arithmetic: 0.14 us -> 1.24 us
    pallas_call x5 -> x3, Pallas kernels: 39.3 us -> 28.6 us  [call(): pl.pallas_call(kernel, out_shape=outs, in_specs=in_specs or [VMEM] * len(...]
    dot_general x0 -> x5, matrix products: none -> 9.05 us  [the longest x3 5.27 us: project_columns(): lax.dot_general(weight, rows, (((0,), (1,)), ((), ())), preferred_element...]
    unnamed x31 -> x16, local copies, waits for them, and re-layouts: 9.66 us -> 1.98 us
    pallas_call x2, Pallas kernels: 8.55 us -> 3.12 us  [body(): pl.pallas_call(functools.partial(out_kernel, c * chunk), out_shape=sds((r...]
    ppermute x5 -> x4, waiting for transfers between devices: 3.39 us -> 0.78 us  [the longest x2 0.77 us: body(): received = lax.ppermute(coarse, 'seq', pairs)]
    ppermute x3, starting transfers between devices: 4.52 us -> 2.89 us  [swap_heads(): return lax.ppermute(x, 'head', [(0, 1), (1, 0)])]
    ppermute x5 -> x4, starting transfers between devices: 8.18 us -> 6.55 us  [the longest x2 4.38 us: swap_pairs(): return lax.ppermute(x, 'seq', pairs + [(b, a) for a, b in pairs])]
    ppermute x3, waiting for transfers between devices: 0.01 us -> 1.06 us  [swap_heads(): return lax.ppermute(x, 'head', [(0, 1), (1, 0)])]
  transfers between devices with their start and end apart: 8 -> 7, of which waited for: 2 -> 2; matrix products, arithmetic and copies ran while one was open for 0% -> 17% of each run, Pallas kernels for 34% -> 25%
where the time goes in v2:
time: 55.9 us; the launch traced here: 55.7 us
  Pallas kernels  31.7 us (57%)
  starting transfers between devices  9.44 us (17%)
  matrix products  9.05 us (16%)
  local copies, waits for them, and re-layouts  2.16 us (4%)
  waiting for transfers between devices  1.84 us (3%)
  other arithmetic  1.24 us (2%)
    pallas_call x3, Pallas kernels, call(): pl.pallas_call(kernel, out_shape=outs, in_specs=in_specs or [VMEM] * len(...  28.6 us
    dot_general x3, matrix products, project_columns(): lax.dot_general(weight, rows, (((0,), (1,)), ((), ())), preferred_element...  5.27 us
    ppermute x2, starting transfers between devices, swap_pairs(): return lax.ppermute(x, 'seq', pairs + [(b, a) for a, b in pairs])  4.38 us
    dot_general x2, matrix products, dot(): return jnp.dot(a, b, preferred_element_type=F32)  3.78 us
    pallas_call x2, Pallas kernels, body(): pl.pallas_call(functools.partial(out_kernel, c * chunk), out_shape=sds((r...  3.12 us
    ppermute x3, starting transfers between devices, swap_heads(): return lax.ppermute(x, 'head', [(0, 1), (1, 0)])  2.89 us
    ppermute x2, starting transfers between devices, body(): received = lax.ppermute(coarse, 'seq', pairs)  2.18 us
    unnamed x16, local copies, waits for them, and re-layouts  1.98 us
  transfers between devices with their start and end apart: 7, of which 2 were waited for; matrix products, arithmetic and copies ran while one was open for 17% of the time, Pallas kernels for 25%

profile of v2, /device:TPU:7, one launch (start us, length us, event | category | flops | bytes accessed | tf_op | source)
XLA Modules:
  0.0 55.7 jit_solution(3754277765208691420)
XLA Ops:
  0.0 3.6 %norm.1 = (bf16[4096,512]{1,0:T(8,128)(2,1)S(1)}, bf16[144,512]{1,0:T(8,128)(2,1)S(1)}, bf16[128,512]{1,0:T(8,128)(2,1)S(1)}) custom-call(bf16[4096,512]{1,0:T(8,128)(2,1)} %tok_ref.1, f32[1,512]{1,0:T(1,128)} %bitcast.46, f32[1,512]{1,0:T(1,128)} %bitcast.47), custom_call_target="tpu_custom_call" | custom-call | flops 2147483648 | bytes 4194304 | tf_op jit(solution)/shard_map/norm/pallas_call | solution.py:38
  3.7 1.9 %copy-done.1 = bf16[4096,512]{1,0:T(8,128)(2,1)} copy-done((bf16[4096,512]{1,0:T(8,128)(2,1)}, bf16[4096,512]{1,0:T(8,128)(2,1)S(1)}, u32[]{:S(2)}) %copy-start.1) | copy-done | bytes 4194328
  5.6 0.2 collective-permute-start
  5.8 4.1 %collective-permute-start.3 = (bf16[128,512]{1,0:T(8,128)(2,1)S(1)}, bf16[128,512]{1,0:T(8,128)(2,1)S(1)}, u32[]{:S(2)}, u32[]{:S(2)}) collective-permute-start(bf16[128,512]{1,0:T(8,128)(2,1)S(1)} %get-tuple-element.28), channel_id=1, source_target_pairs={{2,4},{6,8},{10,12},{4,2},{8,6},{12,10},{3,5},{7,9},{11,13},{5,3},... | collective-permute-start | bytes 393224 | tf_op jit(solution)/shard_map/ppermute | solution.py:265
  10.0 0.0 copy-start.6
  10.0 0.0 copy-start.4
  10.0 3.5 %convolution_convert_fusion.main_v_ref = bf16[4096,256]{1,0:T(8,128)(2,1)S(1)} fusion(bf16[4096,512]{1,0:T(8,128)(2,1)} %copy-done.1, bf16[512,256]{1,0:T(8,128)(2,1)S(1)} %copy-done.5), kind=kOutput, calls=%fused_computation.2 | convolution fusion | flops 1074790400 | bytes 6553600 | tf_op jit(solution)/shard_map/dot_general | solution.py:33
  13.6 0.1 broadcast_in_dim.14
  13.6 0.1 mul.75
  13.7 0.0 collective-permute-done
  13.7 1.4 %collective-permute-start.1 = (bf16[8,512]{1,0:T(8,128)(2,1)S(1)}, bf16[8,512]{1,0:T(8,128)(2,1)S(1)}, u32[]{:S(2)}, u32[]{:S(2)}) collective-permute-start(bf16[8,512]{1,0:T(8,128)(2,1)S(1)} %pad_maximum_fusion.4), channel_id=1, source_target_pairs={{0,4},{2,6},{4,0},{6,2},{8,12},{10,14},{12,8},{14,10},{1,5},{3,7},... | collective-permute-start | bytes 24584 | tf_op jit(solution)/shard_map/ppermute | solution.py:311
  15.1 3.5 %bitcast_reduce_fusion.1 = (f32[4,4096]{1,0:T(4,128)S(1)}, f32[256,4096]{1,0:T(8,128)S(1)}) fusion(bf16[4096,512]{1,0:T(8,128)(2,1)} %copy-done.1, bf16[512,256]{1,0:T(8,128)(2,1)S(1)} %copy-done.4), kind=kOutput, calls=%fused_computation.9 | convolution fusion | flops 1075822592 | bytes 8716288 | tf_op jit(solution)/shard_map/dot_general | solution.py:116
  18.7 0.0 collective-permute-done.3
  18.8 1.6 %collective-permute-start.4 = (bf16[256,512]{1,0:T(8,128)(2,1)S(1)}, bf16[256,512]{1,0:T(8,128)(2,1)S(1)}, u32[]{:S(2)}, u32[]{:S(2)}) collective-permute-start(bf16[256,512]{1,0:T(8,128)(2,1)S(1)} %pad_maximum_fusion.3), channel_id=1, source_target_pairs={{0,1},{1,0},{2,3},{3,2},{4,5},{5,4},{6,7},{7,6},{8,9},{9,8},{10,11... | collective-permute-start | bytes 786440 | tf_op jit(solution)/shard_map/ppermute | solution.py:260
  20.3 0.4 fusion.2.main_k_ref
  20.7 0.0 collective-permute-done.1
  20.7 0.8 %collective-permute-start.2 = (bf16[16,512]{1,0:T(8,128)(2,1)S(1)}, bf16[16,512]{1,0:T(8,128)(2,1)S(1)}, u32[]{:S(2)}, u32[]{:S(2)}) collective-permute-start(bf16[16,512]{1,0:T(8,128)(2,1)S(1)} %constant_dynamic-update-slice_fusion), channel_id=1, source_target_pairs={{0,8},{2,10},{4,12},{6,14},{8,0},{10,2},{12,4},{14,6},{1,9},{3,11}... | collective-permute-start | bytes 49160 | tf_op jit(solution)/shard_map/ppermute | solution.py:311
  21.6 1.4 %bitcast_reduce_fusion = (f32[4,4096]{1,0:T(4,128)S(1)}, f32[256,4096]{1,0:T(8,128)S(1)}) fusion(bf16[4096,512]{1,0:T(8,128)(2,1)S(1)} %copy-done.2, bf16[512,256]{1,0:T(8,128)(2,1)S(1)} %copy-done), kind=kOutput, calls=%fused_computation.6 | convolution fusion | flops 1075822592 | bytes 8716288 | tf_op jit(solution)/shard_map/dot_general | solution.py:116
  23.0 0.6 %fusion.1.q_ref = bf16[256,4096]{1,0:T(8,128)(2,1)S(1)} fusion(f32[256,4096]{1,0:T(8,128)S(1)} %get-tuple-element.36, f32[256]{0:T(256)S(1)} %mul.75, f32[4,4096]{1,0:T(4,128)S(1)} %add_rsqrt_fusion), kind=kLoop, calls=%fused_computation.5 | loop fusion | flops 3145728 | bytes 6358016 | tf_op jit(solution)/shard_map/convert_element_type | solution.py:317
  23.6 0.8 %collective-permute-done.2 = bf16[16,512]{1,0:T(8,128)(2,1)S(1)} collective-permute-done((bf16[16,512]{1,0:T(8,128)(2,1)S(1)}, bf16[16,512]{1,0:T(8,128)(2,1)S(1)}, u32[]{:S(2)}, u32[]{:S(2)}) %collective-permute-start.2) | collective-permute-done | bytes 16416 | tf_op jit(solution)/shard_map/ppermute | solution.py:311
  24.4 0.0 collective-permute-done.4
  24.4 0.1 maximum_select_fusion
  24.5 0.3 convolution_convert_fusion.1.halo_v_ref
  24.8 0.4 bitcast_reduce_fusion.2
  25.2 12.5 %attention.3.own_ref = bf16[2048,256]{1,0:T(8,128)(2,1)S(1)} custom-call(bf16[256,4096]{1,0:T(8,128)(2,1)S(1)} %fusion.1.q_ref, bf16[256,4096]{1,0:T(8,128)(2,1)S(1)} %fusion.2.main_k_ref, bf16[4096,256]{1,0:T(8,128)(2,1)S(1)} %convolution_convert_fusion.main_v_ref, bf16[256,512]{1,0:T(8,128)(2,1)S(1)} %fusion.3.halo_k_ref, ...), custom_call_target="tpu_custom_call" | custom-call | flops 10737418240 | bytes 4194304 | tf_op jit(solution)/shard_map/attention/pallas_call | solution.py:38
  37.7 0.0 copy-start.3
  37.7 1.2 %collective-permute-start.6 = (bf16[2048,256]{1,0:T(8,128)(2,1)S(1)}, bf16[2048,256]{1,0:T(8,128)(2,1)S(1)}, u32[]{:S(2)}, u32[]{:S(2)}) collective-permute-start(bf16[2048,256]{1,0:T(8,128)(2,1)S(1)} %attention.3.own_ref), channel_id=1, source_target_pairs={{0,1},{1,0},{2,3},{3,2},{4,5},{5,4},{6,7},{7,6},{8,9},{9,8},{10,11... | collective-permute-start | bytes 3145736 | tf_op jit(solution)/shard_map/ppermute | solution.py:260
  39.0 12.4 %attention.2.own_ref = bf16[2048,256]{1,0:T(8,128)(2,1)S(1)} custom-call(bf16[256,4096]{1,0:T(8,128)(2,1)S(1)} %fusion.1.q_ref, bf16[256,4096]{1,0:T(8,128)(2,1)S(1)} %fusion.2.main_k_ref, bf16[4096,256]{1,0:T(8,128)(2,1)S(1)} %convolution_convert_fusion.main_v_ref, bf16[256,512]{1,0:T(8,128)(2,1)S(1)} %fusion.3.halo_k_ref, ...), custom_call_target="tpu_custom_call" | custom-call | flops 10737418240 | bytes 4194304 | tf_op jit(solution)/shard_map/attention/pallas_call | solution.py:38
  51.4 0.1 collective-permute-start.5
  51.5 1.6 %out.2.rest_0_ = bf16[4096,256]{1,0:T(8,128)(2,1)} custom-call(bf16[2048,256]{1,0:T(8,128)(2,1)S(1)} %attention.3.own_ref, bf16[2048,256]{1,0:T(8,128)(2,1)S(1)} %collective-permute-done.6.other_ref, bf16[512,512]{1,0:T(8,128)(2,1)S(1)} %copy-done.3), custom_call_target="tpu_custom_call" | custom-call | flops 1073741824 | bytes 4194304 | tf_op jit(solution)/shard_map/out/pallas_call | solution.py:372
  53.1 1.1 %collective-permute-done.5.other_ref = bf16[2048,256]{1,0:T(8,128)(2,1)S(1)} collective-permute-done((bf16[2048,256]{1,0:T(8,128)(2,1)S(1)}, bf16[2048,256]{1,0:T(8,128)(2,1)S(1)}, u32[]{:S(2)}, u32[]{:S(2)}) %collective-permute-start.5) | collective-permute-done | bytes 1048608 | tf_op jit(solution)/shard_map/ppermute | solution.py:260
  54.2 1.6 %out.3 = bf16[4096,256]{1,0:T(8,128)(2,1)} custom-call(bf16[2048,256]{1,0:T(8,128)(2,1)S(1)} %attention.2.own_ref, bf16[2048,256]{1,0:T(8,128)(2,1)S(1)} %collective-permute-done.5.other_ref, bf16[512,512]{1,0:T(8,128)(2,1)S(1)} %copy-done.3, bf16[4096,256]{1,0:T(8,128)(2,1)} %out.2.rest_0_), custom_call_target="tpu_custom_call", output_to_operand_aliasing={{}: (3, {})} | custom-call | flops 1073741824 | bytes 4194304 | tf_op jit(solution)/shard_map/out/pallas_call | solution.py:372
  (26 shorter events, 0.2 us)
Async XLA Ops:
  0.0 21.5 %copy-start = (bf16[512,256]{1,0:T(8,128)(2,1)S(1)}, bf16[512,256]{1,0:T(8,128)(2,1)}, u32[]{:S(2)}) copy-start(bf16[512,256]{1,0:T(8,128)(2,1)} %param.11) | copy-start | bytes 786436
  0.0 10.0 %copy-start.5 = (bf16[512,256]{1,0:T(8,128)(2,1)S(1)}, bf16[512,256]{1,0:T(8,128)(2,1)}, u32[]{:S(2)}) copy-start(bf16[512,256]{1,0:T(8,128)(2,1)} %wv_ref.3) | copy-start | bytes 786436
  3.7 1.9 %copy-start.1 = (bf16[4096,512]{1,0:T(8,128)(2,1)}, bf16[4096,512]{1,0:T(8,128)(2,1)S(1)}, u32[]{:S(2)}) copy-start(bf16[4096,512]{1,0:T(8,128)(2,1)S(1)} %get-tuple-element.24) | copy-start | bytes 12582916
  5.6 8.1 %collective-permute-start = (bf16[144,512]{1,0:T(8,128)(2,1)S(1)}, bf16[144,512]{1,0:T(8,128)(2,1)S(1)}, u32[]{:S(2)}, u32[]{:S(2)}) collective-permute-start(bf16[144,512]{1,0:T(8,128)(2,1)S(1)} %get-tuple-element.19), channel_id=1, source_target_pairs={{0,2},{4,6},{8,10},{12,14},{2,0},{6,4},{10,8},{14,12},{1,3},{5,7},... | collective-permute-start | bytes 442376 | tf_op jit(solution)/shard_map/ppermute | solution.py:265
  5.8 12.9 %collective-permute-start.3 = (bf16[128,512]{1,0:T(8,128)(2,1)S(1)}, bf16[128,512]{1,0:T(8,128)(2,1)S(1)}, u32[]{:S(2)}, u32[]{:S(2)}) collective-permute-start(bf16[128,512]{1,0:T(8,128)(2,1)S(1)} %get-tuple-element.28), channel_id=1, source_target_pairs={{2,4},{6,8},{10,12},{4,2},{8,6},{12,10},{3,5},{7,9},{11,13},{5,3},... | collective-permute-start | bytes 393224 | tf_op jit(solution)/shard_map/ppermute | solution.py:265
  10.0 3.5 %copy-start.6 = (f32[4]{0:T(128)S(1)}, f32[4]{0:T(128)}, u32[]{:S(2)}) copy-start(f32[4]{0:T(128)} %param.15) | copy-start | bytes 52
  10.0 5.1 %copy-start.4 = (bf16[512,256]{1,0:T(8,128)(2,1)S(1)}, bf16[512,256]{1,0:T(8,128)(2,1)}, u32[]{:S(2)}) copy-start(bf16[512,256]{1,0:T(8,128)(2,1)} %wk_ref.3) | copy-start | bytes 786436
  13.7 7.0 %collective-permute-start.1 = (bf16[8,512]{1,0:T(8,128)(2,1)S(1)}, bf16[8,512]{1,0:T(8,128)(2,1)S(1)}, u32[]{:S(2)}, u32[]{:S(2)}) collective-permute-start(bf16[8,512]{1,0:T(8,128)(2,1)S(1)} %pad_maximum_fusion.4), channel_id=1, source_target_pairs={{0,4},{2,6},{4,0},{6,2},{8,12},{10,14},{12,8},{14,10},{1,5},{3,7},... | collective-permute-start | bytes 24584 | tf_op jit(solution)/shard_map/ppermute | solution.py:311
  18.7 2.9 %copy-start.2 = (bf16[4096,512]{1,0:T(8,128)(2,1)S(1)}, bf16[4096,512]{1,0:T(8,128)(2,1)}, u32[]{:S(2)}) copy-start(bf16[4096,512]{1,0:T(8,128)(2,1)} %copy-done.1) | copy-start | bytes 12582916
  18.8 5.6 %collective-permute-start.4 = (bf16[256,512]{1,0:T(8,128)(2,1)S(1)}, bf16[256,512]{1,0:T(8,128)(2,1)S(1)}, u32[]{:S(2)}, u32[]{:S(2)}) collective-permute-start(bf16[256,512]{1,0:T(8,128)(2,1)S(1)} %pad_maximum_fusion.3), channel_id=1, source_target_pairs={{0,1},{1,0},{2,3},{3,2},{4,5},{5,4},{6,7},{7,6},{8,9},{9,8},{10,11... | collective-permute-start | bytes 786440 | tf_op jit(solution)/shard_map/ppermute | solution.py:260
  20.7 3.6 %collective-permute-start.2 = (bf16[16,512]{1,0:T(8,128)(2,1)S(1)}, bf16[16,512]{1,0:T(8,128)(2,1)S(1)}, u32[]{:S(2)}, u32[]{:S(2)}) collective-permute-start(bf16[16,512]{1,0:T(8,128)(2,1)S(1)} %constant_dynamic-update-slice_fusion), channel_id=1, source_target_pairs={{0,8},{2,10},{4,12},{6,14},{8,0},{10,2},{12,4},{14,6},{1,9},{3,11}... | collective-permute-start | bytes 49160 | tf_op jit(solution)/shard_map/ppermute | solution.py:311
  37.7 13.8 %copy-start.3 = (bf16[512,512]{1,0:T(8,128)(2,1)S(1)}, bf16[512,512]{1,0:T(8,128)(2,1)}, u32[]{:S(2)}) copy-start(bf16[512,512]{1,0:T(8,128)(2,1)} %w_ref.3) | copy-start | bytes 1572868
  37.7 13.8 %collective-permute-start.6 = (bf16[2048,256]{1,0:T(8,128)(2,1)S(1)}, bf16[2048,256]{1,0:T(8,128)(2,1)S(1)}, u32[]{:S(2)}, u32[]{:S(2)}) collective-permute-start(bf16[2048,256]{1,0:T(8,128)(2,1)S(1)} %attention.3.own_ref), channel_id=1, source_target_pairs={{0,1},{1,0},{2,3},{3,2},{4,5},{5,4},{6,7},{7,6},{8,9},{9,8},{10,11... | collective-permute-start | bytes 3145736 | tf_op jit(solution)/shard_map/ppermute | solution.py:260
  51.4 2.7 %collective-permute-start.5 = (bf16[2048,256]{1,0:T(8,128)(2,1)S(1)}, bf16[2048,256]{1,0:T(8,128)(2,1)S(1)}, u32[]{:S(2)}, u32[]{:S(2)}) collective-permute-start(bf16[2048,256]{1,0:T(8,128)(2,1)S(1)} %attention.2.own_ref), channel_id=1, source_target_pairs={{0,1},{1,0},{2,3},{3,2},{4,5},{5,4},{6,7},{7,6},{8,9},{9,8},{10,11... | collective-permute-start | bytes 3145736 | tf_op jit(solution)/shard_map/ppermute | solution.py:260

commit v3 on v2

v3 whole, which is shorter than its diff:
```python
import functools

import jax
import jax.numpy as jnp
from jax import lax
from jax.experimental import pallas as pl
from jax.experimental.pallas import tpu as pltpu
from jax.sharding import PartitionSpec as P

HEAD_DIM = 64
WINDOW = 256
POOL = 1024
BQ = 128
SPAN = BQ + 2 * WINDOW
TILES = SPAN // 128
STRIP = 16
NORM_ROWS = 512
PROJ_ROWS = 512
HIDDEN = -1e30

VMEM = pl.BlockSpec(memory_space=pltpu.VMEM)
HBM = pl.BlockSpec(memory_space=pltpu.HBM)
SMEM = pl.BlockSpec(memory_space=pltpu.SMEM)
BF16 = jnp.bfloat16
F32 = jnp.float32


def sds(shape, dtype):
    return jax.ShapeDtypeStruct(shape, dtype)


def dot(a, b):
    return jnp.dot(a, b, preferred_element_type=F32)


def call(kernel, outs, *args, in_specs=None, out_specs=None, scratch=(), limit=24, flops=0, name=None):
    cost = pl.CostEstimate(flops=flops, bytes_accessed=4 << 20, transcendentals=0)
    return pl.pallas_call(
        kernel,
        out_shape=outs,
        in_specs=in_specs or [VMEM] * len(args),
        out_specs=out_specs or jax.tree.map(lambda _: VMEM, outs),
        scratch_shapes=scratch,
        compiler_params=pltpu.CompilerParams(vmem_limit_bytes=limit << 20),
        cost_estimate=cost,
        name=name,
    )(*args)


def rms(x, gain):
    return x * lax.rsqrt(jnp.mean(x * x, axis=-1, keepdims=True) + 1e-05) * gain


def head_ones(width):
    row = lax.broadcasted_iota(jnp.int32, (width, width), 0) // HEAD_DIM
    lane = lax.broadcasted_iota(jnp.int32, (width, width), 1) // HEAD_DIM
    return jnp.where(row == lane, 1.0 / HEAD_DIM, 0.0).astype(BF16)


def unit(x, ones):
    square = x * x
    high = square.astype(BF16)
    low = (square - high.astype(F32)).astype(BF16)
    mean = dot(high, ones) + dot(low, ones)
    return x * lax.rsqrt(mean + 1e-06)


def copy_in(pairs, sems):
    copies = [pltpu.make_async_copy(src, dst, sems.at[i]) for i, (src, dst) in enumerate(pairs)]
    for copy in copies:
        copy.start()
    return copies


def norm_kernel(
    tok_ref,
    gain_ref,
    coarse_gain_ref,
    normed_ref,
    coarse_ref,
    first_ref,
    second_ref,
    buf,
    gains,
    sems,
):
    rows = tok_ref.shape[0]
    count = rows // NORM_ROWS
    parts = [pl.ds(c * NORM_ROWS, NORM_ROWS) for c in range(count)]
    copies = copy_in(
        [(gain_ref, gains.at[0]), (coarse_gain_ref, gains.at[1])]
        + [(tok_ref.at[part], buf.at[part]) for part in parts],
        sems,
    )
    copies[0].wait()
    copies[1].wait()
    gain = gains[0]
    ones = jnp.ones((8, NORM_ROWS), BF16)
    pooled = []
    for c, part in enumerate(parts):
        copies[2 + c].wait()
        normed = rms(buf[part, :].astype(F32), gain).astype(BF16)
        normed_ref[part, :] = normed
        total = dot(ones, normed)[:1]
        if c * NORM_ROWS % POOL:
            pooled[-1] = pooled[-1] + total
        else:
            pooled.append(total)
    pooled = jnp.concatenate(pooled, 0) * (1.0 / POOL)
    last = jnp.where(lax.axis_index("seq") % 2 == 0, rows - WINDOW, 0)
    for ref, start in ((first_ref, last), (second_ref, rows - WINDOW - last)):
        ref[...] = normed_ref[pl.ds(pl.multiple_of(start, WINDOW), WINDOW), :]
    coarse_ref[...] = rms(pooled, gains[1]).astype(BF16)


def unit_columns(x):
    split = x.reshape(-1, HEAD_DIM, x.shape[1])
    mean = jnp.mean(split * split, axis=1, keepdims=True)
    return split * lax.rsqrt(mean + 1e-06)


def project_columns(weight, rows):
    return lax.dot_general(weight, rows, (((0,), (1,)), ((), ())), preferred_element_type=F32)


def row_parts(rows):
    return [pl.ds(start, PROJ_ROWS) for start in range(0, rows, PROJ_ROWS)]


def query_part(normed, w_ref, scale_ref, q_ref, part):
    q = unit_columns(project_columns(w_ref[...], normed))
    for h in range(q.shape[0]):
        factor = scale_ref[h] * HEAD_DIM ** (-0.5)
        q_ref[h * HEAD_DIM : (h + 1) * HEAD_DIM, part] = (q[h] * factor).astype(BF16)


def query_kernel(normed_ref, w_ref, scale_ref, q_ref):
    for part in row_parts(normed_ref.shape[0]):
        query_part(normed_ref[part, :], w_ref, scale_ref, q_ref, part)


def key_value_kernel(normed_ref, wk_ref, wv_ref, k_ref, v_ref):
    for part in row_parts(normed_ref.shape[0]):
        normed = normed_ref[part, :]
        k = unit_columns(project_columns(wk_ref[...], normed))
        k_ref[:, part] = k.reshape(k_ref.shape[0], PROJ_ROWS).astype(BF16)
        v_ref[part, :] = dot(normed, wv_ref[...]).astype(BF16)


def all_kernel(normed_ref, wk_ref, wv_ref, wq_ref, scale_ref, k_ref, v_ref, q_ref):
    key_value_kernel(normed_ref, wk_ref, wv_ref, k_ref, v_ref)
    query_kernel(normed_ref, wq_ref, scale_ref, q_ref)


def halo_kernel(first_ref, second_ref, wk_ref, wv_ref, k_ref, v_ref):
    odd = lax.axis_index("seq") % 2
    for ref, start in ((first_ref, (1 - odd) * WINDOW), (second_ref, odd * WINDOW)):
        part = pl.ds(pl.multiple_of(start, WINDOW), WINDOW)
        keys = unit_columns(project_columns(wk_ref[...], ref[...]))
        k_ref[:, part] = keys.reshape(k_ref.shape[0], WINDOW).astype(BF16)
        v_ref[part, :] = dot(ref[...], wv_ref[...]).astype(BF16)


def far_kernel(coarse_ref, wk_ref, wv_ref, k_ref, v_ref):
    count = coarse_ref.shape[0]
    coarse = coarse_ref[...]
    keys = unit(dot(coarse, wk_ref[...]), head_ones(v_ref.shape[1]))
    v_ref[...] = jnp.zeros_like(v_ref)
    v_ref[:count, :] = keys.astype(BF16)
    k_ref[...] = v_ref[...].T
    v_ref[:count, :] = dot(coarse, wv_ref[...]).astype(BF16)


def attention_kernel(far_count, edges, q_ref, main_k_ref, main_v_ref, *rest):
    if edges:
        halo_k_ref, halo_v_ref, *rest = rest
    far_k_ref, far_v_ref, o_ref, s_ref, p_ref, *rest = rest
    chunk = o_ref.shape[0]
    blocks = chunk // BQ
    width, rows = q_ref.shape
    heads = width // HEAD_DIM
    stack = heads * BQ
    far_width = far_v_ref.shape[0]
    far_tiles = far_width // 128
    tiles = TILES + far_tiles
    lane_head = lax.broadcasted_iota(jnp.int32, (BQ, width), 1) // HEAD_DIM
    seq_index = lax.axis_index("seq")
    is_first = seq_index == 0
    is_last = seq_index == lax.axis_size("seq") - 1
    quarter = chunk // 2

    if edges:
        k_ref, v_ref = rest
        inner = quarter + WINDOW
        k_ref[:, :WINDOW] = halo_k_ref[:, :WINDOW]
        v_ref[:WINDOW, :] = halo_v_ref[:WINDOW, :]
        k_ref[:, WINDOW : WINDOW + inner] = main_k_ref[:, :inner]
        v_ref[WINDOW : WINDOW + inner, :] = main_v_ref[:inner, :]
        k_ref[:, WINDOW + inner : WINDOW + 2 * inner] = main_k_ref[:, rows - inner :]
        v_ref[WINDOW + inner : WINDOW + 2 * inner, :] = main_v_ref[rows - inner :, :]
        k_ref[:, WINDOW + 2 * inner :] = halo_k_ref[:, WINDOW:]
        v_ref[WINDOW + 2 * inner :, :] = halo_v_ref[WINDOW:, :]
    else:
        k_ref, v_ref = main_k_ref, main_v_ref

    def at_second(b):
        return jnp.where(b >= blocks // 2, 1, 0)

    def query_rows(b):
        start = b * BQ + at_second(b) * (rows - chunk) if edges else quarter + b * BQ
        return pl.ds(pl.multiple_of(start, BQ), BQ)

    def key_rows(b):
        start = b * BQ + at_second(b) * 2 * WINDOW if edges else quarter - WINDOW + b * BQ
        return pl.ds(pl.multiple_of(start, BQ), SPAN)

    def scores(b, slot):
        q = q_ref[:, query_rows(b)].T
        queries = jnp.concatenate(
            [jnp.where(lane_head == h, q, jnp.zeros_like(q)) for h in range(heads)], 0
        )
        keys = jnp.concatenate([k_ref[:, key_rows(b)], far_k_ref[...]], 1)
        s_ref[slot] = dot(queries, keys)

    def hide_outside(b, slot):
        for edge, distance, near, outer in (
            (is_first, b, 1, 0),
            (is_last, blocks - 1 - b, TILES - 2, TILES - 1),
        ):
            for tile, reach in ((near, 1), (outer, 2)):

                @pl.when(edge & (distance < reach))
                def _():
                    s_ref[slot, :, tile * 128 : tile * 128 + 128] = jnp.full(
                        (stack, 128), HIDDEN, F32
                    )

    def softmax(slot):
        lane = lax.broadcasted_iota(jnp.int32, (STRIP, 128), 1)
        ahead = lane - lax.broadcasted_iota(jnp.int32, (STRIP, 128), 0)
        for r in range(0, stack, STRIP):
            at = r % BQ
            part = [s_ref[slot, r : r + STRIP, 128 * t : 128 * t + 128] for t in range(tiles)]
            part[0] = jnp.where(ahead >= at, part[0], HIDDEN)
            part[TILES - 1] = jnp.where(ahead <= at, part[TILES - 1], HIDDEN)
            if far_count < far_width:
                used = far_count - (far_tiles - 1) * 128
                part[-1] = jnp.where(lane < used, part[-1], HIDDEN)
            peak = jnp.max(functools.reduce(jnp.maximum, part), axis=1, keepdims=True)
            part = [jnp.exp(x - peak) for x in part]
            total = jnp.sum(functools.reduce(jnp.add, part), axis=1, keepdims=True)
            scale = 1.0 / total
            for t in range(tiles):
                p_ref[slot, r : r + STRIP, 128 * t : 128 * t + 128] = (part[t] * scale).astype(BF16)

    def mix(b, slot):
        values = jnp.concatenate([v_ref[key_rows(b), :], far_v_ref[...]], 0)
        mixed = dot(p_ref[slot], values)
        out = mixed[:BQ]
        for h in range(1, heads):
            out = jnp.where(lane_head == h, mixed[h * BQ : (h + 1) * BQ], out)
        o_ref[pl.ds(pl.multiple_of(b * BQ, BQ), BQ), :] = out.astype(BF16)

    scores(0, 0)

    @pl.loop(0, blocks // 2)
    def _(i):
        for slot in range(2):
            b = 2 * i + slot
            if edges:
                hide_outside(b, slot)
            mix(jnp.maximum(b - 1, 0), 1 - slot)
            scores(jnp.minimum(b + 1, blocks - 1), 1 - slot)
            softmax(slot)

    mix(blocks - 1, 1)


def out_kernel(starts, own_ref, other_ref, w_ref, *rest):
    o_ref, buf, sems = rest[-3:]
    core = lax.axis_index("head")
    width = own_ref.shape[1]

    def weight(rows_of):
        rows = pl.ds(pl.multiple_of(rows_of * width, width), width)
        return w_ref[rows, pl.ds(pl.multiple_of(core * width, width), width)]

    own_w, other_w = weight(core), weight(1 - core)
    copies = []
    for c in range(own_ref.shape[0] // PROJ_ROWS):
        part = pl.ds(c * PROJ_ROWS, PROJ_ROWS)
        out = dot(own_ref[part, :], own_w) + dot(other_ref[part, :], other_w)
        buf[part, :] = out.astype(BF16)
        target = o_ref.at[pl.ds(starts[c], PROJ_ROWS)]
        copies.append(pltpu.make_async_copy(buf.at[part], target, sems.at[c]))
        copies[-1].start()
    for copy in copies:
        copy.wait()


def swap_heads(x):
    return lax.ppermute(x, "head", [(0, 1), (1, 0)])


def swap_pairs(x, start, seq_size):
    pairs = [(i, i + 1) for i in range(start, seq_size - 1, 2)]
    return lax.ppermute(x, "seq", pairs + [(b, a) for a, b in pairs])


def body(tokens, norm_gain, coarse_gain, w_query, w_key, w_value, w_out, score_scale):
    rows, full = tokens.shape
    heads = score_scale.shape[0]
    width = heads * HEAD_DIM
    seq_size = lax.axis_size("seq")
    pooled = rows // POOL
    power = seq_size & (seq_size - 1) == 0

    normed, coarse, first, second = call(
        norm_kernel,
        (
            sds((rows, full), BF16),
            sds((pooled, full), BF16),
            sds((WINDOW, full), BF16),
            sds((WINDOW, full), BF16),
        ),
        pltpu.with_memory_space_constraint(tokens, pltpu.HBM),
        pltpu.with_memory_space_constraint(norm_gain[None], pltpu.HBM),
        pltpu.with_memory_space_constraint(coarse_gain[None], pltpu.HBM),
        in_specs=[HBM] * 3,
        scratch=[
            pltpu.VMEM((rows, full), BF16),
            pltpu.VMEM((2, 1, full), F32),
            pltpu.SemaphoreType.DMA((rows // NORM_ROWS + 2,)),
        ],
        flops=2 << 30,
        name="norm",
    )
    columns = sds((width, rows), BF16)
    project = functools.partial(call, flops=4 << 30)

    def keys_values_of(x):
        outs = (columns, sds((rows, width), BF16))
        return project(key_value_kernel, outs, x, w_key, w_value, name="keys_values")

    def all_of(x):
        outs = (columns, sds((rows, width), BF16), columns)
        specs = [VMEM] * 4 + [SMEM]
        return project(
            all_kernel, outs, x, w_key, w_value, w_query, score_scale, in_specs=specs, name="all"
        )

    def queries_of(x):
        specs = [VMEM, VMEM, SMEM]
        return project(
            query_kernel, columns, x, w_query, score_scale, in_specs=specs, name="queries"
        )

    first_in = second_in = None
    pending = [keys_values_of, queries_of]
    covered = []
    step = 1
    while pending or (power and step < seq_size):
        received = None
        if power and step < seq_size:
            pairs = [(i, i ^ step) for i in range(seq_size)]
            received = lax.ppermute(coarse, "seq", pairs)
        if pending:
            normed, coarse = lax.optimization_barrier((normed, coarse))
            result = pending.pop(0)(normed)
            if received is not None:
                received, result = lax.optimization_barrier((received, result))
            covered.append(result)
        if first_in is None:
            first_in = swap_pairs(first, 0, seq_size)
        if received is not None:
            coarse = jnp.concatenate([coarse, received], 0)
        if second_in is None and step > 1:
            second, coarse = lax.optimization_barrier((second, coarse))
            second_in = swap_pairs(second, 1, seq_size)
        step *= 2
    (keys, values), queries = covered
    if not power:
        coarse = lax.all_gather(coarse, "seq", axis=0, tiled=True)
    far_count = coarse.shape[0]
    far_width = -(-far_count // 128) * 128
    far_keys, far_values = call(
        far_kernel,
        (sds((width, far_width), BF16), sds((far_width, width), BF16)),
        coarse,
        w_key,
        w_value,
        limit=16,
        name="far",
    )
    stack = heads * BQ
    chunk = rows // 2
    scratch = [
        pltpu.VMEM((2, stack, SPAN + far_width), F32),
        pltpu.VMEM((2, stack, SPAN + far_width), BF16),
    ]
    attend = functools.partial(call, flops=10 << 30)
    middle = attend(
        functools.partial(attention_kernel, far_count, False),
        sds((chunk, width), BF16),
        queries,
        keys,
        values,
        far_keys,
        far_values,
        scratch=scratch,
        name="middle",
    )
    middle_in = swap_heads(middle)
    first_in, second_in, middle = lax.optimization_barrier((first_in, second_in, middle))
    halo_keys, halo_values = call(
        halo_kernel,
        (sds((width, 2 * WINDOW), BF16), sds((2 * WINDOW, width), BF16)),
        first_in,
        second_in,
        w_key,
        w_value,
        limit=16,
        name="halo",
    )
    outer = attend(
        functools.partial(attention_kernel, far_count, True),
        sds((chunk, width), BF16),
        queries,
        keys,
        values,
        halo_keys,
        halo_values,
        far_keys,
        far_values,
        scratch=scratch
        + [
            pltpu.VMEM((width, chunk + 4 * WINDOW), BF16),
            pltpu.VMEM((chunk + 4 * WINDOW, width), BF16),
        ],
        name="outer",
    )
    outer_in = swap_heads(outer)
    quarter = rows // 4
    spans = [
        (middle, middle_in, range(quarter, rows - quarter, PROJ_ROWS)),
        (
            outer,
            outer_in,
            [*range(0, quarter, PROJ_ROWS), *range(rows - quarter, rows, PROJ_ROWS)],
        ),
    ]
    out = []
    for attended, swapped, starts in spans:
        out = [
            pl.pallas_call(
                functools.partial(out_kernel, list(starts)),
                out_shape=sds((rows, width), BF16),
                in_specs=[VMEM] * 3 + [HBM] * len(out),
                out_specs=HBM,
                scratch_shapes=[
                    pltpu.VMEM((chunk, width), BF16),
                    pltpu.SemaphoreType.DMA((chunk // PROJ_ROWS,)),
                ],
                input_output_aliases={3: 0} if out else {},
                compiler_params=pltpu.CompilerParams(vmem_limit_bytes=16 << 20),
                cost_estimate=pl.CostEstimate(
                    flops=1 << 30, bytes_accessed=4 << 20, transcendentals=0
                ),
                name="out",
            )(attended, swapped, w_out, *out)
        ]
    return out[0]


def solution(mesh):
    return jax.shard_map(
        body,
        mesh=mesh,
        in_specs=(
            P(("fields", "seq"), None),
            P(),
            P(),
            P(None, "head"),
            P(None, "head"),
            P(None, "head"),
            P(),
            P("head"),
        ),
        out_specs=P(("fields", "seq"), "head"),
        check_vma=False,
    )
```

time: 55.9 us -> 49.3 us (0.88)
  matrix products: 9.05 us -> 0 us
  Pallas kernels: 31.7 us -> 36.2 us
  local copies, waits for them, and re-layouts: 2.16 us -> 0.02 us
  starting transfers between devices: 9.44 us -> 11.5 us
  other arithmetic: 1.24 us -> 0.02 us
  waiting for transfers between devices: 1.84 us -> 1.07 us
    dot_general x5 -> x0, matrix products: 9.05 us -> none  [the longest x3 5.27 us: project_columns(): lax.dot_general(weight, rows, (((0,), (1,)), ((), ())), preferred_element...]
    pallas_call x3 -> x7, Pallas kernels: 28.6 us -> 33.1 us  [call(): pl.pallas_call(kernel, out_shape=outs, in_specs=in_specs or [VMEM] * len(...]
    unnamed x16 -> x10, local copies, waits for them, and re-layouts: 1.98 us -> 0.02 us
    ppermute x2 -> x3, starting transfers between devices: 2.18 us -> 4.02 us  [body(): received = lax.ppermute(coarse, 'seq', pairs)]
    convert_element_type x3 -> x0, other arithmetic: 1.02 us -> none  [the longest x1 0.61 us: body(): (unit_columns(project_columns(w_query, normed)) * factor).astype(BF16)]
    ppermute x3 -> x2, starting transfers between devices: 2.89 us -> 3.75 us  [swap_heads(): return lax.ppermute(x, 'head', [(0, 1), (1, 0)])]
    ppermute x2 -> x3, waiting for transfers between devices: 0.77 us -> 0.01 us  [body(): received = lax.ppermute(coarse, 'seq', pairs)]
    ppermute x2, starting transfers between devices: 4.38 us -> 3.73 us  [swap_pairs(): return lax.ppermute(x, 'seq', pairs + [(b, a) for a, b in pairs])]
  transfers between devices with their start and end apart: 7 -> 7, of which waited for: 2 -> 1; matrix products, arithmetic and copies ran while one was open for 17% -> 0% of each run, Pallas kernels for 25% -> 63%
where the time goes in v3:
time: 49.3 us; the launch traced here: 49.2 us
  Pallas kernels  36.2 us (73%)
  starting transfers between devices  11.5 us (23%)
  waiting for transfers between devices  1.07 us (2%)
    pallas_call x7, Pallas kernels, call(): pl.pallas_call(kernel, out_shape=outs, in_specs=in_specs or [VMEM] * len(...  33.1 us
    ppermute x3, starting transfers between devices, body(): received = lax.ppermute(coarse, 'seq', pairs)  4.02 us
    ppermute x2, starting transfers between devices, swap_heads(): return lax.ppermute(x, 'head', [(0, 1), (1, 0)])  3.75 us
    ppermute x2, starting transfers between devices, swap_pairs(): return lax.ppermute(x, 'seq', pairs + [(b, a) for a, b in pairs])  3.73 us
    pallas_call x2, Pallas kernels, body(): pl.pallas_call(functools.partial(out_kernel, list(starts)), out_shape=sds...  3.12 us
    ppermute x2, waiting for transfers between devices, swap_heads(): return lax.ppermute(x, 'head', [(0, 1), (1, 0)])  1.06 us
  transfers between devices with their start and end apart: 7, of which 1 were waited for; matrix products, arithmetic and copies ran while one was open for 0% of the time, Pallas kernels for 63%

profile of v3, /device:TPU:7, one launch (start us, length us, event | category | flops | bytes accessed | tf_op | source)
XLA Modules:
  0.0 49.2 jit_solution(11474775205820649441)
XLA Ops:
  0.0 0.0 copy-start.1
  0.0 0.0 copy-start.2
  0.0 3.7 %norm.1 = (bf16[4096,512]{1,0:T(8,128)(2,1)S(1)}, bf16[4,512]{1,0:T(4,128)(2,1)S(1)}, bf16[256,512]{1,0:T(8,128)(2,1)S(1)}, bf16[256,512]{1,0:T(8,128)(2,1)S(1)}) custom-call(bf16[4096,512]{1,0:T(8,128)(2,1)} %tok_ref.1, f32[1,512]{1,0:T(1,128)} %bitcast.2, f32[1,512]{1,0:T(1,128)} %bitcast.3), custom_call_target="tpu_custom_call" | custom-call | flops 2147483648 | bytes 4194304 | tf_op jit(solution)/shard_map/norm/pallas_call | solution.py:38
  3.7 0.3 collective-permute-start
  4.0 0.0 copy-done.1
  4.0 0.0 copy-done.2
  4.0 0.0 copy-start.4
  4.0 2.4 %keys_values.1 = (bf16[256,4096]{1,0:T(8,128)(2,1)S(1)}, bf16[4096,256]{1,0:T(8,128)(2,1)S(1)}) custom-call(bf16[4096,512]{1,0:T(8,128)(2,1)S(1)} %get-tuple-element.36.normed_ref, bf16[512,256]{1,0:T(8,128)(2,1)S(1)} %copy-done.1, bf16[512,256]{1,0:T(8,128)(2,1)S(1)} %copy-done.2), custom_call_target="tpu_custom_call" | custom-call | flops 4294967296 | bytes 4194304 | tf_op jit(solution)/shard_map/keys_values/pallas_call | solution.py:38
  6.5 0.0 collective-permute-done
  6.5 1.4 %collective-permute-start.1 = (bf16[8,512]{1,0:T(8,128)(2,1)S(1)}, bf16[8,512]{1,0:T(8,128)(2,1)S(1)}, u32[]{:S(2)}, u32[]{:S(2)}) collective-permute-start(bf16[8,512]{1,0:T(8,128)(2,1)S(1)} %pad_maximum_fusion.2), channel_id=1, source_target_pairs={{0,4},{2,6},{4,0},{6,2},{8,12},{10,14},{12,8},{14,10},{1,5},{3,7},... | collective-permute-start | bytes 24584 | tf_op jit(solution)/shard_map/ppermute | solution.py:366
  7.9 0.0 copy-done.3
  7.9 0.0 copy-done.4
  7.9 1.9 %queries.1.q_ref = bf16[256,4096]{1,0:T(8,128)(2,1)S(1)} custom-call(bf16[4096,512]{1,0:T(8,128)(2,1)S(1)} %get-tuple-element.36.normed_ref, bf16[512,256]{1,0:T(8,128)(2,1)S(1)} %copy-done.3, f32[4]{0:T(128)S(1)} %copy-done.4), custom_call_target="tpu_custom_call" | custom-call | flops 4294967296 | bytes 4194304 | tf_op jit(solution)/shard_map/queries/pallas_call | solution.py:38
  9.8 0.0 collective-permute-done.1
  9.8 2.4 %collective-permute-start.4 = (bf16[16,512]{1,0:T(8,128)(2,1)S(1)}, bf16[16,512]{1,0:T(8,128)(2,1)S(1)}, u32[]{:S(2)}, u32[]{:S(2)}) collective-permute-start(bf16[16,512]{1,0:T(8,128)(2,1)S(1)} %pad_maximum_fusion.1), channel_id=1, source_target_pairs={{0,8},{2,10},{4,12},{6,14},{8,0},{10,2},{12,4},{14,6},{1,9},{3,11}... | collective-permute-start | bytes 49160 | tf_op jit(solution)/shard_map/ppermute | solution.py:366
  12.2 1.2 %collective-permute-start.2 = (bf16[256,512]{1,0:T(8,128)(2,1)S(1)}, bf16[256,512]{1,0:T(8,128)(2,1)S(1)}, u32[]{:S(2)}, u32[]{:S(2)}) collective-permute-start(bf16[256,512]{1,0:T(8,128)(2,1)S(1)} %get-tuple-element.40), channel_id=1, source_target_pairs={{0,2},{4,6},{8,10},{12,14},{2,0},{6,4},{10,8},{14,12},{1,3},{5,7},... | collective-permute-start | bytes 786440 | tf_op jit(solution)/shard_map/ppermute | solution.py:307
  13.4 2.5 %collective-permute-start.3 = (bf16[256,512]{1,0:T(8,128)(2,1)S(1)}, bf16[256,512]{1,0:T(8,128)(2,1)S(1)}, u32[]{:S(2)}, u32[]{:S(2)}) collective-permute-start(bf16[256,512]{1,0:T(8,128)(2,1)S(1)} %get-tuple-element.44), channel_id=1, source_target_pairs={{2,4},{6,8},{10,12},{4,2},{8,6},{12,10},{3,5},{7,9},{11,13},{5,3},... | collective-permute-start | bytes 786440 | tf_op jit(solution)/shard_map/ppermute | solution.py:307
  15.9 0.0 collective-permute-done.4
  16.0 0.4 far.1
  16.4 11.7 %middle.1.own_ref = bf16[2048,256]{1,0:T(8,128)(2,1)S(1)} custom-call(bf16[256,4096]{1,0:T(8,128)(2,1)S(1)} %queries.1.q_ref, bf16[256,4096]{1,0:T(8,128)(2,1)S(1)} %get-tuple-element.38.main_k_ref, bf16[4096,256]{1,0:T(8,128)(2,1)S(1)} %get-tuple-element.39.main_v_ref, bf16[256,128]{1,0:T(8,128)(2,1)S(1)} %get-tuple-element.46.rest_0_.rest_2_, ...), custom_call_target="tpu_custom_call" | custom-call | flops 10737418240 | bytes 4194304 | tf_op jit(solution)/shard_map/middle/pallas_call | solution.py:38
  28.1 3.7 %collective-permute-start.6 = (bf16[2048,256]{1,0:T(8,128)(2,1)S(1)}, bf16[2048,256]{1,0:T(8,128)(2,1)S(1)}, u32[]{:S(2)}, u32[]{:S(2)}) collective-permute-start(bf16[2048,256]{1,0:T(8,128)(2,1)S(1)} %middle.1.own_ref), channel_id=1, source_target_pairs={{0,1},{1,0},{2,3},{3,2},{4,5},{5,4},{6,7},{7,6},{8,9},{9,8},{10,11... | collective-permute-start | bytes 3145736 | tf_op jit(solution)/shard_map/ppermute | solution.py:302
  31.8 0.0 collective-permute-done.2.first_ref
  31.8 0.0 collective-permute-done.3.second_ref
  31.8 0.5 halo.1
  32.2 0.0 copy-start
  32.2 12.5 %outer.1.own_ref = bf16[2048,256]{1,0:T(8,128)(2,1)S(1)} custom-call(bf16[256,4096]{1,0:T(8,128)(2,1)S(1)} %queries.1.q_ref, bf16[256,4096]{1,0:T(8,128)(2,1)S(1)} %get-tuple-element.38.main_k_ref, bf16[4096,256]{1,0:T(8,128)(2,1)S(1)} %get-tuple-element.39.main_v_ref, bf16[256,512]{1,0:T(8,128)(2,1)S(1)} %get-tuple-element.50.rest_0_, ...), custom_call_target="tpu_custom_call" | custom-call | flops 10737418240 | bytes 4194304 | tf_op jit(solution)/shard_map/outer/pallas_call | solution.py:38
  44.7 0.1 collective-permute-start.5
  44.8 0.0 collective-permute-done.6.other_ref
  44.8 0.0 copy-done
  44.8 1.6 %out.2.rest_0_ = bf16[4096,256]{1,0:T(8,128)(2,1)} custom-call(bf16[2048,256]{1,0:T(8,128)(2,1)S(1)} %middle.1.own_ref, bf16[2048,256]{1,0:T(8,128)(2,1)S(1)} %collective-permute-done.6.other_ref, bf16[512,512]{1,0:T(8,128)(2,1)S(1)} %copy-done), custom_call_target="tpu_custom_call" | custom-call | flops 1073741824 | bytes 4194304 | tf_op jit(solution)/shard_map/out/pallas_call | solution.py:455
  46.4 1.1 %collective-permute-done.5.other_ref = bf16[2048,256]{1,0:T(8,128)(2,1)S(1)} collective-permute-done((bf16[2048,256]{1,0:T(8,128)(2,1)S(1)}, bf16[2048,256]{1,0:T(8,128)(2,1)S(1)}, u32[]{:S(2)}, u32[]{:S(2)}) %collective-permute-start.5) | collective-permute-done | bytes 1048608 | tf_op jit(solution)/shard_map/ppermute | solution.py:302
  47.4 1.6 %out.3 = bf16[4096,256]{1,0:T(8,128)(2,1)} custom-call(bf16[2048,256]{1,0:T(8,128)(2,1)S(1)} %outer.1.own_ref, bf16[2048,256]{1,0:T(8,128)(2,1)S(1)} %collective-permute-done.5.other_ref, bf16[512,512]{1,0:T(8,128)(2,1)S(1)} %copy-done, bf16[4096,256]{1,0:T(8,128)(2,1)} %out.2.rest_0_), custom_call_target="tpu_custom_call", output_to_operand_aliasing={{}: (3, {})} | custom-call | flops 1073741824 | bytes 4194304 | tf_op jit(solution)/shard_map/out/pallas_call | solution.py:455
  (4 shorter events, 0.0 us)
Async XLA Ops:
  0.0 4.0 %copy-start.1 = (bf16[512,256]{1,0:T(8,128)(2,1)S(1)}, bf16[512,256]{1,0:T(8,128)(2,1)}, u32[]{:S(2)}) copy-start(bf16[512,256]{1,0:T(8,128)(2,1)} %wk_ref.5) | copy-start | bytes 786436
  0.0 4.0 %copy-start.2 = (bf16[512,256]{1,0:T(8,128)(2,1)S(1)}, bf16[512,256]{1,0:T(8,128)(2,1)}, u32[]{:S(2)}) copy-start(bf16[512,256]{1,0:T(8,128)(2,1)} %wv_ref.5) | copy-start | bytes 786436
  3.7 2.7 %collective-permute-start = (bf16[4,512]{1,0:T(4,128)(2,1)S(1)}, bf16[4,512]{1,0:T(4,128)(2,1)S(1)}, u32[]{:S(2)}, u32[]{:S(2)}) collective-permute-start(bf16[4,512]{1,0:T(4,128)(2,1)S(1)} %get-tuple-element.31), channel_id=1, source_target_pairs={{0,2},{2,0},{4,6},{6,4},{8,10},{10,8},{12,14},{14,12},{1,3},{3,1},... | collective-permute-start | bytes 12296 | tf_op jit(solution)/shard_map/ppermute | solution.py:366
  4.0 3.8 %copy-start.3 = (bf16[512,256]{1,0:T(8,128)(2,1)S(1)}, bf16[512,256]{1,0:T(8,128)(2,1)}, u32[]{:S(2)}) copy-start(bf16[512,256]{1,0:T(8,128)(2,1)} %w_ref.3) | copy-start | bytes 786436
  4.0 3.8 %copy-start.4 = (f32[4]{0:T(128)S(1)}, f32[4]{0:T(128)}, u32[]{:S(2)}) copy-start(f32[4]{0:T(128)} %scale_ref.1) | copy-start | bytes 52
  6.5 3.3 %collective-permute-start.1 = (bf16[8,512]{1,0:T(8,128)(2,1)S(1)}, bf16[8,512]{1,0:T(8,128)(2,1)S(1)}, u32[]{:S(2)}, u32[]{:S(2)}) collective-permute-start(bf16[8,512]{1,0:T(8,128)(2,1)S(1)} %pad_maximum_fusion.2), channel_id=1, source_target_pairs={{0,4},{2,6},{4,0},{6,2},{8,12},{10,14},{12,8},{14,10},{1,5},{3,7},... | collective-permute-start | bytes 24584 | tf_op jit(solution)/shard_map/ppermute | solution.py:366
  9.8 6.1 %collective-permute-start.4 = (bf16[16,512]{1,0:T(8,128)(2,1)S(1)}, bf16[16,512]{1,0:T(8,128)(2,1)S(1)}, u32[]{:S(2)}, u32[]{:S(2)}) collective-permute-start(bf16[16,512]{1,0:T(8,128)(2,1)S(1)} %pad_maximum_fusion.1), channel_id=1, source_target_pairs={{0,8},{2,10},{4,12},{6,14},{8,0},{10,2},{12,4},{14,6},{1,9},{3,11}... | collective-permute-start | bytes 49160 | tf_op jit(solution)/shard_map/ppermute | solution.py:366
  12.2 19.6 %collective-permute-start.2 = (bf16[256,512]{1,0:T(8,128)(2,1)S(1)}, bf16[256,512]{1,0:T(8,128)(2,1)S(1)}, u32[]{:S(2)}, u32[]{:S(2)}) collective-permute-start(bf16[256,512]{1,0:T(8,128)(2,1)S(1)} %get-tuple-element.40), channel_id=1, source_target_pairs={{0,2},{4,6},{8,10},{12,14},{2,0},{6,4},{10,8},{14,12},{1,3},{5,7},... | collective-permute-start | bytes 786440 | tf_op jit(solution)/shard_map/ppermute | solution.py:307
  13.4 18.3 %collective-permute-start.3 = (bf16[256,512]{1,0:T(8,128)(2,1)S(1)}, bf16[256,512]{1,0:T(8,128)(2,1)S(1)}, u32[]{:S(2)}, u32[]{:S(2)}) collective-permute-start(bf16[256,512]{1,0:T(8,128)(2,1)S(1)} %get-tuple-element.44), channel_id=1, source_target_pairs={{2,4},{6,8},{10,12},{4,2},{8,6},{12,10},{3,5},{7,9},{11,13},{5,3},... | collective-permute-start | bytes 786440 | tf_op jit(solution)/shard_map/ppermute | solution.py:307
  28.1 16.7 %collective-permute-start.6 = (bf16[2048,256]{1,0:T(8,128)(2,1)S(1)}, bf16[2048,256]{1,0:T(8,128)(2,1)S(1)}, u32[]{:S(2)}, u32[]{:S(2)}) collective-permute-start(bf16[2048,256]{1,0:T(8,128)(2,1)S(1)} %middle.1.own_ref), channel_id=1, source_target_pairs={{0,1},{1,0},{2,3},{3,2},{4,5},{5,4},{6,7},{7,6},{8,9},{9,8},{10,11... | collective-permute-start | bytes 3145736 | tf_op jit(solution)/shard_map/ppermute | solution.py:302
  32.2 12.6 %copy-start = (bf16[512,512]{1,0:T(8,128)(2,1)S(1)}, bf16[512,512]{1,0:T(8,128)(2,1)}, u32[]{:S(2)}) copy-start(bf16[512,512]{1,0:T(8,128)(2,1)} %w_ref.5) | copy-start | bytes 1572868
  44.7 2.7 %collective-permute-start.5 = (bf16[2048,256]{1,0:T(8,128)(2,1)S(1)}, bf16[2048,256]{1,0:T(8,128)(2,1)S(1)}, u32[]{:S(2)}, u32[]{:S(2)}) collective-permute-start(bf16[2048,256]{1,0:T(8,128)(2,1)S(1)} %outer.1.own_ref), channel_id=1, source_target_pairs={{0,1},{1,0},{2,3},{3,2},{4,5},{5,4},{6,7},{7,6},{8,9},{9,8},{10,11... | collective-permute-start | bytes 3145736 | tf_op jit(solution)/shard_map/ppermute | solution.py:302

commit v4 on v3

--- a/solution.py
+++ b/solution.py
@@ -16,6 +16,8 @@
 STRIP = 16
 NORM_ROWS = 512
 PROJ_ROWS = 512
+EDGE_ROWS = 512
+OUT_ROWS = 512
 HIDDEN = -1e30
 
 VMEM = pl.BlockSpec(memory_space=pltpu.VMEM)
@@ -187,11 +189,11 @@
     seq_index = lax.axis_index("seq")
     is_first = seq_index == 0
     is_last = seq_index == lax.axis_size("seq") - 1
-    quarter = chunk // 2
+    side = chunk // 2 if edges else (rows - chunk) // 2
 
     if edges:
         k_ref, v_ref = rest
-        inner = quarter + WINDOW
+        inner = side + WINDOW
         k_ref[:, :WINDOW] = halo_k_ref[:, :WINDOW]
         v_ref[:WINDOW, :] = halo_v_ref[:WINDOW, :]
         k_ref[:, WINDOW : WINDOW + inner] = main_k_ref[:, :inner]
@@ -207,11 +209,11 @@
         return jnp.where(b >= blocks // 2, 1, 0)
 
     def query_rows(b):
-        start = b * BQ + at_second(b) * (rows - chunk) if edges else quarter + b * BQ
+        start = b * BQ + at_second(b) * (rows - chunk) if edges else side + b * BQ
         return pl.ds(pl.multiple_of(start, BQ), BQ)
 
     def key_rows(b):
-        start = b * BQ + at_second(b) * 2 * WINDOW if edges else quarter - WINDOW + b * BQ
+        start = b * BQ + at_second(b) * 2 * WINDOW if edges else side - WINDOW + b * BQ
         return pl.ds(pl.multiple_of(start, BQ), SPAN)
 
     def scores(b, slot):
@@ -261,18 +263,24 @@
             out = jnp.where(lane_head == h, mixed[h * BQ : (h + 1) * BQ], out)
         o_ref[pl.ds(pl.multiple_of(b * BQ, BQ), BQ), :] = out.astype(BF16)
 
+    def step(b, slot, mixes=True, scored=True):
+        if edges:
+            hide_outside(b, slot)
+        if mixes:
+            mix(b - 1, 1 - slot)
+        if scored:
+            scores(b + 1, 1 - slot)
+        softmax(slot)
+
     scores(0, 0)
-
-    @pl.loop(0, blocks // 2)
+    step(0, 0, mixes=False)
+
+    @pl.loop(0, (blocks - 2) // 2)
     def _(i):
-        for slot in range(2):
-            b = 2 * i + slot
-            if edges:
-                hide_outside(b, slot)
-            mix(jnp.maximum(b - 1, 0), 1 - slot)
-            scores(jnp.minimum(b + 1, blocks - 1), 1 - slot)
-            softmax(slot)
-
+        step(2 * i + 1, 1)
+        step(2 * i + 2, 0)
+
+    step(blocks - 1, 1, scored=False)
     mix(blocks - 1, 1)
 
 
@@ -285,13 +293,13 @@
         rows = pl.ds(pl.multiple_of(rows_of * width, width), width)
         return w_ref[rows, pl.ds(pl.multiple_of(core * width, width), width)]
 
-    own_w, other_w = weight(core), weight(1 - core)
+    both_w = jnp.concatenate([weight(core), weight(1 - core)], 0)
     copies = []
-    for c in range(own_ref.shape[0] // PROJ_ROWS):
-        part = pl.ds(c * PROJ_ROWS, PROJ_ROWS)
-        out = dot(own_ref[part, :], own_w) + dot(other_ref[part, :], other_w)
+    for c in range(own_ref.shape[0] // OUT_ROWS):
+        part = pl.ds(c * OUT_ROWS, OUT_ROWS)
+        out = dot(jnp.concatenate([own_ref[part, :], other_ref[part, :]], 1), both_w)
         buf[part, :] = out.astype(BF16)
-        target = o_ref.at[pl.ds(starts[c], PROJ_ROWS)]
+        target = o_ref.at[pl.ds(starts[c], OUT_ROWS)]
         copies.append(pltpu.make_async_copy(buf.at[part], target, sems.at[c]))
         copies[-1].start()
     for copy in copies:
@@ -358,10 +366,11 @@
     first_in = second_in = None
     pending = [keys_values_of, queries_of]
     covered = []
-    step = 1
-    while pending or (power and step < seq_size):
+    steps = [1 << i for i in reversed(range(seq_size.bit_length() - 1))] if power else []
+    while pending or steps:
         received = None
-        if power and step < seq_size:
+        if steps:
+            step = steps.pop(0)
             pairs = [(i, i ^ step) for i in range(seq_size)]
             received = lax.ppermute(coarse, "seq", pairs)
         if pending:
@@ -370,14 +379,12 @@
             if received is not None:
                 received, result = lax.optimization_barrier((received, result))
             covered.append(result)
-        if first_in is None:
-            first_in = swap_pairs(first, 0, seq_size)
         if received is not None:
             coarse = jnp.concatenate([coarse, received], 0)
-        if second_in is None and step > 1:
+        if not pending and second_in is None:
             second, coarse = lax.optimization_barrier((second, coarse))
+            first_in = swap_pairs(first, 0, seq_size)
             second_in = swap_pairs(second, 1, seq_size)
-        step *= 2
     (keys, values), queries = covered
     if not power:
         coarse = lax.all_gather(coarse, "seq", axis=0, tiled=True)
@@ -393,7 +400,6 @@
         name="far",
     )
     stack = heads * BQ
-    chunk = rows // 2
     scratch = [
         pltpu.VMEM((2, stack, SPAN + far_width), F32),
         pltpu.VMEM((2, stack, SPAN + far_width), BF16),
@@ -401,7 +407,7 @@
     attend = functools.partial(call, flops=10 << 30)
     middle = attend(
         functools.partial(attention_kernel, far_count, False),
-        sds((chunk, width), BF16),
+        sds((rows - 2 * EDGE_ROWS, width), BF16),
         queries,
         keys,
         values,
@@ -424,7 +430,7 @@
     )
     outer = attend(
         functools.partial(attention_kernel, far_count, True),
-        sds((chunk, width), BF16),
+        sds((2 * EDGE_ROWS, width), BF16),
         queries,
         keys,
         values,
@@ -434,32 +440,28 @@
         far_values,
         scratch=scratch
         + [
-            pltpu.VMEM((width, chunk + 4 * WINDOW), BF16),
-            pltpu.VMEM((chunk + 4 * WINDOW, width), BF16),
+            pltpu.VMEM((width, 2 * EDGE_ROWS + 4 * WINDOW), BF16),
+            pltpu.VMEM((2 * EDGE_ROWS + 4 * WINDOW, width), BF16),
         ],
         name="outer",
     )
     outer_in = swap_heads(outer)
-    quarter = rows // 4
+    last = rows - EDGE_ROWS
     spans = [
-        (middle, middle_in, range(quarter, rows - quarter, PROJ_ROWS)),
-        (
-            outer,
-            outer_in,
-            [*range(0, quarter, PROJ_ROWS), *range(rows - quarter, rows, PROJ_ROWS)],
-        ),
+        (middle, middle_in, [*range(EDGE_ROWS, last, OUT_ROWS)]),
+        (outer, outer_in, [*range(0, EDGE_ROWS, OUT_ROWS), *range(last, rows, OUT_ROWS)]),
     ]
     out = []
     for attended, swapped, starts in spans:
         out = [
             pl.pallas_call(
-                functools.partial(out_kernel, list(starts)),
+                functools.partial(out_kernel, starts),
                 out_shape=sds((rows, width), BF16),
                 in_specs=[VMEM] * 3 + [HBM] * len(out),
                 out_specs=HBM,
                 scratch_shapes=[
-                    pltpu.VMEM((chunk, width), BF16),
-                    pltpu.SemaphoreType.DMA((chunk // PROJ_ROWS,)),
+                    pltpu.VMEM(attended.shape, BF16),
+                    pltpu.SemaphoreType.DMA((len(starts),)),
                 ],
                 input_output_aliases={3: 0} if out else {},
                 compiler_params=pltpu.CompilerParams(vmem_limit_bytes=16 << 20),

time: 49.3 us -> 46.8 us (0.949)
  waiting for transfers between devices: 1.07 us -> 0.02 us
  starting transfers between devices: 11.5 us -> 10.7 us
  Pallas kernels: 36.2 us -> 35.6 us
    ppermute x2, waiting for transfers between devices: 1.06 us -> 0.01 us  [swap_heads(): return lax.ppermute(x, 'head', [(0, 1), (1, 0)])]
    pallas_call x7, Pallas kernels: 33.1 us -> 32.4 us  [call(): pl.pallas_call(kernel, out_shape=outs, in_specs=in_specs or [VMEM] * len(...]
    ppermute x2, starting transfers between devices: 3.75 us -> 3.09 us  [swap_heads(): return lax.ppermute(x, 'head', [(0, 1), (1, 0)])]
  transfers between devices with their start and end apart: 7 -> 7, of which waited for: 1 -> 0; matrix products, arithmetic and copies ran while one was open for 0% -> 0% of each run, Pallas kernels for 63% -> 66%
where the time goes in v4:
time: 46.8 us; the launch traced here: 46.6 us
  Pallas kernels  35.6 us (76%)
  starting transfers between devices  10.7 us (23%)
    pallas_call x7, Pallas kernels, call(): pl.pallas_call(kernel, out_shape=outs, in_specs=in_specs or [VMEM] * len(...  32.4 us
    ppermute x3, starting transfers between devices, body(): received = lax.ppermute(coarse, 'seq', pairs)  4.03 us
    ppermute x2, starting transfers between devices, swap_pairs(): return lax.ppermute(x, 'seq', pairs + [(b, a) for a, b in pairs])  3.55 us
    pallas_call x2, Pallas kernels, body(): pl.pallas_call(functools.partial(out_kernel, starts), out_shape=sds((rows...  3.13 us
    ppermute x2, starting transfers between devices, swap_heads(): return lax.ppermute(x, 'head', [(0, 1), (1, 0)])  3.09 us
  transfers between devices with their start and end apart: 7, of which 0 were waited for; matrix products, arithmetic and copies ran while one was open for 0% of the time, Pallas kernels for 66%

profile of v4, /device:TPU:7, one launch (start us, length us, event | category | flops | bytes accessed | tf_op | source)
XLA Modules:
  0.0 46.6 jit_solution(3105052893232730746)
XLA Ops:
  0.0 0.0 copy-start.1
  0.0 0.0 copy-start.2
  0.0 3.7 %norm.1 = (bf16[4096,512]{1,0:T(8,128)(2,1)S(1)}, bf16[4,512]{1,0:T(4,128)(2,1)S(1)}, bf16[256,512]{1,0:T(8,128)(2,1)S(1)}, bf16[256,512]{1,0:T(8,128)(2,1)S(1)}) custom-call(bf16[4096,512]{1,0:T(8,128)(2,1)} %tok_ref.1, f32[1,512]{1,0:T(1,128)} %bitcast.2, f32[1,512]{1,0:T(1,128)} %bitcast.3), custom_call_target="tpu_custom_call" | custom-call | flops 2147483648 | bytes 4194304 | tf_op jit(solution)/shard_map/norm/pallas_call | solution.py:40
  3.7 2.4 %collective-permute-start = (bf16[4,512]{1,0:T(4,128)(2,1)S(1)}, bf16[4,512]{1,0:T(4,128)(2,1)S(1)}, u32[]{:S(2)}, u32[]{:S(2)}) collective-permute-start(bf16[4,512]{1,0:T(4,128)(2,1)S(1)} %get-tuple-element.31), channel_id=1, source_target_pairs={{0,8},{2,10},{4,12},{6,14},{8,0},{10,2},{12,4},{14,6},{1,9},{3,11}... | collective-permute-start | bytes 12296 | tf_op jit(solution)/shard_map/ppermute | solution.py:375
  6.1 0.0 copy-done.1
  6.1 0.0 copy-done.2
  6.1 0.0 copy-start.3
  6.1 2.4 %keys_values.1 = (bf16[256,4096]{1,0:T(8,128)(2,1)S(1)}, bf16[4096,256]{1,0:T(8,128)(2,1)S(1)}) custom-call(bf16[4096,512]{1,0:T(8,128)(2,1)S(1)} %get-tuple-element.36.normed_ref, bf16[512,256]{1,0:T(8,128)(2,1)S(1)} %copy-done.1, bf16[512,256]{1,0:T(8,128)(2,1)S(1)} %copy-done.2), custom_call_target="tpu_custom_call" | custom-call | flops 4294967296 | bytes 4194304 | tf_op jit(solution)/shard_map/keys_values/pallas_call | solution.py:40
  8.6 0.0 collective-permute-done
  8.6 1.4 %collective-permute-start.1 = (bf16[8,512]{1,0:T(8,128)(2,1)S(1)}, bf16[8,512]{1,0:T(8,128)(2,1)S(1)}, u32[]{:S(2)}, u32[]{:S(2)}) collective-permute-start(bf16[8,512]{1,0:T(8,128)(2,1)S(1)} %pad_maximum_fusion.2), channel_id=1, source_target_pairs={{0,4},{2,6},{4,0},{6,2},{8,12},{10,14},{12,8},{14,10},{1,5},{3,7},... | collective-permute-start | bytes 24584 | tf_op jit(solution)/shard_map/ppermute | solution.py:375
  9.9 0.0 copy-done.3
  9.9 0.0 copy-done.4
  9.9 1.9 %queries.1.q_ref = bf16[256,4096]{1,0:T(8,128)(2,1)S(1)} custom-call(bf16[4096,512]{1,0:T(8,128)(2,1)S(1)} %get-tuple-element.36.normed_ref, bf16[512,256]{1,0:T(8,128)(2,1)S(1)} %copy-done.3, f32[4]{0:T(128)S(1)} %copy-done.4), custom_call_target="tpu_custom_call" | custom-call | flops 4294967296 | bytes 4194304 | tf_op jit(solution)/shard_map/queries/pallas_call | solution.py:40
  11.9 0.0 collective-permute-done.1
  11.9 0.3 collective-permute-start.4
  12.2 1.2 %collective-permute-start.2 = (bf16[256,512]{1,0:T(8,128)(2,1)S(1)}, bf16[256,512]{1,0:T(8,128)(2,1)S(1)}, u32[]{:S(2)}, u32[]{:S(2)}) collective-permute-start(bf16[256,512]{1,0:T(8,128)(2,1)S(1)} %get-tuple-element.40), channel_id=1, source_target_pairs={{0,2},{4,6},{8,10},{12,14},{2,0},{6,4},{10,8},{14,12},{1,3},{5,7},... | collective-permute-start | bytes 786440 | tf_op jit(solution)/shard_map/ppermute | solution.py:315
  13.4 2.3 %collective-permute-start.3 = (bf16[256,512]{1,0:T(8,128)(2,1)S(1)}, bf16[256,512]{1,0:T(8,128)(2,1)S(1)}, u32[]{:S(2)}, u32[]{:S(2)}) collective-permute-start(bf16[256,512]{1,0:T(8,128)(2,1)S(1)} %get-tuple-element.44), channel_id=1, source_target_pairs={{2,4},{6,8},{10,12},{4,2},{8,6},{12,10},{3,5},{7,9},{11,13},{5,3},... | collective-permute-start | bytes 786440 | tf_op jit(solution)/shard_map/ppermute | solution.py:315
  15.8 0.0 collective-permute-done.4
  15.8 0.4 far.1
  16.2 17.0 %middle.1.own_ref = bf16[3072,256]{1,0:T(8,128)(2,1)S(1)} custom-call(bf16[256,4096]{1,0:T(8,128)(2,1)S(1)} %queries.1.q_ref, bf16[256,4096]{1,0:T(8,128)(2,1)S(1)} %get-tuple-element.38.main_k_ref, bf16[4096,256]{1,0:T(8,128)(2,1)S(1)} %get-tuple-element.39.main_v_ref, bf16[256,128]{1,0:T(8,128)(2,1)S(1)} %get-tuple-element.46.rest_0_.rest_2_, ...), custom_call_target="tpu_custom_call" | custom-call | flops 10737418240 | bytes 4194304 | tf_op jit(solution)/shard_map/middle/pallas_call | solution.py:40
  33.2 3.0 %collective-permute-start.6 = (bf16[3072,256]{1,0:T(8,128)(2,1)S(1)}, bf16[3072,256]{1,0:T(8,128)(2,1)S(1)}, u32[]{:S(2)}, u32[]{:S(2)}) collective-permute-start(bf16[3072,256]{1,0:T(8,128)(2,1)S(1)} %middle.1.own_ref), channel_id=1, source_target_pairs={{0,1},{1,0},{2,3},{3,2},{4,5},{5,4},{6,7},{7,6},{8,9},{9,8},{10,11... | collective-permute-start | bytes 4718600 | tf_op jit(solution)/shard_map/ppermute | solution.py:310
  36.2 0.0 collective-permute-done.2.first_ref
  36.2 0.0 collective-permute-done.3.second_ref
  36.2 0.5 halo.1
  36.6 0.0 copy-start
  36.7 6.5 %outer.1.own_ref = bf16[1024,256]{1,0:T(8,128)(2,1)S(1)} custom-call(bf16[256,4096]{1,0:T(8,128)(2,1)S(1)} %queries.1.q_ref, bf16[256,4096]{1,0:T(8,128)(2,1)S(1)} %get-tuple-element.38.main_k_ref, bf16[4096,256]{1,0:T(8,128)(2,1)S(1)} %get-tuple-element.39.main_v_ref, bf16[256,512]{1,0:T(8,128)(2,1)S(1)} %get-tuple-element.50.rest_0_, ...), custom_call_target="tpu_custom_call" | custom-call | flops 10737418240 | bytes 4194304 | tf_op jit(solution)/shard_map/outer/pallas_call | solution.py:40
  43.2 0.1 collective-permute-start.5
  43.3 0.0 collective-permute-done.6.other_ref
  43.3 0.0 copy-done
  43.3 1.9 %out.2.rest_0_ = bf16[4096,256]{1,0:T(8,128)(2,1)} custom-call(bf16[3072,256]{1,0:T(8,128)(2,1)S(1)} %middle.1.own_ref, bf16[3072,256]{1,0:T(8,128)(2,1)S(1)} %collective-permute-done.6.other_ref, bf16[512,512]{1,0:T(8,128)(2,1)S(1)} %copy-done), custom_call_target="tpu_custom_call" | custom-call | flops 1073741824 | bytes 4194304 | tf_op jit(solution)/shard_map/out/pallas_call | solution.py:457
  45.2 0.0 collective-permute-done.5.other_ref
  45.2 1.3 %out.3 = bf16[4096,256]{1,0:T(8,128)(2,1)} custom-call(bf16[1024,256]{1,0:T(8,128)(2,1)S(1)} %outer.1.own_ref, bf16[1024,256]{1,0:T(8,128)(2,1)S(1)} %collective-permute-done.5.other_ref, bf16[512,512]{1,0:T(8,128)(2,1)S(1)} %copy-done, bf16[4096,256]{1,0:T(8,128)(2,1)} %out.2.rest_0_), custom_call_target="tpu_custom_call", output_to_operand_aliasing={{}: (3, {})} | custom-call | flops 1073741824 | bytes 4194304 | tf_op jit(solution)/shard_map/out/pallas_call | solution.py:457
  (4 shorter events, 0.0 us)
Async XLA Ops:
  0.0 6.1 %copy-start.1 = (bf16[512,256]{1,0:T(8,128)(2,1)S(1)}, bf16[512,256]{1,0:T(8,128)(2,1)}, u32[]{:S(2)}) copy-start(bf16[512,256]{1,0:T(8,128)(2,1)} %wk_ref.5) | copy-start | bytes 786436
  0.0 6.1 %copy-start.2 = (bf16[512,256]{1,0:T(8,128)(2,1)S(1)}, bf16[512,256]{1,0:T(8,128)(2,1)}, u32[]{:S(2)}) copy-start(bf16[512,256]{1,0:T(8,128)(2,1)} %wv_ref.5) | copy-start | bytes 786436
  3.7 4.8 %collective-permute-start = (bf16[4,512]{1,0:T(4,128)(2,1)S(1)}, bf16[4,512]{1,0:T(4,128)(2,1)S(1)}, u32[]{:S(2)}, u32[]{:S(2)}) collective-permute-start(bf16[4,512]{1,0:T(4,128)(2,1)S(1)} %get-tuple-element.31), channel_id=1, source_target_pairs={{0,8},{2,10},{4,12},{6,14},{8,0},{10,2},{12,4},{14,6},{1,9},{3,11}... | collective-permute-start | bytes 12296 | tf_op jit(solution)/shard_map/ppermute | solution.py:375
  6.1 3.8 %copy-start.3 = (bf16[512,256]{1,0:T(8,128)(2,1)S(1)}, bf16[512,256]{1,0:T(8,128)(2,1)}, u32[]{:S(2)}) copy-start(bf16[512,256]{1,0:T(8,128)(2,1)} %w_ref.3) | copy-start | bytes 786436
  6.1 3.8 %copy-start.4 = (f32[4]{0:T(128)S(1)}, f32[4]{0:T(128)}, u32[]{:S(2)}) copy-start(f32[4]{0:T(128)} %scale_ref.1) | copy-start | bytes 52
  8.6 3.3 %collective-permute-start.1 = (bf16[8,512]{1,0:T(8,128)(2,1)S(1)}, bf16[8,512]{1,0:T(8,128)(2,1)S(1)}, u32[]{:S(2)}, u32[]{:S(2)}) collective-permute-start(bf16[8,512]{1,0:T(8,128)(2,1)S(1)} %pad_maximum_fusion.2), channel_id=1, source_target_pairs={{0,4},{2,6},{4,0},{6,2},{8,12},{10,14},{12,8},{14,10},{1,5},{3,7},... | collective-permute-start | bytes 24584 | tf_op jit(solution)/shard_map/ppermute | solution.py:375
  11.9 3.8 %collective-permute-start.4 = (bf16[16,512]{1,0:T(8,128)(2,1)S(1)}, bf16[16,512]{1,0:T(8,128)(2,1)S(1)}, u32[]{:S(2)}, u32[]{:S(2)}) collective-permute-start(bf16[16,512]{1,0:T(8,128)(2,1)S(1)} %pad_maximum_fusion.1), channel_id=1, source_target_pairs={{0,2},{2,0},{4,6},{6,4},{8,10},{10,8},{12,14},{14,12},{1,3},{3,1},... | collective-permute-start | bytes 49160 | tf_op jit(solution)/shard_map/ppermute | solution.py:375
  12.2 24.0 %collective-permute-start.2 = (bf16[256,512]{1,0:T(8,128)(2,1)S(1)}, bf16[256,512]{1,0:T(8,128)(2,1)S(1)}, u32[]{:S(2)}, u32[]{:S(2)}) collective-permute-start(bf16[256,512]{1,0:T(8,128)(2,1)S(1)} %get-tuple-element.40), channel_id=1, source_target_pairs={{0,2},{4,6},{8,10},{12,14},{2,0},{6,4},{10,8},{14,12},{1,3},{5,7},... | collective-permute-start | bytes 786440 | tf_op jit(solution)/shard_map/ppermute | solution.py:315
  13.4 22.7 %collective-permute-start.3 = (bf16[256,512]{1,0:T(8,128)(2,1)S(1)}, bf16[256,512]{1,0:T(8,128)(2,1)S(1)}, u32[]{:S(2)}, u32[]{:S(2)}) collective-permute-start(bf16[256,512]{1,0:T(8,128)(2,1)S(1)} %get-tuple-element.44), channel_id=1, source_target_pairs={{2,4},{6,8},{10,12},{4,2},{8,6},{12,10},{3,5},{7,9},{11,13},{5,3},... | collective-permute-start | bytes 786440 | tf_op jit(solution)/shard_map/ppermute | solution.py:315
  33.2 10.1 %collective-permute-start.6 = (bf16[3072,256]{1,0:T(8,128)(2,1)S(1)}, bf16[3072,256]{1,0:T(8,128)(2,1)S(1)}, u32[]{:S(2)}, u32[]{:S(2)}) collective-permute-start(bf16[3072,256]{1,0:T(8,128)(2,1)S(1)} %middle.1.own_ref), channel_id=1, source_target_pairs={{0,1},{1,0},{2,3},{3,2},{4,5},{5,4},{6,7},{7,6},{8,9},{9,8},{10,11... | collective-permute-start | bytes 4718600 | tf_op jit(solution)/shard_map/ppermute | solution.py:310
  36.6 6.6 %copy-start = (bf16[512,512]{1,0:T(8,128)(2,1)S(1)}, bf16[512,512]{1,0:T(8,128)(2,1)}, u32[]{:S(2)}) copy-start(bf16[512,512]{1,0:T(8,128)(2,1)} %w_ref.5) | copy-start | bytes 1572868
  43.2 2.0 %collective-permute-start.5 = (bf16[1024,256]{1,0:T(8,128)(2,1)S(1)}, bf16[1024,256]{1,0:T(8,128)(2,1)S(1)}, u32[]{:S(2)}, u32[]{:S(2)}) collective-permute-start(bf16[1024,256]{1,0:T(8,128)(2,1)S(1)} %outer.1.own_ref), channel_id=1, source_target_pairs={{0,1},{1,0},{2,3},{3,2},{4,5},{5,4},{6,7},{7,6},{8,9},{9,8},{10,11... | collective-permute-start | bytes 1572872 | tf_op jit(solution)/shard_map/ppermute | solution.py:310

commit v5 on v4

--- a/solution.py
+++ b/solution.py
@@ -17,7 +17,7 @@
 NORM_ROWS = 512
 PROJ_ROWS = 512
 EDGE_ROWS = 512
-OUT_ROWS = 512
+OUT_ROWS = 256
 HIDDEN = -1e30
 
 VMEM = pl.BlockSpec(memory_space=pltpu.VMEM)

time: 46.8 us -> 46.7 us (level)
  transfers between devices with their start and end apart: 7 -> 7, of which waited for: 0 -> 1; matrix products, arithmetic and copies ran while one was open for 0% -> 0% of each run, Pallas kernels for 66% -> 66%
where the time goes in v5:
time: 46.7 us; the launch traced here: 46.5 us
  Pallas kernels  35.4 us (76%)
  starting transfers between devices  10.7 us (23%)
    pallas_call x7, Pallas kernels, call(): pl.pallas_call(kernel, out_shape=outs, in_specs=in_specs or [VMEM] * len(...  32.4 us
    ppermute x3, starting transfers between devices, body(): received = lax.ppermute(coarse, 'seq', pairs)  4.03 us
    ppermute x2, starting transfers between devices, swap_pairs(): return lax.ppermute(x, 'seq', pairs + [(b, a) for a, b in pairs])  3.55 us
    ppermute x2, starting transfers between devices, swap_heads(): return lax.ppermute(x, 'head', [(0, 1), (1, 0)])  3.09 us
    pallas_call x2, Pallas kernels, body(): pl.pallas_call(functools.partial(out_kernel, starts), out_shape=sds((rows...  2.98 us
  transfers between devices with their start and end apart: 7, of which 1 were waited for; matrix products, arithmetic and copies ran while one was open for 0% of the time, Pallas kernels for 66%

profile of v5, /device:TPU:7, one launch (start us, length us, event | category | flops | bytes accessed | tf_op | source)
XLA Modules:
  0.0 46.5 jit_solution(10992623363726913881)
XLA Ops:
  0.0 0.0 copy-start.1
  0.0 0.0 copy-start.2
  0.0 3.7 %norm.1 = (bf16[4096,512]{1,0:T(8,128)(2,1)S(1)}, bf16[4,512]{1,0:T(4,128)(2,1)S(1)}, bf16[256,512]{1,0:T(8,128)(2,1)S(1)}, bf16[256,512]{1,0:T(8,128)(2,1)S(1)}) custom-call(bf16[4096,512]{1,0:T(8,128)(2,1)} %tok_ref.1, f32[1,512]{1,0:T(1,128)} %bitcast.2, f32[1,512]{1,0:T(1,128)} %bitcast.3), custom_call_target="tpu_custom_call" | custom-call | flops 2147483648 | bytes 4194304 | tf_op jit(solution)/shard_map/norm/pallas_call | solution.py:40
  3.7 2.4 %collective-permute-start = (bf16[4,512]{1,0:T(4,128)(2,1)S(1)}, bf16[4,512]{1,0:T(4,128)(2,1)S(1)}, u32[]{:S(2)}, u32[]{:S(2)}) collective-permute-start(bf16[4,512]{1,0:T(4,128)(2,1)S(1)} %get-tuple-element.31), channel_id=1, source_target_pairs={{0,8},{2,10},{4,12},{6,14},{8,0},{10,2},{12,4},{14,6},{1,9},{3,11}... | collective-permute-start | bytes 12296 | tf_op jit(solution)/shard_map/ppermute | solution.py:375
  6.1 0.0 copy-done.1
  6.1 0.0 copy-done.2
  6.1 0.0 copy-start.3
  6.1 2.4 %keys_values.1 = (bf16[256,4096]{1,0:T(8,128)(2,1)S(1)}, bf16[4096,256]{1,0:T(8,128)(2,1)S(1)}) custom-call(bf16[4096,512]{1,0:T(8,128)(2,1)S(1)} %get-tuple-element.36.normed_ref, bf16[512,256]{1,0:T(8,128)(2,1)S(1)} %copy-done.1, bf16[512,256]{1,0:T(8,128)(2,1)S(1)} %copy-done.2), custom_call_target="tpu_custom_call" | custom-call | flops 4294967296 | bytes 4194304 | tf_op jit(solution)/shard_map/keys_values/pallas_call | solution.py:40
  8.6 0.0 collective-permute-done
  8.6 1.4 %collective-permute-start.1 = (bf16[8,512]{1,0:T(8,128)(2,1)S(1)}, bf16[8,512]{1,0:T(8,128)(2,1)S(1)}, u32[]{:S(2)}, u32[]{:S(2)}) collective-permute-start(bf16[8,512]{1,0:T(8,128)(2,1)S(1)} %pad_maximum_fusion.2), channel_id=1, source_target_pairs={{0,4},{2,6},{4,0},{6,2},{8,12},{10,14},{12,8},{14,10},{1,5},{3,7},... | collective-permute-start | bytes 24584 | tf_op jit(solution)/shard_map/ppermute | solution.py:375
  9.9 0.0 copy-done.3
  9.9 0.0 copy-done.4
  9.9 1.9 %queries.1.q_ref = bf16[256,4096]{1,0:T(8,128)(2,1)S(1)} custom-call(bf16[4096,512]{1,0:T(8,128)(2,1)S(1)} %get-tuple-element.36.normed_ref, bf16[512,256]{1,0:T(8,128)(2,1)S(1)} %copy-done.3, f32[4]{0:T(128)S(1)} %copy-done.4), custom_call_target="tpu_custom_call" | custom-call | flops 4294967296 | bytes 4194304 | tf_op jit(solution)/shard_map/queries/pallas_call | solution.py:40
  11.9 0.0 collective-permute-done.1
  11.9 0.3 collective-permute-start.4
  12.2 1.2 %collective-permute-start.2 = (bf16[256,512]{1,0:T(8,128)(2,1)S(1)}, bf16[256,512]{1,0:T(8,128)(2,1)S(1)}, u32[]{:S(2)}, u32[]{:S(2)}) collective-permute-start(bf16[256,512]{1,0:T(8,128)(2,1)S(1)} %get-tuple-element.40), channel_id=1, source_target_pairs={{0,2},{4,6},{8,10},{12,14},{2,0},{6,4},{10,8},{14,12},{1,3},{5,7},... | collective-permute-start | bytes 786440 | tf_op jit(solution)/shard_map/ppermute | solution.py:315
  13.4 2.3 %collective-permute-start.3 = (bf16[256,512]{1,0:T(8,128)(2,1)S(1)}, bf16[256,512]{1,0:T(8,128)(2,1)S(1)}, u32[]{:S(2)}, u32[]{:S(2)}) collective-permute-start(bf16[256,512]{1,0:T(8,128)(2,1)S(1)} %get-tuple-element.44), channel_id=1, source_target_pairs={{2,4},{6,8},{10,12},{4,2},{8,6},{12,10},{3,5},{7,9},{11,13},{5,3},... | collective-permute-start | bytes 786440 | tf_op jit(solution)/shard_map/ppermute | solution.py:315
  15.8 0.0 collective-permute-done.4
  15.8 0.4 far.1
  16.2 17.0 %middle.1.own_ref = bf16[3072,256]{1,0:T(8,128)(2,1)S(1)} custom-call(bf16[256,4096]{1,0:T(8,128)(2,1)S(1)} %queries.1.q_ref, bf16[256,4096]{1,0:T(8,128)(2,1)S(1)} %get-tuple-element.38.main_k_ref, bf16[4096,256]{1,0:T(8,128)(2,1)S(1)} %get-tuple-element.39.main_v_ref, bf16[256,128]{1,0:T(8,128)(2,1)S(1)} %get-tuple-element.46.rest_0_.rest_2_, ...), custom_call_target="tpu_custom_call" | custom-call | flops 10737418240 | bytes 4194304 | tf_op jit(solution)/shard_map/middle/pallas_call | solution.py:40
  33.2 3.0 %collective-permute-start.6 = (bf16[3072,256]{1,0:T(8,128)(2,1)S(1)}, bf16[3072,256]{1,0:T(8,128)(2,1)S(1)}, u32[]{:S(2)}, u32[]{:S(2)}) collective-permute-start(bf16[3072,256]{1,0:T(8,128)(2,1)S(1)} %middle.1.own_ref), channel_id=1, source_target_pairs={{0,1},{1,0},{2,3},{3,2},{4,5},{5,4},{6,7},{7,6},{8,9},{9,8},{10,11... | collective-permute-start | bytes 4718600 | tf_op jit(solution)/shard_map/ppermute | solution.py:310
  36.2 0.0 collective-permute-done.2.first_ref
  36.2 0.0 collective-permute-done.3.second_ref
  36.2 0.5 halo.1
  36.6 0.0 copy-start
  36.7 6.5 %outer.1.own_ref = bf16[1024,256]{1,0:T(8,128)(2,1)S(1)} custom-call(bf16[256,4096]{1,0:T(8,128)(2,1)S(1)} %queries.1.q_ref, bf16[256,4096]{1,0:T(8,128)(2,1)S(1)} %get-tuple-element.38.main_k_ref, bf16[4096,256]{1,0:T(8,128)(2,1)S(1)} %get-tuple-element.39.main_v_ref, bf16[256,512]{1,0:T(8,128)(2,1)S(1)} %get-tuple-element.50.rest_0_, ...), custom_call_target="tpu_custom_call" | custom-call | flops 10737418240 | bytes 4194304 | tf_op jit(solution)/shard_map/outer/pallas_call | solution.py:40
  43.2 0.1 collective-permute-start.5
  43.3 0.0 collective-permute-done.6.other_ref
  43.3 0.0 copy-done
  43.3 1.8 %out.2.rest_0_ = bf16[4096,256]{1,0:T(8,128)(2,1)} custom-call(bf16[3072,256]{1,0:T(8,128)(2,1)S(1)} %middle.1.own_ref, bf16[3072,256]{1,0:T(8,128)(2,1)S(1)} %collective-permute-done.6.other_ref, bf16[512,512]{1,0:T(8,128)(2,1)S(1)} %copy-done), custom_call_target="tpu_custom_call" | custom-call | flops 1073741824 | bytes 4194304 | tf_op jit(solution)/shard_map/out/pallas_call | solution.py:457
  45.1 0.1 collective-permute-done.5.other_ref
  45.2 1.2 %out.3 = bf16[4096,256]{1,0:T(8,128)(2,1)} custom-call(bf16[1024,256]{1,0:T(8,128)(2,1)S(1)} %outer.1.own_ref, bf16[1024,256]{1,0:T(8,128)(2,1)S(1)} %collective-permute-done.5.other_ref, bf16[512,512]{1,0:T(8,128)(2,1)S(1)} %copy-done, bf16[4096,256]{1,0:T(8,128)(2,1)} %out.2.rest_0_), custom_call_target="tpu_custom_call", output_to_operand_aliasing={{}: (3, {})} | custom-call | flops 1073741824 | bytes 4194304 | tf_op jit(solution)/shard_map/out/pallas_call | solution.py:457
  (4 shorter events, 0.0 us)
Async XLA Ops:
  0.0 6.1 %copy-start.1 = (bf16[512,256]{1,0:T(8,128)(2,1)S(1)}, bf16[512,256]{1,0:T(8,128)(2,1)}, u32[]{:S(2)}) copy-start(bf16[512,256]{1,0:T(8,128)(2,1)} %wk_ref.5) | copy-start | bytes 786436
  0.0 6.1 %copy-start.2 = (bf16[512,256]{1,0:T(8,128)(2,1)S(1)}, bf16[512,256]{1,0:T(8,128)(2,1)}, u32[]{:S(2)}) copy-start(bf16[512,256]{1,0:T(8,128)(2,1)} %wv_ref.5) | copy-start | bytes 786436
  3.7 4.8 %collective-permute-start = (bf16[4,512]{1,0:T(4,128)(2,1)S(1)}, bf16[4,512]{1,0:T(4,128)(2,1)S(1)}, u32[]{:S(2)}, u32[]{:S(2)}) collective-permute-start(bf16[4,512]{1,0:T(4,128)(2,1)S(1)} %get-tuple-element.31), channel_id=1, source_target_pairs={{0,8},{2,10},{4,12},{6,14},{8,0},{10,2},{12,4},{14,6},{1,9},{3,11}... | collective-permute-start | bytes 12296 | tf_op jit(solution)/shard_map/ppermute | solution.py:375
  6.1 3.8 %copy-start.3 = (bf16[512,256]{1,0:T(8,128)(2,1)S(1)}, bf16[512,256]{1,0:T(8,128)(2,1)}, u32[]{:S(2)}) copy-start(bf16[512,256]{1,0:T(8,128)(2,1)} %w_ref.3) | copy-start | bytes 786436
  6.1 3.8 %copy-start.4 = (f32[4]{0:T(128)S(1)}, f32[4]{0:T(128)}, u32[]{:S(2)}) copy-start(f32[4]{0:T(128)} %scale_ref.1) | copy-start | bytes 52
  8.6 3.3 %collective-permute-start.1 = (bf16[8,512]{1,0:T(8,128)(2,1)S(1)}, bf16[8,512]{1,0:T(8,128)(2,1)S(1)}, u32[]{:S(2)}, u32[]{:S(2)}) collective-permute-start(bf16[8,512]{1,0:T(8,128)(2,1)S(1)} %pad_maximum_fusion.2), channel_id=1, source_target_pairs={{0,4},{2,6},{4,0},{6,2},{8,12},{10,14},{12,8},{14,10},{1,5},{3,7},... | collective-permute-start | bytes 24584 | tf_op jit(solution)/shard_map/ppermute | solution.py:375
  11.9 3.8 %collective-permute-start.4 = (bf16[16,512]{1,0:T(8,128)(2,1)S(1)}, bf16[16,512]{1,0:T(8,128)(2,1)S(1)}, u32[]{:S(2)}, u32[]{:S(2)}) collective-permute-start(bf16[16,512]{1,0:T(8,128)(2,1)S(1)} %pad_maximum_fusion.1), channel_id=1, source_target_pairs={{0,2},{2,0},{4,6},{6,4},{8,10},{10,8},{12,14},{14,12},{1,3},{3,1},... | collective-permute-start | bytes 49160 | tf_op jit(solution)/shard_map/ppermute | solution.py:375
  12.2 24.0 %collective-permute-start.2 = (bf16[256,512]{1,0:T(8,128)(2,1)S(1)}, bf16[256,512]{1,0:T(8,128)(2,1)S(1)}, u32[]{:S(2)}, u32[]{:S(2)}) collective-permute-start(bf16[256,512]{1,0:T(8,128)(2,1)S(1)} %get-tuple-element.40), channel_id=1, source_target_pairs={{0,2},{4,6},{8,10},{12,14},{2,0},{6,4},{10,8},{14,12},{1,3},{5,7},... | collective-permute-start | bytes 786440 | tf_op jit(solution)/shard_map/ppermute | solution.py:315
  13.4 22.7 %collective-permute-start.3 = (bf16[256,512]{1,0:T(8,128)(2,1)S(1)}, bf16[256,512]{1,0:T(8,128)(2,1)S(1)}, u32[]{:S(2)}, u32[]{:S(2)}) collective-permute-start(bf16[256,512]{1,0:T(8,128)(2,1)S(1)} %get-tuple-element.44), channel_id=1, source_target_pairs={{2,4},{6,8},{10,12},{4,2},{8,6},{12,10},{3,5},{7,9},{11,13},{5,3},... | collective-permute-start | bytes 786440 | tf_op jit(solution)/shard_map/ppermute | solution.py:315
  33.2 10.1 %collective-permute-start.6 = (bf16[3072,256]{1,0:T(8,128)(2,1)S(1)}, bf16[3072,256]{1,0:T(8,128)(2,1)S(1)}, u32[]{:S(2)}, u32[]{:S(2)}) collective-permute-start(bf16[3072,256]{1,0:T(8,128)(2,1)S(1)} %middle.1.own_ref), channel_id=1, source_target_pairs={{0,1},{1,0},{2,3},{3,2},{4,5},{5,4},{6,7},{7,6},{8,9},{9,8},{10,11... | collective-permute-start | bytes 4718600 | tf_op jit(solution)/shard_map/ppermute | solution.py:310
  36.6 6.6 %copy-start = (bf16[512,512]{1,0:T(8,128)(2,1)S(1)}, bf16[512,512]{1,0:T(8,128)(2,1)}, u32[]{:S(2)}) copy-start(bf16[512,512]{1,0:T(8,128)(2,1)} %w_ref.5) | copy-start | bytes 1572868
  43.2 2.0 %collective-permute-start.5 = (bf16[1024,256]{1,0:T(8,128)(2,1)S(1)}, bf16[1024,256]{1,0:T(8,128)(2,1)S(1)}, u32[]{:S(2)}, u32[]{:S(2)}) collective-permute-start(bf16[1024,256]{1,0:T(8,128)(2,1)S(1)} %outer.1.own_ref), channel_id=1, source_target_pairs={{0,1},{1,0},{2,3},{3,2},{4,5},{5,4},{6,7},{7,6},{8,9},{9,8},{10,11... | collective-permute-start | bytes 1572872 | tf_op jit(solution)/shard_map/ppermute | solution.py:310

commit v6 on v5

--- a/solution.py
+++ b/solution.py
@@ -154,15 +154,6 @@
     query_kernel(normed_ref, wq_ref, scale_ref, q_ref)
 
 
-def halo_kernel(first_ref, second_ref, wk_ref, wv_ref, k_ref, v_ref):
-    odd = lax.axis_index("seq") % 2
-    for ref, start in ((first_ref, (1 - odd) * WINDOW), (second_ref, odd * WINDOW)):
-        part = pl.ds(pl.multiple_of(start, WINDOW), WINDOW)
-        keys = unit_columns(project_columns(wk_ref[...], ref[...]))
-        k_ref[:, part] = keys.reshape(k_ref.shape[0], WINDOW).astype(BF16)
-        v_ref[part, :] = dot(ref[...], wv_ref[...]).astype(BF16)
-
-
 def far_kernel(coarse_ref, wk_ref, wv_ref, k_ref, v_ref):
     count = coarse_ref.shape[0]
     coarse = coarse_ref[...]
@@ -175,7 +166,7 @@
 
 def attention_kernel(far_count, edges, q_ref, main_k_ref, main_v_ref, *rest):
     if edges:
-        halo_k_ref, halo_v_ref, *rest = rest
+        first_ref, second_ref, wk_ref, wv_ref, *rest = rest
     far_k_ref, far_v_ref, o_ref, s_ref, p_ref, *rest = rest
     chunk = o_ref.shape[0]
     blocks = chunk // BQ
@@ -194,14 +185,17 @@
     if edges:
         k_ref, v_ref = rest
         inner = side + WINDOW
-        k_ref[:, :WINDOW] = halo_k_ref[:, :WINDOW]
-        v_ref[:WINDOW, :] = halo_v_ref[:WINDOW, :]
+        odd = seq_index % 2
+        top = WINDOW + 2 * inner
+        for ref, start in ((first_ref, (1 - odd) * top), (second_ref, odd * top)):
+            part = pl.ds(pl.multiple_of(start, WINDOW), WINDOW)
+            keys = unit_columns(project_columns(wk_ref[...], ref[...]))
+            k_ref[:, part] = keys.reshape(width, WINDOW).astype(BF16)
+            v_ref[part, :] = dot(ref[...], wv_ref[...]).astype(BF16)
         k_ref[:, WINDOW : WINDOW + inner] = main_k_ref[:, :inner]
         v_ref[WINDOW : WINDOW + inner, :] = main_v_ref[:inner, :]
         k_ref[:, WINDOW + inner : WINDOW + 2 * inner] = main_k_ref[:, rows - inner :]
         v_ref[WINDOW + inner : WINDOW + 2 * inner, :] = main_v_ref[rows - inner :, :]
-        k_ref[:, WINDOW + 2 * inner :] = halo_k_ref[:, WINDOW:]
-        v_ref[WINDOW + 2 * inner :, :] = halo_v_ref[WINDOW:, :]
     else:
         k_ref, v_ref = main_k_ref, main_v_ref
 
@@ -367,6 +361,8 @@
     pending = [keys_values_of, queries_of]
     covered = []
     steps = [1 << i for i in reversed(range(seq_size.bit_length() - 1))] if power else []
+    if len(steps) > 2:
+        steps[0], steps[1] = steps[1], steps[0]
     while pending or steps:
         received = None
         if steps:
@@ -418,24 +414,16 @@
     )
     middle_in = swap_heads(middle)
     first_in, second_in, middle = lax.optimization_barrier((first_in, second_in, middle))
-    halo_keys, halo_values = call(
-        halo_kernel,
-        (sds((width, 2 * WINDOW), BF16), sds((2 * WINDOW, width), BF16)),
-        first_in,
-        second_in,
-        w_key,
-        w_value,
-        limit=16,
-        name="halo",
-    )
     outer = attend(
         functools.partial(attention_kernel, far_count, True),
         sds((2 * EDGE_ROWS, width), BF16),
         queries,
         keys,
         values,
-        halo_keys,
-        halo_values,
+        first_in,
+        second_in,
+        w_key,
+        w_value,
         far_keys,
         far_values,
         scratch=scratch

time: 46.7 us -> 46.4 us (level)
  starting transfers between devices: 10.7 us -> 10.2 us
    pallas_call x7 -> x6, Pallas kernels: 32.4 us -> 32.3 us  [call(): pl.pallas_call(kernel, out_shape=outs, in_specs=in_specs or [VMEM] * len(...]
where the time goes in v6:
time: 46.4 us; the launch traced here: 45.9 us
  Pallas kernels  35.3 us (76%)
  starting transfers between devices  10.2 us (22%)
    pallas_call x6, Pallas kernels, call(): pl.pallas_call(kernel, out_shape=outs, in_specs=in_specs or [VMEM] * len(...  32.3 us
    ppermute x3, starting transfers between devices, body(): received = lax.ppermute(coarse, 'seq', pairs)  4.02 us
    ppermute x2, starting transfers between devices, swap_pairs(): return lax.ppermute(x, 'seq', pairs + [(b, a) for a, b in pairs])  3.25 us
    pallas_call x2, Pallas kernels, body(): pl.pallas_call(functools.partial(out_kernel, starts), out_shape=sds((rows...  2.98 us
    ppermute x2, starting transfers between devices, swap_heads(): return lax.ppermute(x, 'head', [(0, 1), (1, 0)])  2.93 us
  transfers between devices with their start and end apart: 7, of which 1 were waited for; matrix products, arithmetic and copies ran while one was open for 0% of the time, Pallas kernels for 66%

profile of v6, /device:TPU:7, one launch (start us, length us, event | category | flops | bytes accessed | tf_op | source)
XLA Modules:
  0.0 45.9 jit_solution(6912237136355892059)
XLA Ops:
  0.0 0.0 copy-start.1
  0.0 0.0 copy-start.2
  0.0 3.7 %norm.1 = (bf16[4096,512]{1,0:T(8,128)(2,1)S(1)}, bf16[4,512]{1,0:T(4,128)(2,1)S(1)}, bf16[256,512]{1,0:T(8,128)(2,1)S(1)}, bf16[256,512]{1,0:T(8,128)(2,1)S(1)}) custom-call(bf16[4096,512]{1,0:T(8,128)(2,1)} %tok_ref.1, f32[1,512]{1,0:T(1,128)} %bitcast.2, f32[1,512]{1,0:T(1,128)} %bitcast.3), custom_call_target="tpu_custom_call" | custom-call | flops 2147483648 | bytes 4194304 | tf_op jit(solution)/shard_map/norm/pallas_call | solution.py:40
  3.7 1.4 %collective-permute-start = (bf16[4,512]{1,0:T(4,128)(2,1)S(1)}, bf16[4,512]{1,0:T(4,128)(2,1)S(1)}, u32[]{:S(2)}, u32[]{:S(2)}) collective-permute-start(bf16[4,512]{1,0:T(4,128)(2,1)S(1)} %get-tuple-element.29), channel_id=1, source_target_pairs={{0,4},{2,6},{4,0},{6,2},{8,12},{10,14},{12,8},{14,10},{1,5},{3,7},... | collective-permute-start | bytes 12296 | tf_op jit(solution)/shard_map/ppermute | solution.py:371
  5.1 0.0 copy-done.1
  5.1 0.0 copy-done.2
  5.1 0.0 copy-start.3
  5.1 0.0 copy-start.4
  5.1 2.4 %keys_values.1 = (bf16[256,4096]{1,0:T(8,128)(2,1)S(1)}, bf16[4096,256]{1,0:T(8,128)(2,1)S(1)}) custom-call(bf16[4096,512]{1,0:T(8,128)(2,1)S(1)} %get-tuple-element.34.normed_ref, bf16[512,256]{1,0:T(8,128)(2,1)S(1)} %copy-done.1, bf16[512,256]{1,0:T(8,128)(2,1)S(1)} %copy-done.2), custom_call_target="tpu_custom_call" | custom-call | flops 4294967296 | bytes 4194304 | tf_op jit(solution)/shard_map/keys_values/pallas_call | solution.py:40
  7.5 0.0 collective-permute-done
  7.6 2.4 %collective-permute-start.1 = (bf16[8,512]{1,0:T(8,128)(2,1)S(1)}, bf16[8,512]{1,0:T(8,128)(2,1)S(1)}, u32[]{:S(2)}, u32[]{:S(2)}) collective-permute-start(bf16[8,512]{1,0:T(8,128)(2,1)S(1)} %pad_maximum_fusion.2), channel_id=1, source_target_pairs={{0,8},{2,10},{4,12},{6,14},{8,0},{10,2},{12,4},{14,6},{1,9},{3,11}... | collective-permute-start | bytes 24584 | tf_op jit(solution)/shard_map/ppermute | solution.py:371
  9.9 0.0 copy-done.3
  9.9 0.0 copy-done.4
  9.9 1.9 %queries.1.q_ref = bf16[256,4096]{1,0:T(8,128)(2,1)S(1)} custom-call(bf16[4096,512]{1,0:T(8,128)(2,1)S(1)} %get-tuple-element.34.normed_ref, bf16[512,256]{1,0:T(8,128)(2,1)S(1)} %copy-done.3, f32[4]{0:T(128)S(1)} %copy-done.4), custom_call_target="tpu_custom_call" | custom-call | flops 4294967296 | bytes 4194304 | tf_op jit(solution)/shard_map/queries/pallas_call | solution.py:40
  11.9 0.0 collective-permute-done.1
  11.9 0.3 collective-permute-start.4
  12.2 1.2 %collective-permute-start.2 = (bf16[256,512]{1,0:T(8,128)(2,1)S(1)}, bf16[256,512]{1,0:T(8,128)(2,1)S(1)}, u32[]{:S(2)}, u32[]{:S(2)}) collective-permute-start(bf16[256,512]{1,0:T(8,128)(2,1)S(1)} %get-tuple-element.38), channel_id=1, source_target_pairs={{0,2},{4,6},{8,10},{12,14},{2,0},{6,4},{10,8},{14,12},{1,3},{5,7},... | collective-permute-start | bytes 786440 | tf_op jit(solution)/shard_map/ppermute | solution.py:309
  13.4 2.0 %collective-permute-start.3 = (bf16[256,512]{1,0:T(8,128)(2,1)S(1)}, bf16[256,512]{1,0:T(8,128)(2,1)S(1)}, u32[]{:S(2)}, u32[]{:S(2)}) collective-permute-start(bf16[256,512]{1,0:T(8,128)(2,1)S(1)} %get-tuple-element.42), channel_id=1, source_target_pairs={{2,4},{6,8},{10,12},{4,2},{8,6},{12,10},{3,5},{7,9},{11,13},{5,3},... | collective-permute-start | bytes 786440 | tf_op jit(solution)/shard_map/ppermute | solution.py:309
  15.5 0.0 collective-permute-done.4
  15.5 0.4 far.1
  15.9 17.0 %middle.1.own_ref = bf16[3072,256]{1,0:T(8,128)(2,1)S(1)} custom-call(bf16[256,4096]{1,0:T(8,128)(2,1)S(1)} %queries.1.q_ref, bf16[256,4096]{1,0:T(8,128)(2,1)S(1)} %get-tuple-element.36.main_k_ref, bf16[4096,256]{1,0:T(8,128)(2,1)S(1)} %get-tuple-element.37.main_v_ref, bf16[256,128]{1,0:T(8,128)(2,1)S(1)} %get-tuple-element.44.rest_0_.rest_4_, ...), custom_call_target="tpu_custom_call" | custom-call | flops 10737418240 | bytes 4194304 | tf_op jit(solution)/shard_map/middle/pallas_call | solution.py:40
  32.9 0.0 copy-start
  32.9 2.8 %collective-permute-start.6 = (bf16[3072,256]{1,0:T(8,128)(2,1)S(1)}, bf16[3072,256]{1,0:T(8,128)(2,1)S(1)}, u32[]{:S(2)}, u32[]{:S(2)}) collective-permute-start(bf16[3072,256]{1,0:T(8,128)(2,1)S(1)} %middle.1.own_ref), channel_id=1, source_target_pairs={{0,1},{1,0},{2,3},{3,2},{4,5},{5,4},{6,7},{7,6},{8,9},{9,8},{10,11... | collective-permute-start | bytes 4718600 | tf_op jit(solution)/shard_map/ppermute | solution.py:304
  35.7 0.0 collective-permute-done.2.rest_0_
  35.7 0.0 collective-permute-done.3.rest_1_
  35.7 6.8 %outer.1.own_ref = bf16[1024,256]{1,0:T(8,128)(2,1)S(1)} custom-call(bf16[256,4096]{1,0:T(8,128)(2,1)S(1)} %queries.1.q_ref, bf16[256,4096]{1,0:T(8,128)(2,1)S(1)} %get-tuple-element.36.main_k_ref, bf16[4096,256]{1,0:T(8,128)(2,1)S(1)} %get-tuple-element.37.main_v_ref, bf16[256,512]{1,0:T(8,128)(2,1)S(1)} %collective-permute-done.2.rest_0_, ...), custom_call_target="tpu_custom_call" | custom-call | flops 10737418240 | bytes 4194304 | tf_op jit(solution)/shard_map/outer/pallas_call | solution.py:40
  42.6 0.1 collective-permute-start.5
  42.7 0.0 collective-permute-done.6.other_ref
  42.7 0.0 copy-done
  42.7 1.8 %out.2.rest_0_ = bf16[4096,256]{1,0:T(8,128)(2,1)} custom-call(bf16[3072,256]{1,0:T(8,128)(2,1)S(1)} %middle.1.own_ref, bf16[3072,256]{1,0:T(8,128)(2,1)S(1)} %collective-permute-done.6.other_ref, bf16[512,512]{1,0:T(8,128)(2,1)S(1)} %copy-done), custom_call_target="tpu_custom_call" | custom-call | flops 1073741824 | bytes 4194304 | tf_op jit(solution)/shard_map/out/pallas_call | solution.py:445
  44.5 0.1 collective-permute-done.5.other_ref
  44.5 1.2 %out.3 = bf16[4096,256]{1,0:T(8,128)(2,1)} custom-call(bf16[1024,256]{1,0:T(8,128)(2,1)S(1)} %outer.1.own_ref, bf16[1024,256]{1,0:T(8,128)(2,1)S(1)} %collective-permute-done.5.other_ref, bf16[512,512]{1,0:T(8,128)(2,1)S(1)} %copy-done, bf16[4096,256]{1,0:T(8,128)(2,1)} %out.2.rest_0_), custom_call_target="tpu_custom_call", output_to_operand_aliasing={{}: (3, {})} | custom-call | flops 1073741824 | bytes 4194304 | tf_op jit(solution)/shard_map/out/pallas_call | solution.py:445
  (3 shorter events, 0.0 us)
Async XLA Ops:
  0.0 5.1 %copy-start.1 = (bf16[512,256]{1,0:T(8,128)(2,1)S(1)}, bf16[512,256]{1,0:T(8,128)(2,1)}, u32[]{:S(2)}) copy-start(bf16[512,256]{1,0:T(8,128)(2,1)} %rest_2_.1) | copy-start | bytes 786436
  0.0 5.1 %copy-start.2 = (bf16[512,256]{1,0:T(8,128)(2,1)S(1)}, bf16[512,256]{1,0:T(8,128)(2,1)}, u32[]{:S(2)}) copy-start(bf16[512,256]{1,0:T(8,128)(2,1)} %rest_3_.1) | copy-start | bytes 786436
  3.7 3.8 %collective-permute-start = (bf16[4,512]{1,0:T(4,128)(2,1)S(1)}, bf16[4,512]{1,0:T(4,128)(2,1)S(1)}, u32[]{:S(2)}, u32[]{:S(2)}) collective-permute-start(bf16[4,512]{1,0:T(4,128)(2,1)S(1)} %get-tuple-element.29), channel_id=1, source_target_pairs={{0,4},{2,6},{4,0},{6,2},{8,12},{10,14},{12,8},{14,10},{1,5},{3,7},... | collective-permute-start | bytes 12296 | tf_op jit(solution)/shard_map/ppermute | solution.py:371
  5.1 4.8 %copy-start.3 = (bf16[512,256]{1,0:T(8,128)(2,1)S(1)}, bf16[512,256]{1,0:T(8,128)(2,1)}, u32[]{:S(2)}) copy-start(bf16[512,256]{1,0:T(8,128)(2,1)} %w_ref.3) | copy-start | bytes 786436
  5.1 4.8 %copy-start.4 = (f32[4]{0:T(128)S(1)}, f32[4]{0:T(128)}, u32[]{:S(2)}) copy-start(f32[4]{0:T(128)} %scale_ref.1) | copy-start | bytes 52
  7.6 4.3 %collective-permute-start.1 = (bf16[8,512]{1,0:T(8,128)(2,1)S(1)}, bf16[8,512]{1,0:T(8,128)(2,1)S(1)}, u32[]{:S(2)}, u32[]{:S(2)}) collective-permute-start(bf16[8,512]{1,0:T(8,128)(2,1)S(1)} %pad_maximum_fusion.2), channel_id=1, source_target_pairs={{0,8},{2,10},{4,12},{6,14},{8,0},{10,2},{12,4},{14,6},{1,9},{3,11}... | collective-permute-start | bytes 24584 | tf_op jit(solution)/shard_map/ppermute | solution.py:371
  11.9 3.5 %collective-permute-start.4 = (bf16[16,512]{1,0:T(8,128)(2,1)S(1)}, bf16[16,512]{1,0:T(8,128)(2,1)S(1)}, u32[]{:S(2)}, u32[]{:S(2)}) collective-permute-start(bf16[16,512]{1,0:T(8,128)(2,1)S(1)} %pad_maximum_fusion.1), channel_id=1, source_target_pairs={{0,2},{2,0},{4,6},{6,4},{8,10},{10,8},{12,14},{14,12},{1,3},{3,1},... | collective-permute-start | bytes 49160 | tf_op jit(solution)/shard_map/ppermute | solution.py:371
  12.2 23.5 %collective-permute-start.2 = (bf16[256,512]{1,0:T(8,128)(2,1)S(1)}, bf16[256,512]{1,0:T(8,128)(2,1)S(1)}, u32[]{:S(2)}, u32[]{:S(2)}) collective-permute-start(bf16[256,512]{1,0:T(8,128)(2,1)S(1)} %get-tuple-element.38), channel_id=1, source_target_pairs={{0,2},{4,6},{8,10},{12,14},{2,0},{6,4},{10,8},{14,12},{1,3},{5,7},... | collective-permute-start | bytes 786440 | tf_op jit(solution)/shard_map/ppermute | solution.py:309
  13.4 22.3 %collective-permute-start.3 = (bf16[256,512]{1,0:T(8,128)(2,1)S(1)}, bf16[256,512]{1,0:T(8,128)(2,1)S(1)}, u32[]{:S(2)}, u32[]{:S(2)}) collective-permute-start(bf16[256,512]{1,0:T(8,128)(2,1)S(1)} %get-tuple-element.42), channel_id=1, source_target_pairs={{2,4},{6,8},{10,12},{4,2},{8,6},{12,10},{3,5},{7,9},{11,13},{5,3},... | collective-permute-start | bytes 786440 | tf_op jit(solution)/shard_map/ppermute | solution.py:309
  32.9 9.8 %copy-start = (bf16[512,512]{1,0:T(8,128)(2,1)S(1)}, bf16[512,512]{1,0:T(8,128)(2,1)}, u32[]{:S(2)}) copy-start(bf16[512,512]{1,0:T(8,128)(2,1)} %w_ref.5) | copy-start | bytes 1572868
  32.9 9.8 %collective-permute-start.6 = (bf16[3072,256]{1,0:T(8,128)(2,1)S(1)}, bf16[3072,256]{1,0:T(8,128)(2,1)S(1)}, u32[]{:S(2)}, u32[]{:S(2)}) collective-permute-start(bf16[3072,256]{1,0:T(8,128)(2,1)S(1)} %middle.1.own_ref), channel_id=1, source_target_pairs={{0,1},{1,0},{2,3},{3,2},{4,5},{5,4},{6,7},{7,6},{8,9},{9,8},{10,11... | collective-permute-start | bytes 4718600 | tf_op jit(solution)/shard_map/ppermute | solution.py:304
  42.6 2.0 %collective-permute-start.5 = (bf16[1024,256]{1,0:T(8,128)(2,1)S(1)}, bf16[1024,256]{1,0:T(8,128)(2,1)S(1)}, u32[]{:S(2)}, u32[]{:S(2)}) collective-permute-start(bf16[1024,256]{1,0:T(8,128)(2,1)S(1)} %outer.1.own_ref), channel_id=1, source_target_pairs={{0,1},{1,0},{2,3},{3,2},{4,5},{5,4},{6,7},{7,6},{8,9},{9,8},{10,11... | collective-permute-start | bytes 1572872 | tf_op jit(solution)/shard_map/ppermute | solution.py:304

commit v7 on v6

--- a/solution.py
+++ b/solution.py
@@ -167,7 +167,10 @@
 def attention_kernel(far_count, edges, q_ref, main_k_ref, main_v_ref, *rest):
     if edges:
         first_ref, second_ref, wk_ref, wv_ref, *rest = rest
-    far_k_ref, far_v_ref, o_ref, s_ref, p_ref, *rest = rest
+        far_k_ref, far_v_ref, o_ref, s_ref, p_ref, *rest = rest
+    else:
+        coarse_ref, wk_ref, wv_ref, o_ref, far_k_ref, far_v_ref, s_ref, p_ref = rest
+        far_kernel(coarse_ref, wk_ref, wv_ref, far_k_ref, far_v_ref)
     chunk = o_ref.shape[0]
     blocks = chunk // BQ
     width, rows = q_ref.shape
@@ -386,29 +389,25 @@
         coarse = lax.all_gather(coarse, "seq", axis=0, tiled=True)
     far_count = coarse.shape[0]
     far_width = -(-far_count // 128) * 128
-    far_keys, far_values = call(
-        far_kernel,
-        (sds((width, far_width), BF16), sds((far_width, width), BF16)),
-        coarse,
-        w_key,
-        w_value,
-        limit=16,
-        name="far",
-    )
     stack = heads * BQ
     scratch = [
         pltpu.VMEM((2, stack, SPAN + far_width), F32),
         pltpu.VMEM((2, stack, SPAN + far_width), BF16),
     ]
     attend = functools.partial(call, flops=10 << 30)
-    middle = attend(
+    middle, far_keys, far_values = attend(
         functools.partial(attention_kernel, far_count, False),
-        sds((rows - 2 * EDGE_ROWS, width), BF16),
+        (
+            sds((rows - 2 * EDGE_ROWS, width), BF16),
+            sds((width, far_width), BF16),
+            sds((far_width, width), BF16),
+        ),
         queries,
         keys,
         values,
-        far_keys,
-        far_values,
+        coarse,
+        w_key,
+        w_value,
         scratch=scratch,
         name="middle",
     )

time: 46.4 us -> 46.3 us (level)
    pallas_call x6 -> x5, Pallas kernels: 32.3 us -> 32.2 us  [call(): pl.pallas_call(kernel, out_shape=outs, in_specs=in_specs or [VMEM] * len(...]
where the time goes in v7:
time: 46.3 us; the launch traced here: 45.8 us
  Pallas kernels  35.2 us (76%)
  starting transfers between devices  10.2 us (22%)
    pallas_call x5, Pallas kernels, call(): pl.pallas_call(kernel, out_shape=outs, in_specs=in_specs or [VMEM] * len(...  32.2 us
    ppermute x3, starting transfers between devices, body(): received = lax.ppermute(coarse, 'seq', pairs)  4.02 us
    ppermute x2, starting transfers between devices, swap_pairs(): return lax.ppermute(x, 'seq', pairs + [(b, a) for a, b in pairs])  3.25 us
    pallas_call x2, Pallas kernels, body(): pl.pallas_call(functools.partial(out_kernel, starts), out_shape=sds((rows...  2.97 us
    ppermute x2, starting transfers between devices, swap_heads(): return lax.ppermute(x, 'head', [(0, 1), (1, 0)])  2.96 us
  transfers between devices with their start and end apart: 7, of which 1 were waited for; matrix products, arithmetic and copies ran while one was open for 0% of the time, Pallas kernels for 66%

profile of v7, /device:TPU:7, one launch (start us, length us, event | category | flops | bytes accessed | tf_op | source)
XLA Modules:
  0.0 45.8 jit_solution(17462510391868139061)
XLA Ops:
  0.0 0.0 copy-start.2
  0.0 0.0 copy-start.3
  0.0 3.7 %norm.1 = (bf16[4096,512]{1,0:T(8,128)(2,1)S(1)}, bf16[4,512]{1,0:T(4,128)(2,1)S(1)}, bf16[256,512]{1,0:T(8,128)(2,1)S(1)}, bf16[256,512]{1,0:T(8,128)(2,1)S(1)}) custom-call(bf16[4096,512]{1,0:T(8,128)(2,1)} %tok_ref.1, f32[1,512]{1,0:T(1,128)} %bitcast.2, f32[1,512]{1,0:T(1,128)} %bitcast.3), custom_call_target="tpu_custom_call" | custom-call | flops 2147483648 | bytes 4194304 | tf_op jit(solution)/shard_map/norm/pallas_call | solution.py:40
  3.7 1.4 %collective-permute-start = (bf16[4,512]{1,0:T(4,128)(2,1)S(1)}, bf16[4,512]{1,0:T(4,128)(2,1)S(1)}, u32[]{:S(2)}, u32[]{:S(2)}) collective-permute-start(bf16[4,512]{1,0:T(4,128)(2,1)S(1)} %get-tuple-element.30), channel_id=1, source_target_pairs={{0,4},{2,6},{4,0},{6,2},{8,12},{10,14},{12,8},{14,10},{1,5},{3,7},... | collective-permute-start | bytes 12296 | tf_op jit(solution)/shard_map/ppermute | solution.py:374
  5.1 0.0 copy-done.2
  5.1 0.0 copy-done.3
  5.1 0.0 copy-start.1
  5.1 0.0 copy-start.4
  5.1 2.4 %keys_values.1 = (bf16[256,4096]{1,0:T(8,128)(2,1)S(1)}, bf16[4096,256]{1,0:T(8,128)(2,1)S(1)}) custom-call(bf16[4096,512]{1,0:T(8,128)(2,1)S(1)} %get-tuple-element.35.normed_ref, bf16[512,256]{1,0:T(8,128)(2,1)S(1)} %copy-done.2, bf16[512,256]{1,0:T(8,128)(2,1)S(1)} %copy-done.3), custom_call_target="tpu_custom_call" | custom-call | flops 4294967296 | bytes 4194304 | tf_op jit(solution)/shard_map/keys_values/pallas_call | solution.py:40
  7.5 0.0 collective-permute-done
  7.6 2.4 %collective-permute-start.1 = (bf16[8,512]{1,0:T(8,128)(2,1)S(1)}, bf16[8,512]{1,0:T(8,128)(2,1)S(1)}, u32[]{:S(2)}, u32[]{:S(2)}) collective-permute-start(bf16[8,512]{1,0:T(8,128)(2,1)S(1)} %pad_maximum_fusion.2), channel_id=1, source_target_pairs={{0,8},{2,10},{4,12},{6,14},{8,0},{10,2},{12,4},{14,6},{1,9},{3,11}... | collective-permute-start | bytes 24584 | tf_op jit(solution)/shard_map/ppermute | solution.py:374
  9.9 0.0 copy-done.1
  9.9 0.0 copy-done.4
  9.9 1.9 %queries.1.q_ref = bf16[256,4096]{1,0:T(8,128)(2,1)S(1)} custom-call(bf16[4096,512]{1,0:T(8,128)(2,1)S(1)} %get-tuple-element.35.normed_ref, bf16[512,256]{1,0:T(8,128)(2,1)S(1)} %copy-done.1, f32[4]{0:T(128)S(1)} %copy-done.4), custom_call_target="tpu_custom_call" | custom-call | flops 4294967296 | bytes 4194304 | tf_op jit(solution)/shard_map/queries/pallas_call | solution.py:40
  11.9 0.0 collective-permute-done.1
  11.9 0.3 collective-permute-start.4
  12.2 1.2 %collective-permute-start.2 = (bf16[256,512]{1,0:T(8,128)(2,1)S(1)}, bf16[256,512]{1,0:T(8,128)(2,1)S(1)}, u32[]{:S(2)}, u32[]{:S(2)}) collective-permute-start(bf16[256,512]{1,0:T(8,128)(2,1)S(1)} %get-tuple-element.39), channel_id=1, source_target_pairs={{0,2},{4,6},{8,10},{12,14},{2,0},{6,4},{10,8},{14,12},{1,3},{5,7},... | collective-permute-start | bytes 786440 | tf_op jit(solution)/shard_map/ppermute | solution.py:312
  13.5 2.0 %collective-permute-start.3 = (bf16[256,512]{1,0:T(8,128)(2,1)S(1)}, bf16[256,512]{1,0:T(8,128)(2,1)S(1)}, u32[]{:S(2)}, u32[]{:S(2)}) collective-permute-start(bf16[256,512]{1,0:T(8,128)(2,1)S(1)} %get-tuple-element.43), channel_id=1, source_target_pairs={{2,4},{6,8},{10,12},{4,2},{8,6},{12,10},{3,5},{7,9},{11,13},{5,3},... | collective-permute-start | bytes 786440 | tf_op jit(solution)/shard_map/ppermute | solution.py:312
  15.5 0.0 collective-permute-done.4
  15.5 17.3 %middle.1 = (bf16[3072,256]{1,0:T(8,128)(2,1)S(1)}, bf16[256,128]{1,0:T(8,128)(2,1)S(1)}, bf16[128,256]{1,0:T(8,128)(2,1)S(1)}) custom-call(bf16[256,4096]{1,0:T(8,128)(2,1)S(1)} %queries.1.q_ref, bf16[256,4096]{1,0:T(8,128)(2,1)S(1)} %get-tuple-element.37.main_k_ref, bf16[4096,256]{1,0:T(8,128)(2,1)S(1)} %get-tuple-element.38.main_v_ref, ...), custom_call_target="tpu_custom_call" | custom-call | flops 10737418240 | bytes 4194304 | tf_op jit(solution)/shard_map/middle/pallas_call | solution.py:40
  32.8 2.8 %collective-permute-start.6 = (bf16[3072,256]{1,0:T(8,128)(2,1)S(1)}, bf16[3072,256]{1,0:T(8,128)(2,1)S(1)}, u32[]{:S(2)}, u32[]{:S(2)}) collective-permute-start(bf16[3072,256]{1,0:T(8,128)(2,1)S(1)} %get-tuple-element.50.own_ref), channel_id=1, source_target_pairs={{0,1},{1,0},{2,3},{3,2},{4,5},{5,4},{6,7},{7,6},{8,9},{9,8},{10,11... | collective-permute-start | bytes 4718600 | tf_op jit(solution)/shard_map/ppermute | solution.py:307
  35.6 0.0 collective-permute-done.2.rest_0_
  35.6 0.0 collective-permute-done.3.rest_1_
  35.6 0.0 copy-start
  35.6 6.8 %outer.1.own_ref = bf16[1024,256]{1,0:T(8,128)(2,1)S(1)} custom-call(bf16[256,4096]{1,0:T(8,128)(2,1)S(1)} %queries.1.q_ref, bf16[256,4096]{1,0:T(8,128)(2,1)S(1)} %get-tuple-element.37.main_k_ref, bf16[4096,256]{1,0:T(8,128)(2,1)S(1)} %get-tuple-element.38.main_v_ref, bf16[256,512]{1,0:T(8,128)(2,1)S(1)} %collective-permute-done.2.rest_0_, ...), custom_call_target="tpu_custom_call" | custom-call | flops 10737418240 | bytes 4194304 | tf_op jit(solution)/shard_map/outer/pallas_call | solution.py:40
  42.5 0.1 collective-permute-start.5
  42.6 0.0 collective-permute-done.6.other_ref
  42.6 0.0 copy-done
  42.6 1.8 %out.2.rest_0_ = bf16[4096,256]{1,0:T(8,128)(2,1)} custom-call(bf16[3072,256]{1,0:T(8,128)(2,1)S(1)} %get-tuple-element.50.own_ref, bf16[3072,256]{1,0:T(8,128)(2,1)S(1)} %collective-permute-done.6.other_ref, bf16[512,512]{1,0:T(8,128)(2,1)S(1)} %copy-done), custom_call_target="tpu_custom_call" | custom-call | flops 1073741824 | bytes 4194304 | tf_op jit(solution)/shard_map/out/pallas_call | solution.py:444
  44.4 0.1 collective-permute-done.5.other_ref
  44.5 1.2 %out.3 = bf16[4096,256]{1,0:T(8,128)(2,1)} custom-call(bf16[1024,256]{1,0:T(8,128)(2,1)S(1)} %outer.1.own_ref, bf16[1024,256]{1,0:T(8,128)(2,1)S(1)} %collective-permute-done.5.other_ref, bf16[512,512]{1,0:T(8,128)(2,1)S(1)} %copy-done, bf16[4096,256]{1,0:T(8,128)(2,1)} %out.2.rest_0_), custom_call_target="tpu_custom_call", output_to_operand_aliasing={{}: (3, {})} | custom-call | flops 1073741824 | bytes 4194304 | tf_op jit(solution)/shard_map/out/pallas_call | solution.py:444
  (3 shorter events, 0.0 us)
Async XLA Ops:
  0.0 5.1 %copy-start.2 = (bf16[512,256]{1,0:T(8,128)(2,1)S(1)}, bf16[512,256]{1,0:T(8,128)(2,1)}, u32[]{:S(2)}) copy-start(bf16[512,256]{1,0:T(8,128)(2,1)} %rest_2_.3) | copy-start | bytes 786436
  0.0 5.1 %copy-start.3 = (bf16[512,256]{1,0:T(8,128)(2,1)S(1)}, bf16[512,256]{1,0:T(8,128)(2,1)}, u32[]{:S(2)}) copy-start(bf16[512,256]{1,0:T(8,128)(2,1)} %rest_3_.1) | copy-start | bytes 786436
  3.7 3.8 %collective-permute-start = (bf16[4,512]{1,0:T(4,128)(2,1)S(1)}, bf16[4,512]{1,0:T(4,128)(2,1)S(1)}, u32[]{:S(2)}, u32[]{:S(2)}) collective-permute-start(bf16[4,512]{1,0:T(4,128)(2,1)S(1)} %get-tuple-element.30), channel_id=1, source_target_pairs={{0,4},{2,6},{4,0},{6,2},{8,12},{10,14},{12,8},{14,10},{1,5},{3,7},... | collective-permute-start | bytes 12296 | tf_op jit(solution)/shard_map/ppermute | solution.py:374
  5.1 4.8 %copy-start.1 = (bf16[512,256]{1,0:T(8,128)(2,1)S(1)}, bf16[512,256]{1,0:T(8,128)(2,1)}, u32[]{:S(2)}) copy-start(bf16[512,256]{1,0:T(8,128)(2,1)} %w_ref.3) | copy-start | bytes 786436
  5.1 4.8 %copy-start.4 = (f32[4]{0:T(128)S(1)}, f32[4]{0:T(128)}, u32[]{:S(2)}) copy-start(f32[4]{0:T(128)} %scale_ref.1) | copy-start | bytes 52
  7.6 4.3 %collective-permute-start.1 = (bf16[8,512]{1,0:T(8,128)(2,1)S(1)}, bf16[8,512]{1,0:T(8,128)(2,1)S(1)}, u32[]{:S(2)}, u32[]{:S(2)}) collective-permute-start(bf16[8,512]{1,0:T(8,128)(2,1)S(1)} %pad_maximum_fusion.2), channel_id=1, source_target_pairs={{0,8},{2,10},{4,12},{6,14},{8,0},{10,2},{12,4},{14,6},{1,9},{3,11}... | collective-permute-start | bytes 24584 | tf_op jit(solution)/shard_map/ppermute | solution.py:374
  11.9 3.5 %collective-permute-start.4 = (bf16[16,512]{1,0:T(8,128)(2,1)S(1)}, bf16[16,512]{1,0:T(8,128)(2,1)S(1)}, u32[]{:S(2)}, u32[]{:S(2)}) collective-permute-start(bf16[16,512]{1,0:T(8,128)(2,1)S(1)} %pad_maximum_fusion.1), channel_id=1, source_target_pairs={{0,2},{2,0},{4,6},{6,4},{8,10},{10,8},{12,14},{14,12},{1,3},{3,1},... | collective-permute-start | bytes 49160 | tf_op jit(solution)/shard_map/ppermute | solution.py:374
  12.2 23.4 %collective-permute-start.2 = (bf16[256,512]{1,0:T(8,128)(2,1)S(1)}, bf16[256,512]{1,0:T(8,128)(2,1)S(1)}, u32[]{:S(2)}, u32[]{:S(2)}) collective-permute-start(bf16[256,512]{1,0:T(8,128)(2,1)S(1)} %get-tuple-element.39), channel_id=1, source_target_pairs={{0,2},{4,6},{8,10},{12,14},{2,0},{6,4},{10,8},{14,12},{1,3},{5,7},... | collective-permute-start | bytes 786440 | tf_op jit(solution)/shard_map/ppermute | solution.py:312
  13.5 22.2 %collective-permute-start.3 = (bf16[256,512]{1,0:T(8,128)(2,1)S(1)}, bf16[256,512]{1,0:T(8,128)(2,1)S(1)}, u32[]{:S(2)}, u32[]{:S(2)}) collective-permute-start(bf16[256,512]{1,0:T(8,128)(2,1)S(1)} %get-tuple-element.43), channel_id=1, source_target_pairs={{2,4},{6,8},{10,12},{4,2},{8,6},{12,10},{3,5},{7,9},{11,13},{5,3},... | collective-permute-start | bytes 786440 | tf_op jit(solution)/shard_map/ppermute | solution.py:312
  32.8 9.8 %collective-permute-start.6 = (bf16[3072,256]{1,0:T(8,128)(2,1)S(1)}, bf16[3072,256]{1,0:T(8,128)(2,1)S(1)}, u32[]{:S(2)}, u32[]{:S(2)}) collective-permute-start(bf16[3072,256]{1,0:T(8,128)(2,1)S(1)} %get-tuple-element.50.own_ref), channel_id=1, source_target_pairs={{0,1},{1,0},{2,3},{3,2},{4,5},{5,4},{6,7},{7,6},{8,9},{9,8},{10,11... | collective-permute-start | bytes 4718600 | tf_op jit(solution)/shard_map/ppermute | solution.py:307
  35.6 7.0 %copy-start = (bf16[512,512]{1,0:T(8,128)(2,1)S(1)}, bf16[512,512]{1,0:T(8,128)(2,1)}, u32[]{:S(2)}) copy-start(bf16[512,512]{1,0:T(8,128)(2,1)} %w_ref.5) | copy-start | bytes 1572868
  42.5 2.0 %collective-permute-start.5 = (bf16[1024,256]{1,0:T(8,128)(2,1)S(1)}, bf16[1024,256]{1,0:T(8,128)(2,1)S(1)}, u32[]{:S(2)}, u32[]{:S(2)}) collective-permute-start(bf16[1024,256]{1,0:T(8,128)(2,1)S(1)} %outer.1.own_ref), channel_id=1, source_target_pairs={{0,1},{1,0},{2,3},{3,2},{4,5},{5,4},{6,7},{7,6},{8,9},{9,8},{10,11... | collective-permute-start | bytes 1572872 | tf_op jit(solution)/shard_map/ppermute | solution.py:307
